TPU v7x, 32 devices: a whole 2x2x4 slice. The times are simulated.
32 devices in a mesh: rep: 2 (over y), seq: 4 (over z), head: 2 (over x), sub: 2 (over core).
Axes of the slice: x: 2, y: 2, z: 4, core: 2. Of those that a mesh axis runs over, the one named last changes fastest.
Arguments:
- queries: bfloat16 [4096, 2048], P(('rep', 'seq', 'sub'), 'head'), parts along dimension 0, may hold values from -1.5 to 1.5
- key_vectors: bfloat16 [4096, 2048], P(('rep', 'seq'), 'head'), parts along dimension 0, may hold values from -1.5 to 1.5
- value_vectors: bfloat16 [4096, 2048], P(('rep', 'seq'), 'head'), parts along dimension 0, may hold values from -6 to 6
- gate_bins: int32 [4096, 16], P(('rep', 'seq'), 'head'), parts along dimension 0, may hold values from 0 to 2048
- doc_lengths: int32 [6], P('rep'), parts along dimension 0, may hold values from 1 to 1536, as said below
- decay_rates: float32 [16], P('head'), may hold values from 0.15 to 86
- ridge_terms: float32 [16], P('head'), may hold values from 0.5 to 2
Outputs:
- mesa_output: bfloat16 [4096, 2048], P(('rep', 'seq', 'sub'), 'head'), parts along dimension 0
There are 2 independent parts, one for each index of `rep`. A program takes and returns all parts, laid end to end along the dimension named above; an argument that names none is the same for every part. Nothing has to cross between parts.
Inputs may be any that keep to these rules, and one draw needn't show every extreme that they name: `doc_lengths`: the lengths sum to 2048.
All inputs are finite; a program needn't handle non-finite values.
Results may differ from a plain program's by a relative error of at most 0.001.
Values sent between devices are 32-bit elements; how exact they have to be, the bound alone decides.
No kernel may reach another device: no remote copies, remote signals or barrier semaphores. Data moves between devices by JAX's collectives and lax.ppermute only.
A program may use at most 64 MiB of HBM per device.

v0:
```python
import functools

import jax
import jax.numpy as jnp
from jax import lax
from jax.experimental import pallas as pl
from jax.experimental.pallas import tpu as pltpu
from jax.sharding import PartitionSpec as P

ITERS = 4
guard = 1e-06
f32 = jnp.float32
bf16 = jnp.bfloat16
PAD = 8
PER_STEP = 2


def dot_nn(a, b):
    return lax.dot_general(a, b, (((1,), (0,)), ((), ())), preferred_element_type=f32)


def dot_nt(a, b):
    return lax.dot_general(a, b, (((1,), (1,)), ((), ())), preferred_element_type=f32)


def split(x):
    high = x.astype(bf16)
    low = (x - high.astype(f32)).astype(bf16)
    return high, low


def iota(shape, axis):
    return lax.broadcasted_iota(jnp.int32, shape, axis)


def doc_of(doc_ref, position):
    count = jnp.zeros_like(position)
    start = jnp.int32(0)
    for index in range(doc_ref.shape[0]):
        count = count + (start <= position).astype(jnp.int32)
        start = start + doc_ref[index]
    return count


def split_bins(bins):
    whole = bins.astype(f32)
    high = jnp.floor(whole * (1.0 / 128.0))
    low = whole - 128.0 * high
    return high.astype(bf16), low.astype(bf16)


def running_rows(bins):
    size = bins.shape[1]
    high, low = split_bins(bins)
    step = jnp.where(iota((size, size), 0) <= iota((size, size), 1), 1.0, 0.0).astype(bf16)
    return 128.0 * dot_nn(high, step) + dot_nn(low, step)


def running_columns(bins):
    size = bins.shape[1]
    high, low = split_bins(bins)
    step = jnp.where(iota((size, size), 1) <= iota((size, size), 0), 1.0, 0.0).astype(bf16)
    return 128.0 * dot_nt(step, high) + dot_nt(step, low)


def scale_column(rate_ref, total):
    count = rate_ref.shape[0]
    column = jnp.zeros((count, 1), f32)
    for head in range(count):
        column = jnp.where(iota((count, 1), 0) == head, rate_ref[head], column)
    return column * (-1.0 / total)


def weighted_sums(key_t, weight, both):
    width = key_t.shape[0]
    product = dot_nn(jnp.concatenate(split(key_t.astype(f32) * weight), 0), both)
    return product[:width] + product[width:]


def pack_gram(gram, decay):
    width = gram.shape[0]
    half = width // 2
    turned = pltpu.roll(gram[half:], half, 1)
    row, col = iota((half, width), 0), iota((half, width), 1)
    packed = jnp.where((col < half) & (row > col), turned, gram[:half])
    diagonal = jnp.sum(jnp.where(row == col, turned, 0.0), axis=0, keepdims=True)
    tail = jnp.where(iota((PAD, width), 0) == 0, diagonal, decay)
    return packed, tail


def unpack_gram(packed, diagonal):
    half, width = packed.shape
    turned = pltpu.roll(packed, half, 1)
    crossed = jnp.concatenate([packed, turned], 0).T
    row, col = iota((half, width), 0), iota((half, width), 1)
    top = jnp.where(row <= col, packed, crossed[:half])
    low_col = col - half
    bottom = jnp.where((low_col >= 0) & (row > low_col), turned, crossed[half:])
    bottom = jnp.where(row == low_col, pltpu.roll(jnp.broadcast_to(diagonal, (half, width)), half, 1), bottom)
    return jnp.concatenate([top, bottom], 0)


def sums_kernel(
    where_ref, doc_ref, rate_ref, key_ref, value_ref, bins_ref, gram_ref, memory_ref, weight_ref, decay_ref,
    *, total, heads, width,
):
    shard = key_ref.shape[0]
    first = where_ref[0] * shard
    core = where_ref[1]
    scale = scale_column(rate_ref, total)
    cumulative = running_rows(bins_ref[...])
    last = cumulative[:, shard - 1 :]
    position = first + iota((1, shard), 1)
    end_doc = doc_of(doc_ref, first + shard - 1)
    weight_ref[...] = jnp.where(
        doc_of(doc_ref, position) == end_doc, jnp.exp(scale * (last - cumulative)), 0.0
    )
    through = end_doc == doc_of(doc_ref, first - 1)
    decay_ref[...] = jnp.broadcast_to(jnp.where(through, jnp.exp(scale * last), 0.0), decay_ref.shape)
    for i in range(heads):
        head = core * heads + i
        cols = slice(i * width, (i + 1) * width)
        key = key_ref[:, cols]
        both = jnp.concatenate([key, value_ref[:, cols]], 1)
        sums = weighted_sums(key.T, weight_ref[pl.ds(head, 1), :], both)
        packed, tail = pack_gram(sums[:, :width], decay_ref[pl.ds(head, 1), :])
        gram_ref[i, : width // 2, :] = packed
        gram_ref[i, width // 2 :, :] = tail
        memory_ref[i] = sums[:, width:]


def prepare_kernel(
    where_ref, doc_ref, rate_ref, query_ref, key_ref, value_ref, bins_ref,
    gate_ref, query_t_ref, key_t_ref, value_t_ref, within_ref, mid_gram_ref, mid_memory_ref, carried_ref,
    row_ref, column_ref, mid_ref, decay_ref, *, total, width,
):
    shard, rows = key_ref.shape[0], query_ref.shape[0]
    first = where_ref[0] * shard
    start = where_ref[1] * rows
    own = pl.ds(pl.multiple_of(start, rows), rows)
    before_doc = doc_of(doc_ref, first + start - 1)
    key_pos = first + start + iota((rows, 1), 0)
    own_pos = first + start + iota((1, rows), 1)
    own_doc = doc_of(doc_ref, own_pos)

    @pl.when(pl.program_id(0) == 0)
    def _():
        scale = scale_column(rate_ref, total)
        bins = bins_ref[...]
        cumulative = running_rows(bins)
        row_ref[...] = cumulative
        column_ref[...] = running_columns(bins)
        token = iota((1, shard), 1)
        before = jnp.sum(jnp.where(token == start - 1, cumulative, 0.0), axis=1, keepdims=True)
        mid_live = (token < start) & (doc_of(doc_ref, first + token) == before_doc)
        mid_ref[...] = jnp.where(
            mid_live, jnp.exp(scale * jnp.maximum(before - cumulative, 0.0)), 0.0
        )
        through = before_doc == doc_of(doc_ref, first - 1)
        decay_ref[...] = jnp.broadcast_to(
            jnp.where(through, jnp.exp(scale * before), 0.0), decay_ref.shape
        )
        carried_ref[...] = jnp.where(
            own_doc == before_doc, jnp.exp(scale * jnp.maximum(row_ref[:, own] - before, 0.0)), 0.0
        )

    allowed = (key_pos <= own_pos) & (doc_of(doc_ref, key_pos) == own_doc)
    columns = column_ref[own, :]
    for i in range(query_ref.shape[1] // width):
        head = pl.program_id(0) * PER_STEP + i
        scale = rate_ref[head] * (-1.0 / total)
        cols = slice(i * width, (i + 1) * width)
        key_t = key_ref[:, cols].T
        both = jnp.concatenate([key_ref[:, cols], value_ref[:, cols]], 1)
        sums = weighted_sums(key_t, mid_ref[pl.ds(head, 1), :], both)
        packed, tail = pack_gram(sums[:, :width], decay_ref[pl.ds(head, 1), :])
        mid_gram_ref[i, : width // 2, :] = packed
        mid_gram_ref[i, width // 2 :, :] = tail
        mid_memory_ref[i] = sums[:, width:]
        key_own = key_ref[own, cols]
        own_t = key_own.T
        query_t = query_ref[:, cols].T
        query_t_ref[i] = query_t
        key_t_ref[i] = own_t
        value_t_ref[i] = value_ref[own, cols].T
        column = jnp.sum(jnp.where(iota(columns.shape, 1) == head, columns, 0.0), axis=1, keepdims=True)
        gap = jnp.maximum(row_ref[pl.ds(head, 1), own] - column, 0.0)
        gate = jnp.where(allowed, jnp.exp(scale * gap), 0.0)
        gate_ref[i] = gate
        weighted = dot_nn(key_own, query_t) * gate
        within_ref[i] = dot_nn(jnp.concatenate([own_t, own_t], 1), jnp.concatenate(split(weighted), 0))


def solve_kernel(
    where_ref, ridge_ref, key_ref, gate_ref, query_t_ref, key_t_ref, value_t_ref, within_ref, mid_ref, carried_ref,
    gram_ref, solution_ref, chunk_ref, *, cores, turn, width,
):
    rows = query_t_ref.shape[2]
    core = where_ref[1]
    steps = pl.num_programs(0)
    group = lax.rem(core + turn, cores)
    own = pl.ds(pl.multiple_of(core * rows, rows), rows)
    half = width // 2
    per_step = range(query_t_ref.shape[0])
    base = (group * steps + pl.program_id(0)) * query_t_ref.shape[0]

    def row_sum(x):
        return jnp.sum(x, axis=0, keepdims=True)

    ridge = [ridge_ref[base + i] for i in per_step]
    carried = [carried_ref[pl.ds(base + i, 1), :] for i in per_step]
    system, keys, key_pair = [], [], []
    direction, residual, energy, result = [], [], [], []
    for i in per_step:
        cols = slice(i * width, (i + 1) * width)
        decay = mid_ref[i, half + 1 : half + 2, :]
        packed = mid_ref[i, :half, :] + decay * gram_ref[i, :half, :]
        diagonal = mid_ref[i, half : half + 1, :] + decay * gram_ref[i, half : half + 1, :]
        high, low = split(unpack_gram(packed, diagonal))
        key = key_ref[own, cols]
        keys.append(jnp.concatenate([key, key], 1))
        key_pair.append(jnp.concatenate([key_t_ref[i], key_t_ref[i]], 1))
        system.append(
            jnp.concatenate(
                [jnp.concatenate([high, low], 0), jnp.concatenate([high, jnp.zeros_like(low)], 0)], 1
            )
        )
        direction.append(query_t_ref[i].astype(f32))
        residual.append(direction[i])
        energy.append(row_sum(direction[i] * direction[i]))
        result.append(None)
    for iteration in range(ITERS):
        last = iteration == ITERS - 1
        earlier = []
        parts = []
        for i in per_step:
            if iteration == 0:
                product = dot_nn(system[i][:, :width], query_t_ref[i])
            else:
                pair = jnp.concatenate(split(direction[i]), 0)
                product = dot_nn(system[i], pair)
                plain = dot_nn(keys[i], pair)
                parts.append((plain, plain * gate_ref[i]))
            earlier.append(
                carried[i] * (product[:width] + product[width:]) + ridge[i] * direction[i]
            )
        for i in per_step:
            if iteration == 0:
                applied = earlier[i] + within_ref[i]
                curvature = row_sum(direction[i] * applied)
            elif not last:
                applied = earlier[i] + dot_nn(key_pair[i], jnp.concatenate(split(parts[i][1]), 0))
                curvature = row_sum(direction[i] * applied)
            else:
                curvature = row_sum(parts[i][0] * parts[i][1]) + row_sum(direction[i] * earlier[i])
            stepsize = energy[i] / (curvature + guard)
            moved = stepsize * direction[i]
            result[i] = moved if iteration == 0 else result[i] + moved
            if not last:
                residual[i] = residual[i] - stepsize * applied
                energy_next = row_sum(residual[i] * residual[i])
                direction[i] = residual[i] + (energy_next / (energy[i] + guard)) * direction[i]
                energy[i] = energy_next
    for i in per_step:
        weighted = dot_nn(keys[i], jnp.concatenate(split(result[i]), 0)) * gate_ref[i]
        value_t = value_t_ref[i]
        chunk = dot_nn(jnp.concatenate([value_t, value_t], 1), jnp.concatenate(split(weighted), 0))
        chunk_ref[i] = chunk.T
        high, low = split(carried[i] * result[i])
        solution_ref[i] = jnp.concatenate([high.T, low.T], 1)


def read_kernel(where_ref, solution_ref, chunk_ref, mid_ref, mid_memory_ref, memory_ref, *rest, width):
    out_ref = rest[-1]
    half = width // 2
    for i in range(solution_ref.shape[0]):
        decay = mid_ref[i, 1:2, :]
        memory = mid_memory_ref[i] + decay * memory_ref[i]
        high, low = split(memory)
        pair = jnp.concatenate(
            [jnp.concatenate([high, high], 0), jnp.concatenate([low, jnp.zeros_like(low)], 0)], 1
        )
        product = dot_nn(solution_ref[i], pair)
        out = product[:, :width] + product[:, width:] + chunk_ref[i]
        out_ref[:, i * width : (i + 1) * width] = out.astype(out_ref.dtype)


def per_device(queries, key_vectors, value_vectors, gate_bins, doc_lengths, decay_rates, ridge_terms):
    head_count = decay_rates.shape[0]
    shard = key_vectors.shape[0]
    rows = queries.shape[0]
    width = key_vectors.shape[1] // head_count
    half = width // 2
    seq = lax.axis_size("seq")
    cores = lax.axis_size("sub")
    heads = head_count // cores
    total = shard * seq
    where = jnp.stack([lax.axis_index("seq"), lax.axis_index("sub")]).astype(jnp.int32)
    bins = gate_bins.T
    smem = pl.BlockSpec(memory_space=pltpu.SMEM)
    any_space = pl.BlockSpec(memory_space=pl.ANY)

    def full(*shape):
        return pl.BlockSpec(shape, lambda i, where_ref: (0,) * len(shape))

    def call(kernel, grid, in_specs, out_specs, out_shape, scratch, name, cost, **options):
        return pl.pallas_call(
            kernel,
            grid_spec=pltpu.PrefetchScalarGridSpec(
                num_scalar_prefetch=1,
                grid=(grid,),
                in_specs=in_specs,
                out_specs=out_specs,
                scratch_shapes=scratch,
            ),
            out_shape=out_shape,
            name=name,
            cost_estimate=pl.CostEstimate(flops=cost, bytes_accessed=4 << 20, transcendentals=0),
            **options,
        )

    group = pl.BlockSpec((shard, heads * width), lambda i, where_ref: (0, where_ref[1]))
    gram_sum, memory_sum = call(
        functools.partial(sums_kernel, total=total, heads=heads, width=width),
        1,
        [smem, smem, group, group, full(head_count, shard)],
        [full(heads, half + PAD, width), full(heads, width, width)],
        [
            jax.ShapeDtypeStruct((heads, half + PAD, width), f32),
            jax.ShapeDtypeStruct((heads, width, width), f32),
        ],
        [pltpu.VMEM((head_count, shard), f32), pltpu.VMEM((head_count, width), f32)],
        "shard_sums",
        1 << 30,
    )(where, doc_lengths, decay_rates, key_vectors, value_vectors, bins)

    step = min(PER_STEP, heads)

    def head_block(*shape):
        return pl.BlockSpec((step, *shape), lambda i, where_ref: (i,) + (0,) * len(shape))

    def step_block(count):
        return pl.BlockSpec((count, step * width), lambda i, where_ref: (0, i))

    def per_head(*shape, dtype=f32):
        return jax.ShapeDtypeStruct((head_count, *shape), dtype)

    gate, query_t, key_t, value_t, within, mid_gram, mid_memory, carried = call(
        functools.partial(prepare_kernel, total=total, width=width),
        head_count // step,
        [smem, smem, step_block(rows), step_block(shard), step_block(shard), full(head_count, shard)],
        [
            head_block(rows, rows),
            head_block(width, rows),
            head_block(width, rows),
            head_block(width, rows),
            head_block(width, rows),
            head_block(half + PAD, width),
            head_block(width, width),
            full(head_count, rows),
        ],
        [
            per_head(rows, rows),
            per_head(width, rows, dtype=bf16),
            per_head(width, rows, dtype=bf16),
            per_head(width, rows, dtype=bf16),
            per_head(width, rows),
            per_head(half + PAD, width),
            per_head(width, width),
            per_head(rows),
        ],
        [
            pltpu.VMEM((head_count, shard), f32),
            pltpu.VMEM((shard, head_count), f32),
            pltpu.VMEM((head_count, shard), f32),
            pltpu.VMEM((head_count, width), f32),
        ],
        "prepare",
        4 << 30,
    )(where, doc_lengths, decay_rates, queries, key_vectors, value_vectors, bins)

    own_decay = gram_sum[:, half + 1 : half + 2, :]
    body = (jnp.arange(half + PAD) < half + 1)[None, :, None]
    gram_prior = memory_prior = None
    covered = 0
    while covered < seq - 1:
        if covered == 0:
            hop = functools.partial(lax.ppermute, axis_name="seq", perm=[(i, i + 1) for i in range(seq - 1)])
            gram_prior, memory_prior = hop(gram_sum), hop(memory_sum)
            covered = 1
        else:
            shift = covered + 1
            hop = functools.partial(
                lax.ppermute, axis_name="seq", perm=[(i, i + shift) for i in range(seq - shift)]
            )
            prior_decay = gram_prior[:, half + 1 : half + 2, :]
            gram_in = hop(jnp.where(body, gram_sum, 0.0) + own_decay * gram_prior)
            memory_in = hop(memory_sum + own_decay * memory_prior)
            gram_prior = jnp.where(body, gram_prior, 0.0) + prior_decay * gram_in
            memory_prior = memory_prior + prior_decay * memory_in
            covered = covered + shift

    def swap(x):
        return lax.ppermute(x, "sub", [(i, (i + 1) % cores) for i in range(cores)])

    steps = heads // step
    solved = []
    for turn in range(cores):

        def group_index(i, where_ref, turn=turn):
            return lax.rem(where_ref[1] + turn, cores) * steps + i

        def block(*shape):
            return pl.BlockSpec(
                (step, *shape), lambda i, where_ref: (group_index(i, where_ref),) + (0,) * len(shape)
            )

        def local_block(*shape):
            return pl.BlockSpec((step, *shape), lambda i, where_ref: (i,) + (0,) * len(shape))

        solved.append(
            call(
                functools.partial(solve_kernel, cores=cores, turn=turn, width=width),
                steps,
                [
                    smem,
                    pl.BlockSpec((shard, step * width), lambda i, where_ref: (0, group_index(i, where_ref))),
                    block(rows, rows),
                    block(width, rows),
                    block(width, rows),
                    block(width, rows),
                    block(width, rows),
                    block(half + PAD, width),
                    full(head_count, rows),
                    local_block(half + PAD, width),
                ],
                [local_block(rows, 2 * width), local_block(rows, width)],
                [
                    jax.ShapeDtypeStruct((heads, rows, 2 * width), bf16),
                    jax.ShapeDtypeStruct((heads, rows, width), f32),
                ],
                [],
                f"solve_{turn}",
                2 << 30,
            )(
                where, ridge_terms, key_vectors, gate, query_t, key_t, value_t, within, mid_gram, carried,
                gram_prior if turn == 0 else swap(gram_prior),
            )
        )

    output = None
    for turn in range(cores):

        def group_all(*shape, turn=turn):
            return pl.BlockSpec(
                (heads, *shape),
                lambda i, where_ref: (lax.rem(where_ref[1] + turn, cores),) + (0,) * len(shape),
            )

        in_specs = [
            full(heads, rows, 2 * width),
            full(heads, rows, width),
            pl.BlockSpec(
                (heads, PAD, width),
                lambda i, where_ref, turn=turn: (lax.rem(where_ref[1] + turn, cores), half // PAD, 0),
            ),
            group_all(width, width),
            full(heads, width, width),
        ]
        operands = [where, *solved[turn], mid_gram, mid_memory, memory_prior if turn == 0 else swap(memory_prior)]
        aliases = {}
        if output is not None:
            aliases = {len(operands): 0}
            in_specs.append(any_space)
            operands.append(output)
        output = call(
            functools.partial(read_kernel, width=width),
            1,
            in_specs,
            pl.BlockSpec(
                (rows, heads * width), lambda i, where_ref, turn=turn: (0, lax.rem(where_ref[1] + turn, cores))
            ),
            jax.ShapeDtypeStruct((rows, head_count * width), bf16),
            [],
            f"read_{turn}",
            1 << 28,
            input_output_aliases=aliases,
        )(*operands)
    return output


def solution(mesh):
    in_specs = (
        P(("rep", "seq", "sub"), "head"),
        P(("rep", "seq"), "head"),
        P(("rep", "seq"), "head"),
        P(("rep", "seq"), "head"),
        P("rep"),
        P("head"),
        P("head"),
    )
    out_specs = P(("rep", "seq", "sub"), "head")
    return jax.shard_map(per_device, mesh=mesh, in_specs=in_specs, out_specs=out_specs, check_vma=False)
```

profile of v0, /device:TPU:31, one launch (start us, length us, event | category | flops | bytes accessed | tf_op | source)
XLA Modules:
  0.0 57.9 jit_solution(2129818009018356050)
XLA Ops:
  0.0 0.6 %pad_add_fusion.where_ref = s32[2]{0:T(128)} fusion(s32[1]{0:T(128)} %bitcast.1, s32[1]{0:T(128)} %bitcast), kind=kLoop, calls=%fused_computation.4 | loop fusion | flops 2 | bytes 16 | tf_op jit(solution)/shard_map/stack | solution.py:298
  0.6 3.4 %shard_sums.1 = (f32[4,72,128]{2,1,0:T(8,128)}, f32[4,128,128]{2,1,0:T(8,128)}) custom-call(s32[2]{0:T(128)} %pad_add_fusion.where_ref, s32[3]{0:T(128)} %doc_ref.3, f32[8]{0:T(128)} %rate_ref.3, bf16[512,1024]{1,0:T(8,128)(2,1)} %key_ref.7, bf16[512,1024]{1,0:T(8,128)(2,1)} %value_ref.3, s32[8,512]{1,0:T(8,128)} %bitcast.9), custom_call_target="tpu_custom_call" | custom-call | flops 1073741824 | bytes 4194304 | tf_op jit(solution)/shard_map/shard_sums/pallas_call | solution.py:323
  4.0 1.3 %collective-permute-start = (f32[4,72,128]{2,1,0:T(8,128)}, f32[4,72,128]{2,1,0:T(8,128)S(1)}, u32[]{:S(2)}, u32[]{:S(2)}) collective-permute-start(f32[4,72,128]{2,1,0:T(8,128)} %get-tuple-element.26), channel_id=1, source_target_pairs={{0,4},{4,8},{8,12},{1,5},{5,9},{9,13},{2,6},{6,10},{10,14},{3,7},{... | collective-permute-start | bytes 442376 | tf_op jit(solution)/shard_map/ppermute | solution.py:389
  5.3 1.3 %collective-permute-start.3 = (f32[4,128,128]{2,1,0:T(8,128)}, f32[4,128,128]{2,1,0:T(8,128)S(1)}, u32[]{:S(2)}, u32[]{:S(2)}) collective-permute-start(f32[4,128,128]{2,1,0:T(8,128)} %get-tuple-element.30), channel_id=1, source_target_pairs={{0,4},{4,8},{8,12},{1,5},{5,9},{9,13},{2,6},{6,10},{10,14},{3,7},{... | collective-permute-start | bytes 786440 | tf_op jit(solution)/shard_map/ppermute | solution.py:389
  6.6 0.7 %slice.7 = f32[4,1,128]{2,1,0:T(1,128)S(1)} slice(f32[4,72,128]{2,1,0:T(8,128)} %get-tuple-element.26), slice={[0:4], [65:66], [0:128]} | slice | bytes 4096 | tf_op jit(solution)/shard_map/slice | solution.py:382
  7.3 3.5 %collective-permute-done = f32[4,72,128]{2,1,0:T(8,128)S(1)} collective-permute-done((f32[4,72,128]{2,1,0:T(8,128)}, f32[4,72,128]{2,1,0:T(8,128)S(1)}, u32[]{:S(2)}, u32[]{:S(2)}) %collective-permute-start) | collective-permute-done | bytes 147488 | tf_op jit(solution)/shard_map/ppermute | solution.py:389
  10.8 1.0 %multiply_add_fusion.3 = f32[4,72,128]{2,1,0:T(8,128)S(1)} fusion(f32[4,72,128]{2,1,0:T(8,128)S(1)} %collective-permute-done, f32[4,72,128]{2,1,0:T(8,128)} %get-tuple-element.26, f32[4,128]{1,0:T(4,128)S(1)} %bitcast.7, pred[72]{0:T(512)(128)(4,1)S(1)} %iota_compare_fusion), kind=kLoop, calls=%fused_computation.3 | loop fusion | flops 110592 | bytes 444488 | tf_op jit(solution)/shard_map/add | solution.py:397
  11.8 1.3 %collective-permute-start.1 = (f32[4,72,128]{2,1,0:T(8,128)S(1)}, f32[4,72,128]{2,1,0:T(8,128)S(1)}, u32[]{:S(2)}, u32[]{:S(2)}) collective-permute-start(f32[4,72,128]{2,1,0:T(8,128)S(1)} %multiply_add_fusion.3), channel_id=1, source_target_pairs={{0,8},{4,12},{1,9},{5,13},{2,10},{6,14},{3,11},{7,15},{16,24},{20,... | collective-permute-start | bytes 442376 | tf_op jit(solution)/shard_map/ppermute | solution.py:397
  13.1 3.3 %collective-permute-done.3 = f32[4,128,128]{2,1,0:T(8,128)S(1)} collective-permute-done((f32[4,128,128]{2,1,0:T(8,128)}, f32[4,128,128]{2,1,0:T(8,128)S(1)}, u32[]{:S(2)}, u32[]{:S(2)}) %collective-permute-start.3) | collective-permute-done | bytes 262176 | tf_op jit(solution)/shard_map/ppermute | solution.py:389
  16.4 1.0 %multiply_add_fusion.1 = f32[4,128,128]{2,1,0:T(8,128)S(1)} fusion(f32[4,128,128]{2,1,0:T(8,128)} %get-tuple-element.30, f32[4,128,128]{2,1,0:T(8,128)S(1)} %collective-permute-done.3, f32[4,128]{1,0:T(4,128)S(1)} %bitcast.8), kind=kLoop, calls=%fused_computation.1 | loop fusion | flops 131072 | bytes 788480 | tf_op jit(solution)/shard_map/add | solution.py:398
  17.4 1.3 %collective-permute-start.4 = (f32[4,128,128]{2,1,0:T(8,128)S(1)}, f32[4,128,128]{2,1,0:T(8,128)S(1)}, u32[]{:S(2)}, u32[]{:S(2)}) collective-permute-start(f32[4,128,128]{2,1,0:T(8,128)S(1)} %multiply_add_fusion.1), channel_id=1, source_target_pairs={{0,8},{4,12},{1,9},{5,13},{2,10},{6,14},{3,11},{7,15},{16,24},{20,... | collective-permute-start | bytes 786440 | tf_op jit(solution)/shard_map/ppermute | solution.py:398
  18.7 7.3 %prepare.1 = (f32[8,256,256]{2,1,0:T(8,128)}, bf16[8,128,256]{2,1,0:T(8,128)(2,1)}, bf16[8,128,256]{2,1,0:T(8,128)(2,1)}, bf16[8,128,256]{2,1,0:T(8,128)(2,1)}, ...) custom-call(s32[2]{0:T(128)} %pad_add_fusion.where_ref, s32[3]{0:T(128)} %doc_ref.3, ...), custom_call_target="tpu_custom_call" | custom-call | flops 4294967296 | bytes 4194304 | tf_op jit(solution)/shard_map/prepare/pallas_call | solution.py:348
  26.0 0.2 collective-permute-done.1
  26.2 0.1 multiply_add_fusion.2.gram_ref
  26.3 0.0 copy-start.2
  26.3 4.1 %collective-permute-start.2 = (f32[4,72,128]{2,1,0:T(8,128)S(1)}, f32[4,72,128]{2,1,0:T(8,128)S(1)}, u32[]{:S(2)}, u32[]{:S(2)}) collective-permute-start(f32[4,72,128]{2,1,0:T(8,128)S(1)} %multiply_add_fusion.2.gram_ref), channel_id=1, source_target_pairs={{0,1},{1,0},{2,3},{3,2},{4,5},{5,4},{6,7},{7,6},{8,9},{9,8},{10,11... | collective-permute-start | bytes 442376 | tf_op jit(solution)/shard_map/ppermute | solution.py:404
  30.4 4.2 %collective-permute-done.4 = f32[4,128,128]{2,1,0:T(8,128)S(1)} collective-permute-done((f32[4,128,128]{2,1,0:T(8,128)S(1)}, f32[4,128,128]{2,1,0:T(8,128)S(1)}, u32[]{:S(2)}, u32[]{:S(2)}) %collective-permute-start.4) | collective-permute-done | bytes 262176 | tf_op jit(solution)/shard_map/ppermute | solution.py:398
  34.7 0.0 copy-start
  34.7 0.9 %collective-permute-start.5 = (f32[4,128,128]{2,1,0:T(8,128)S(1)}, f32[4,128,128]{2,1,0:T(8,128)S(1)}, u32[]{:S(2)}, u32[]{:S(2)}) collective-permute-start(f32[4,128,128]{2,1,0:T(8,128)S(1)} %multiply_add_fusion.memory_ref), channel_id=1, source_target_pairs={{0,1},{1,0},{2,3},{3,2},{4,5},{5,4},{6,7},{7,6},{8,9},{9,8},{10,11... | collective-permute-start | bytes 786440 | tf_op jit(solution)/shard_map/ppermute | solution.py:404
  35.6 0.0 copy-done.2
  35.6 7.4 %solve_0.1 = (bf16[4,256,256]{2,1,0:T(8,128)(2,1)}, f32[4,256,128]{2,1,0:T(8,128)}) custom-call(s32[2]{0:T(128)} %pad_add_fusion.where_ref, f32[8]{0:T(128)} %ridge_ref.3, bf16[512,1024]{1,0:T(8,128)(2,1)} %key_ref.7, f32[8,256,256]{2,1,0:T(8,128)} %get-tuple-element.19.gate_ref, bf16[8,128,256]{2,1,0:T(8,128)(2,1)} %get-tuple-element.20.query_t_ref, ...), custom_call_target="tpu_custom_call" | custom-call | flops 2147483648 | bytes 4194304 | tf_op jit(solution)/shard_map/solve_0/pallas_call | solution.py:422
  43.0 0.0 copy-done
  43.0 0.0 collective-permute-done.2.gram_ref
  43.0 0.0 copy-start.3
  43.0 0.7 %copy-done.3 = f32[4,72,128]{2,1,0:T(8,128)} copy-done((f32[4,72,128]{2,1,0:T(8,128)}, f32[4,72,128]{2,1,0:T(8,128)S(1)}, u32[]{:S(2)}) %copy-start.3) | copy-done | bytes 147480
  43.7 7.4 %solve_1.1 = (bf16[4,256,256]{2,1,0:T(8,128)(2,1)}, f32[4,256,128]{2,1,0:T(8,128)}) custom-call(s32[2]{0:T(128)} %pad_add_fusion.where_ref, f32[8]{0:T(128)} %ridge_ref.3, bf16[512,1024]{1,0:T(8,128)(2,1)} %key_ref.7, f32[8,256,256]{2,1,0:T(8,128)} %get-tuple-element.19.gate_ref, bf16[8,128,256]{2,1,0:T(8,128)(2,1)} %get-tuple-element.20.query_t_ref, ...), custom_call_target="tpu_custom_call" | custom-call | flops 2147483648 | bytes 4194304 | tf_op jit(solution)/shard_map/solve_1/pallas_call | solution.py:422
  51.1 3.0 %read_0.1.rest_0_ = bf16[256,1024]{1,0:T(8,128)(2,1)} custom-call(s32[2]{0:T(128)} %pad_add_fusion.where_ref, bf16[4,256,256]{2,1,0:T(8,128)(2,1)} %get-tuple-element.31.solution_ref, f32[4,256,128]{2,1,0:T(8,128)} %get-tuple-element.32.chunk_ref, f32[8,72,128]{2,1,0:T(8,128)} %get-tuple-element.24.mid_ref, f32[8,128,128]{2,1,0:T(8,128)} %get-tuple-element.29.mid_memory_ref, ...), custom_call_target="tpu_custom_call" | custom-call | flops 268435456 | bytes 4194304 | tf_op jit(solution)/shard_map/read_0/pallas_call | solution.py:476
  54.1 0.0 collective-permute-done.5.memory_ref
  54.2 0.0 copy-start.1
  54.2 0.7 %copy-done.1 = f32[4,128,128]{2,1,0:T(8,128)} copy-done((f32[4,128,128]{2,1,0:T(8,128)}, f32[4,128,128]{2,1,0:T(8,128)S(1)}, u32[]{:S(2)}) %copy-start.1) | copy-done | bytes 262168
  54.9 3.0 %read_1.1 = bf16[256,1024]{1,0:T(8,128)(2,1)} custom-call(s32[2]{0:T(128)} %pad_add_fusion.where_ref, bf16[4,256,256]{2,1,0:T(8,128)(2,1)} %get-tuple-element.27.solution_ref, f32[4,256,128]{2,1,0:T(8,128)} %get-tuple-element.28.chunk_ref, f32[8,72,128]{2,1,0:T(8,128)} %get-tuple-element.24.mid_ref, ...), custom_call_target="tpu_custom_call", output_to_operand_aliasing={{}: (6, {})} | custom-call | flops 268435456 | bytes 4194304 | tf_op jit(solution)/shard_map/read_1/pallas_call | solution.py:476
  (3 shorter events, 0.0 us)
Async XLA Ops:
  4.0 6.8 %collective-permute-start = (f32[4,72,128]{2,1,0:T(8,128)}, f32[4,72,128]{2,1,0:T(8,128)S(1)}, u32[]{:S(2)}, u32[]{:S(2)}) collective-permute-start(f32[4,72,128]{2,1,0:T(8,128)} %get-tuple-element.26), channel_id=1, source_target_pairs={{0,4},{4,8},{8,12},{1,5},{5,9},{9,13},{2,6},{6,10},{10,14},{3,7},{... | collective-permute-start | bytes 442376 | tf_op jit(solution)/shard_map/ppermute | solution.py:389
  5.3 11.2 %collective-permute-start.3 = (f32[4,128,128]{2,1,0:T(8,128)}, f32[4,128,128]{2,1,0:T(8,128)S(1)}, u32[]{:S(2)}, u32[]{:S(2)}) collective-permute-start(f32[4,128,128]{2,1,0:T(8,128)} %get-tuple-element.30), channel_id=1, source_target_pairs={{0,4},{4,8},{8,12},{1,5},{5,9},{9,13},{2,6},{6,10},{10,14},{3,7},{... | collective-permute-start | bytes 786440 | tf_op jit(solution)/shard_map/ppermute | solution.py:389
  11.8 14.4 %collective-permute-start.1 = (f32[4,72,128]{2,1,0:T(8,128)S(1)}, f32[4,72,128]{2,1,0:T(8,128)S(1)}, u32[]{:S(2)}, u32[]{:S(2)}) collective-permute-start(f32[4,72,128]{2,1,0:T(8,128)S(1)} %multiply_add_fusion.3), channel_id=1, source_target_pairs={{0,8},{4,12},{1,9},{5,13},{2,10},{6,14},{3,11},{7,15},{16,24},{20,... | collective-permute-start | bytes 442376 | tf_op jit(solution)/shard_map/ppermute | solution.py:397
  17.4 17.2 %collective-permute-start.4 = (f32[4,128,128]{2,1,0:T(8,128)S(1)}, f32[4,128,128]{2,1,0:T(8,128)S(1)}, u32[]{:S(2)}, u32[]{:S(2)}) collective-permute-start(f32[4,128,128]{2,1,0:T(8,128)S(1)} %multiply_add_fusion.1), channel_id=1, source_target_pairs={{0,8},{4,12},{1,9},{5,13},{2,10},{6,14},{3,11},{7,15},{16,24},{20,... | collective-permute-start | bytes 786440 | tf_op jit(solution)/shard_map/ppermute | solution.py:398
  26.3 9.3 %copy-start.2 = (f32[4,72,128]{2,1,0:T(8,128)}, f32[4,72,128]{2,1,0:T(8,128)S(1)}, u32[]{:S(2)}) copy-start(f32[4,72,128]{2,1,0:T(8,128)S(1)} %multiply_add_fusion.2.gram_ref) | copy-start | bytes 442372
  26.3 16.7 %collective-permute-start.2 = (f32[4,72,128]{2,1,0:T(8,128)S(1)}, f32[4,72,128]{2,1,0:T(8,128)S(1)}, u32[]{:S(2)}, u32[]{:S(2)}) collective-permute-start(f32[4,72,128]{2,1,0:T(8,128)S(1)} %multiply_add_fusion.2.gram_ref), channel_id=1, source_target_pairs={{0,1},{1,0},{2,3},{3,2},{4,5},{5,4},{6,7},{7,6},{8,9},{9,8},{10,11... | collective-permute-start | bytes 442376 | tf_op jit(solution)/shard_map/ppermute | solution.py:404
  34.7 8.3 %copy-start = (f32[4,128,128]{2,1,0:T(8,128)}, f32[4,128,128]{2,1,0:T(8,128)S(1)}, u32[]{:S(2)}) copy-start(f32[4,128,128]{2,1,0:T(8,128)S(1)} %multiply_add_fusion.memory_ref) | copy-start | bytes 786436
  34.7 19.5 %collective-permute-start.5 = (f32[4,128,128]{2,1,0:T(8,128)S(1)}, f32[4,128,128]{2,1,0:T(8,128)S(1)}, u32[]{:S(2)}, u32[]{:S(2)}) collective-permute-start(f32[4,128,128]{2,1,0:T(8,128)S(1)} %multiply_add_fusion.memory_ref), channel_id=1, source_target_pairs={{0,1},{1,0},{2,3},{3,2},{4,5},{5,4},{6,7},{7,6},{8,9},{9,8},{10,11... | collective-permute-start | bytes 786440 | tf_op jit(solution)/shard_map/ppermute | solution.py:404
  43.0 0.7 %copy-start.3 = (f32[4,72,128]{2,1,0:T(8,128)}, f32[4,72,128]{2,1,0:T(8,128)S(1)}, u32[]{:S(2)}) copy-start(f32[4,72,128]{2,1,0:T(8,128)S(1)} %collective-permute-done.2.gram_ref) | copy-start | bytes 442372
  54.2 0.7 %copy-start.1 = (f32[4,128,128]{2,1,0:T(8,128)}, f32[4,128,128]{2,1,0:T(8,128)S(1)}, u32[]{:S(2)}) copy-start(f32[4,128,128]{2,1,0:T(8,128)S(1)} %collective-permute-done.5.memory_ref) | copy-start | bytes 786436
where the time goes:
time: 58.4 us; the launch traced here: 57.9 us
  Pallas kernels  31.6 us (54%)
  waiting for transfers between devices  11.2 us (19%)
  starting transfers between devices  10.2 us (17%)
  other arithmetic  2.7 us (5%)
  local copies, waits for them, and re-layouts  2.11 us (4%)
    pallas_call x2, Pallas kernels, per_device(): call(functools.partial(solve_kernel, cores=cores, turn=turn, width=width)...  14.9 us
    pallas_call x1, Pallas kernels, per_device(): call(functools.partial(prepare_kernel, total=total, width=width), head_co...  7.29 us
    ppermute x2, waiting for transfers between devices, per_device(): gram_prior, memory_prior = (hop(gram_sum), hop(memory_sum))  6.82 us
    pallas_call x2, Pallas kernels, per_device(): call(functools.partial(read_kernel, width=width), 1, in_specs, pl.BlockSp...  6.09 us
    ppermute x2, starting transfers between devices, swap(): return lax.ppermute(x, 'sub', [(i, (i + 1) % cores) for i in range(cores)])  5.02 us
    ppermute x1, waiting for transfers between devices, per_device(): memory_in = hop(memory_sum + own_decay * memory_prior)  4.2 us
    pallas_call x1, Pallas kernels, per_device(): call(functools.partial(sums_kernel, total=total, heads=heads, width=width...  3.37 us
    ppermute x2, starting transfers between devices, per_device(): gram_prior, memory_prior = (hop(gram_sum), hop(memory_sum))  2.57 us
  transfers between devices with their start and end apart: 6, of which 4 were waited for; matrix products, arithmetic and copies ran while one was open for 5% of the time, Pallas kernels for 44%

commit v1 on v0

--- a/solution.py
+++ b/solution.py
@@ -12,7 +12,8 @@
 f32 = jnp.float32
 bf16 = jnp.bfloat16
 PAD = 8
-PER_STEP = 2
+PER_STEP = 4
+VMEM = 24 << 20
 
 
 def dot_nn(a, b):
@@ -207,67 +208,79 @@
     def row_sum(x):
         return jnp.sum(x, axis=0, keepdims=True)
 
-    ridge = [ridge_ref[base + i] for i in per_step]
-    carried = [carried_ref[pl.ds(base + i, 1), :] for i in per_step]
-    system, keys, key_pair = [], [], []
-    direction, residual, energy, result = [], [], [], []
-    for i in per_step:
+    def head_program(i):
         cols = slice(i * width, (i + 1) * width)
+        ridge = ridge_ref[base + i]
+        carried = carried_ref[pl.ds(base + i, 1), :]
         decay = mid_ref[i, half + 1 : half + 2, :]
         packed = mid_ref[i, :half, :] + decay * gram_ref[i, :half, :]
         diagonal = mid_ref[i, half : half + 1, :] + decay * gram_ref[i, half : half + 1, :]
         high, low = split(unpack_gram(packed, diagonal))
+        system = jnp.concatenate(
+            [jnp.concatenate([high, low], 0), jnp.concatenate([high, jnp.zeros_like(low)], 0)], 1
+        )
         key = key_ref[own, cols]
-        keys.append(jnp.concatenate([key, key], 1))
-        key_pair.append(jnp.concatenate([key_t_ref[i], key_t_ref[i]], 1))
-        system.append(
-            jnp.concatenate(
-                [jnp.concatenate([high, low], 0), jnp.concatenate([high, jnp.zeros_like(low)], 0)], 1
-            )
-        )
-        direction.append(query_t_ref[i].astype(f32))
-        residual.append(direction[i])
-        energy.append(row_sum(direction[i] * direction[i]))
-        result.append(None)
-    for iteration in range(ITERS):
-        last = iteration == ITERS - 1
-        earlier = []
-        parts = []
-        for i in per_step:
+        keys = jnp.concatenate([key, key], 1)
+        key_pair = jnp.concatenate([key_t_ref[i], key_t_ref[i]], 1)
+        query_t = query_t_ref[i]
+        direction = query_t.astype(f32)
+        residual = direction
+        energy = row_sum(direction * direction)
+        result = None
+        yield
+        for iteration in range(ITERS):
+            last = iteration == ITERS - 1
             if iteration == 0:
-                product = dot_nn(system[i][:, :width], query_t_ref[i])
+                product = dot_nn(system[:, :width], query_t)
             else:
-                pair = jnp.concatenate(split(direction[i]), 0)
-                product = dot_nn(system[i], pair)
-                plain = dot_nn(keys[i], pair)
-                parts.append((plain, plain * gate_ref[i]))
-            earlier.append(
-                carried[i] * (product[:width] + product[width:]) + ridge[i] * direction[i]
-            )
-        for i in per_step:
+                pair = jnp.concatenate(split(direction), 0)
+                plain = dot_nn(keys, pair)
+                product = dot_nn(system, pair)
+            yield
+            if iteration > 0:
+                weighted = plain * gate_ref[i]
+                if not last:
+                    weighted_pair = jnp.concatenate(split(weighted), 0)
+            earlier = carried * (product[:width] + product[width:]) + ridge * direction
+            yield
             if iteration == 0:
-                applied = earlier[i] + within_ref[i]
-                curvature = row_sum(direction[i] * applied)
+                applied = earlier + within_ref[i]
             elif not last:
-                applied = earlier[i] + dot_nn(key_pair[i], jnp.concatenate(split(parts[i][1]), 0))
-                curvature = row_sum(direction[i] * applied)
+                within = dot_nn(key_pair, weighted_pair)
+                yield
+                applied = earlier + within
+            if last:
+                curvature = row_sum(plain * weighted) + row_sum(direction * earlier)
             else:
-                curvature = row_sum(parts[i][0] * parts[i][1]) + row_sum(direction[i] * earlier[i])
-            stepsize = energy[i] / (curvature + guard)
-            moved = stepsize * direction[i]
-            result[i] = moved if iteration == 0 else result[i] + moved
+                curvature = row_sum(direction * applied)
+            stepsize = energy / (curvature + guard)
+            moved = stepsize * direction
+            result = moved if iteration == 0 else result + moved
             if not last:
-                residual[i] = residual[i] - stepsize * applied
-                energy_next = row_sum(residual[i] * residual[i])
-                direction[i] = residual[i] + (energy_next / (energy[i] + guard)) * direction[i]
-                energy[i] = energy_next
-    for i in per_step:
-        weighted = dot_nn(keys[i], jnp.concatenate(split(result[i]), 0)) * gate_ref[i]
+                residual = residual - stepsize * applied
+                energy_next = row_sum(residual * residual)
+                direction = residual + (energy_next / (energy + guard)) * direction
+                energy = energy_next
+            yield
+        plain = dot_nn(keys, jnp.concatenate(split(result), 0))
+        high, low = split(carried * result)
+        solution_ref[i] = jnp.concatenate([high.T, low.T], 1)
+        yield
+        weighted_pair = jnp.concatenate(split(plain * gate_ref[i]), 0)
+        yield
         value_t = value_t_ref[i]
-        chunk = dot_nn(jnp.concatenate([value_t, value_t], 1), jnp.concatenate(split(weighted), 0))
+        chunk = dot_nn(jnp.concatenate([value_t, value_t], 1), weighted_pair)
+        yield
         chunk_ref[i] = chunk.T
-        high, low = split(carried[i] * result[i])
-        solution_ref[i] = jnp.concatenate([high.T, low.T], 1)
+
+    programs = [head_program(i) for i in per_step]
+    running = []
+    while programs or running:
+        if programs:
+            running.append(programs.pop(0))
+        for program in list(running):
+            if next(program, running) is running:
+                running.remove(program)
 
 
 def read_kernel(where_ref, solution_ref, chunk_ref, mid_ref, mid_memory_ref, memory_ref, *rest, width):
@@ -316,6 +329,7 @@
             out_shape=out_shape,
             name=name,
             cost_estimate=pl.CostEstimate(flops=cost, bytes_accessed=4 << 20, transcendentals=0),
+            compiler_params=pltpu.CompilerParams(vmem_limit_bytes=VMEM),
             **options,
         )
 
@@ -397,8 +411,9 @@
             gram_in = hop(jnp.where(body, gram_sum, 0.0) + own_decay * gram_prior)
             memory_in = hop(memory_sum + own_decay * memory_prior)
             gram_prior = jnp.where(body, gram_prior, 0.0) + prior_decay * gram_in
-            memory_prior = memory_prior + prior_decay * memory_in
             covered = covered + shift
+            if covered < seq - 1:
+                memory_prior = memory_prior + prior_decay * memory_in
 
     def swap(x):
         return lax.ppermute(x, "sub", [(i, (i + 1) % cores) for i in range(cores)])
@@ -448,6 +463,9 @@
             )
         )
 
+    if covered > 1:
+        solved, memory_in = lax.optimization_barrier((solved, memory_in))
+        memory_prior = memory_prior + prior_decay * memory_in
     output = None
     for turn in range(cores):
 

time: 58.4 us -> 45.7 us (0.78)
  Pallas kernels: 31.6 us -> 17.4 us
  starting transfers between devices: 10.2 us -> 17.9 us
  waiting for transfers between devices: 11.2 us -> 5.11 us
  local copies, waits for them, and re-layouts: 2.11 us -> 4.5 us
  other arithmetic: 2.7 us -> 0.33 us
    ppermute x2, starting transfers between devices: 5.02 us -> 12.7 us  [swap(): return lax.ppermute(x, 'sub', [(i, (i + 1) % cores) for i in range(cores)])]
    pallas_call x2, Pallas kernels: 14.9 us -> 8.22 us  [per_device(): call(functools.partial(solve_kernel, cores=cores, turn=turn, width=width)...]
    ppermute x1, waiting for transfers between devices: 4.2 us -> 0.01 us  [per_device(): memory_in = hop(memory_sum + own_decay * memory_prior)]
    pallas_call x1, Pallas kernels: 7.29 us -> 4.14 us  [per_device(): call(functools.partial(prepare_kernel, total=total, width=width), head_co...]
    unnamed x8 -> x18, local copies, waits for them, and re-layouts: 1.38 us -> 4.49 us
    pallas_call x2, Pallas kernels: 6.09 us -> 3.15 us  [per_device(): call(functools.partial(read_kernel, width=width), 1, in_specs, pl.BlockSp...]
    ppermute x2, waiting for transfers between devices: 6.82 us -> 4.01 us  [per_device(): gram_prior, memory_prior = (hop(gram_sum), hop(memory_sum))]
    pallas_call x1, Pallas kernels: 3.37 us -> 1.9 us  [per_device(): call(functools.partial(sums_kernel, total=total, heads=heads, width=width...]
  transfers between devices with their start and end apart: 6 -> 6, of which waited for: 4 -> 2; matrix products, arithmetic and copies ran while one was open for 5% -> 0% of each run, Pallas kernels for 44% -> 31%
where the time goes in v1:
time: 45.7 us; the launch traced here: 45.4 us
  starting transfers between devices  17.9 us (39%)
  Pallas kernels  17.4 us (38%)
  waiting for transfers between devices  5.11 us (11%)
  local copies, waits for them, and re-layouts  4.5 us (10%)
    ppermute x2, starting transfers between devices, swap(): return lax.ppermute(x, 'sub', [(i, (i + 1) % cores) for i in range(cores)])  12.7 us
    pallas_call x2, Pallas kernels, per_device(): call(functools.partial(solve_kernel, cores=cores, turn=turn, width=width)...  8.22 us
    unnamed x18, local copies, waits for them, and re-layouts  4.49 us
    pallas_call x1, Pallas kernels, per_device(): call(functools.partial(prepare_kernel, total=total, width=width), head_co...  4.14 us
    ppermute x2, waiting for transfers between devices, per_device(): gram_prior, memory_prior = (hop(gram_sum), hop(memory_sum))  4.01 us
    pallas_call x2, Pallas kernels, per_device(): call(functools.partial(read_kernel, width=width), 1, in_specs, pl.BlockSp...  3.15 us
    ppermute x2, starting transfers between devices, per_device(): gram_prior, memory_prior = (hop(gram_sum), hop(memory_sum))  2.58 us
    pallas_call x1, Pallas kernels, per_device(): call(functools.partial(sums_kernel, total=total, heads=heads, width=width...  1.9 us
  transfers between devices with their start and end apart: 6, of which 2 were waited for; matrix products, arithmetic and copies ran while one was open for 0% of the time, Pallas kernels for 31%

profile of v1, /device:TPU:31, one launch (start us, length us, event | category | flops | bytes accessed | tf_op | source)
XLA Modules:
  0.0 45.4 jit_solution(13142033602452644207)
XLA Ops:
  0.0 0.1 pad_add_fusion.where_ref
  0.1 0.0 copy-start
  0.1 1.2 %copy-done = bf16[512,1024]{1,0:T(8,128)(2,1)S(1)} copy-done((bf16[512,1024]{1,0:T(8,128)(2,1)S(1)}, bf16[512,1024]{1,0:T(8,128)(2,1)}, u32[]{:S(2)}) %copy-start) | copy-done | bytes 1048600
  1.3 1.2 %copy-done.2 = bf16[512,1024]{1,0:T(8,128)(2,1)S(1)} copy-done((bf16[512,1024]{1,0:T(8,128)(2,1)S(1)}, bf16[512,1024]{1,0:T(8,128)(2,1)}, u32[]{:S(2)}) %copy-start.2) | copy-done | bytes 1048600
  2.5 0.7 %copy-done.5 = s32[512,8]{0,1:T(8,128)S(1)} copy-done((s32[512,8]{0,1:T(8,128)S(1)}, s32[512,8]{0,1:T(8,128)}, u32[]{:S(2)}) %copy-start.5) | copy-done | bytes 16408
  3.2 0.7 %copy-done.6 = s32[3]{0:T(128)S(1)} copy-done((s32[3]{0:T(128)S(1)}, s32[3]{0:T(128)}, u32[]{:S(2)}) %copy-start.6) | copy-done | bytes 36
  3.9 0.7 %copy-done.7 = f32[8]{0:T(128)S(1)} copy-done((f32[8]{0:T(128)S(1)}, f32[8]{0:T(128)}, u32[]{:S(2)}) %copy-start.7) | copy-done | bytes 56
  4.6 1.9 %shard_sums.1 = (f32[4,72,128]{2,1,0:T(8,128)S(1)}, f32[4,128,128]{2,1,0:T(8,128)S(1)}) custom-call(s32[2]{0:T(128)S(1)} %pad_add_fusion.where_ref, s32[3]{0:T(128)S(1)} %copy-done.6, f32[8]{0:T(128)S(1)} %copy-done.7, bf16[512,1024]{1,0:T(8,128)(2,1)S(1)} %copy-done.2, bf16[512,1024]{1,0:T(8,128)(2,1)S(1)} %copy-done, s32[8,512]{1,0:T(8,128)S(1)} %bitcast.5), custom_call_target="tpu_custom_call" | custom-call | flops 1073741824 | bytes 4194304 | tf_op jit(solution)/shard_map/shard_sums/pallas_call | solution.py:337
  6.5 1.3 %collective-permute-start = (f32[4,72,128]{2,1,0:T(8,128)S(1)}, f32[4,72,128]{2,1,0:T(8,128)S(1)}, u32[]{:S(2)}, u32[]{:S(2)}) collective-permute-start(f32[4,72,128]{2,1,0:T(8,128)S(1)} %get-tuple-element.31), channel_id=1, source_target_pairs={{0,4},{4,8},{8,12},{1,5},{5,9},{9,13},{2,6},{6,10},{10,14},{3,7},{... | collective-permute-start | bytes 442376 | tf_op jit(solution)/shard_map/ppermute | solution.py:403
  7.8 0.0 copy-start.8
  7.8 1.3 %collective-permute-start.3 = (f32[4,128,128]{2,1,0:T(8,128)S(1)}, f32[4,128,128]{2,1,0:T(8,128)S(1)}, u32[]{:S(2)}, u32[]{:S(2)}) collective-permute-start(f32[4,128,128]{2,1,0:T(8,128)S(1)} %get-tuple-element.36), channel_id=1, source_target_pairs={{0,4},{4,8},{8,12},{1,5},{5,9},{9,13},{2,6},{6,10},{10,14},{3,7},{... | collective-permute-start | bytes 786440 | tf_op jit(solution)/shard_map/ppermute | solution.py:403
  9.1 0.0 copy-done.1
  9.1 0.0 copy-done.3
  9.1 0.0 copy-done.4
  9.1 4.1 %prepare.1 = (f32[8,256,256]{2,1,0:T(8,128)S(1)}, bf16[8,128,256]{2,1,0:T(8,128)(2,1)S(1)}, bf16[8,128,256]{2,1,0:T(8,128)(2,1)S(1)}, bf16[8,128,256]{2,1,0:T(8,...) custom-call(s32[2]{0:T(128)S(1)} %pad_add_fusion.where_ref, ...), custom_call_target="tpu_custom_call" | custom-call | flops 4294967296 | bytes 4194304 | tf_op jit(solution)/shard_map/prepare/pallas_call | solution.py:362
  13.3 0.0 collective-permute-done
  13.3 0.1 multiply_add_fusion.3
  13.4 1.3 %collective-permute-start.1 = (f32[4,72,128]{2,1,0:T(8,128)S(1)}, f32[4,72,128]{2,1,0:T(8,128)S(1)}, u32[]{:S(2)}, u32[]{:S(2)}) collective-permute-start(f32[4,72,128]{2,1,0:T(8,128)S(1)} %multiply_add_fusion.3), channel_id=1, source_target_pairs={{0,8},{4,12},{1,9},{5,13},{2,10},{6,14},{3,11},{7,15},{16,24},{20,... | collective-permute-start | bytes 442376 | tf_op jit(solution)/shard_map/ppermute | solution.py:411
  14.7 4.0 %collective-permute-done.3 = f32[4,128,128]{2,1,0:T(8,128)S(1)} collective-permute-done((f32[4,128,128]{2,1,0:T(8,128)S(1)}, f32[4,128,128]{2,1,0:T(8,128)S(1)}, u32[]{:S(2)}, u32[]{:S(2)}) %collective-permute-start.3) | collective-permute-done | bytes 262176 | tf_op jit(solution)/shard_map/ppermute | solution.py:403
  18.7 1.3 %collective-permute-start.4 = (f32[4,128,128]{2,1,0:T(8,128)S(1)}, f32[4,128,128]{2,1,0:T(8,128)S(1)}, u32[]{:S(2)}, u32[]{:S(2)}) collective-permute-start(f32[4,128,128]{2,1,0:T(8,128)S(1)} %multiply_add_fusion.1), channel_id=1, source_target_pairs={{0,8},{4,12},{1,9},{5,13},{2,10},{6,14},{3,11},{7,15},{16,24},{20,... | collective-permute-start | bytes 786440 | tf_op jit(solution)/shard_map/ppermute | solution.py:412
  20.0 1.1 %collective-permute-done.1 = f32[4,72,128]{2,1,0:T(8,128)S(1)} collective-permute-done((f32[4,72,128]{2,1,0:T(8,128)S(1)}, f32[4,72,128]{2,1,0:T(8,128)S(1)}, u32[]{:S(2)}, u32[]{:S(2)}) %collective-permute-start.1) | collective-permute-done | bytes 147488 | tf_op jit(solution)/shard_map/ppermute | solution.py:411
  21.1 0.1 multiply_add_fusion.2.gram_ref
  21.2 12.6 %collective-permute-start.2 = (f32[4,72,128]{2,1,0:T(8,128)S(1)}, f32[4,72,128]{2,1,0:T(8,128)S(1)}, u32[]{:S(2)}, u32[]{:S(2)}) collective-permute-start(f32[4,72,128]{2,1,0:T(8,128)S(1)} %multiply_add_fusion.2.gram_ref), channel_id=1, source_target_pairs={{0,1},{1,0},{2,3},{3,2},{4,5},{5,4},{6,7},{7,6},{8,9},{9,8},{10,11... | collective-permute-start | bytes 442376 | tf_op jit(solution)/shard_map/ppermute | solution.py:419
  33.8 0.0 copy-done.8
  33.8 4.1 %solve_0.1 = (bf16[4,256,256]{2,1,0:T(8,128)(2,1)S(1)}, f32[4,256,128]{2,1,0:T(8,128)S(1)}) custom-call(s32[2]{0:T(128)S(1)} %pad_add_fusion.where_ref, f32[8]{0:T(128)S(1)} %copy-done.8, bf16[512,1024]{1,0:T(8,128)(2,1)S(1)} %copy-done.3, f32[8,256,256]{2,1,0:T(8,128)S(1)} %get-tuple-element.24.gate_ref, ...), custom_call_target="tpu_custom_call" | custom-call | flops 2147483648 | bytes 4194304 | tf_op jit(solution)/shard_map/solve_0/pallas_call | solution.py:437
  37.9 0.0 collective-permute-done.2.gram_ref
  38.0 4.1 %solve_1.1 = (bf16[4,256,256]{2,1,0:T(8,128)(2,1)S(1)}, f32[4,256,128]{2,1,0:T(8,128)S(1)}) custom-call(s32[2]{0:T(128)S(1)} %pad_add_fusion.where_ref, f32[8]{0:T(128)S(1)} %copy-done.8, bf16[512,1024]{1,0:T(8,128)(2,1)S(1)} %copy-done.3, f32[8,256,256]{2,1,0:T(8,128)S(1)} %get-tuple-element.24.gate_ref, ...), custom_call_target="tpu_custom_call" | custom-call | flops 2147483648 | bytes 4194304 | tf_op jit(solution)/shard_map/solve_1/pallas_call | solution.py:437
  42.1 0.0 collective-permute-done.4
  42.1 0.1 collective-permute-start.5
  42.2 1.6 %read_0.1.rest_0_ = bf16[256,1024]{1,0:T(8,128)(2,1)} custom-call(s32[2]{0:T(128)S(1)} %pad_add_fusion.where_ref, bf16[4,256,256]{2,1,0:T(8,128)(2,1)S(1)} %get-tuple-element.41.solution_ref, f32[4,256,128]{2,1,0:T(8,128)S(1)} %get-tuple-element.42.chunk_ref, f32[8,72,128]{2,1,0:T(8,128)S(1)} %get-tuple-element.29.mid_ref, ...), custom_call_target="tpu_custom_call" | custom-call | flops 268435456 | bytes 4194304 | tf_op jit(solution)/shard_map/read_0/pallas_call | solution.py:494
  43.8 0.0 collective-permute-done.5.memory_ref
  43.8 1.6 %read_1.1 = bf16[256,1024]{1,0:T(8,128)(2,1)} custom-call(s32[2]{0:T(128)S(1)} %pad_add_fusion.where_ref, bf16[4,256,256]{2,1,0:T(8,128)(2,1)S(1)} %get-tuple-element.37.solution_ref, f32[4,256,128]{2,1,0:T(8,128)S(1)} %get-tuple-element.38.chunk_ref, f32[8,72,128]{2,1,0:T(8,128)S(1)} %get-tuple-element.29.mid_ref, ...), custom_call_target="tpu_custom_call", output_to_operand_aliasing={{}: (6, {})} | custom-call | flops 268435456 | bytes 4194304 | tf_op jit(solution)/shard_map/read_1/pallas_call | solution.py:494
  (12 shorter events, 0.1 us)
Async XLA Ops:
  0.1 1.2 %copy-start = (bf16[512,1024]{1,0:T(8,128)(2,1)S(1)}, bf16[512,1024]{1,0:T(8,128)(2,1)}, u32[]{:S(2)}) copy-start(bf16[512,1024]{1,0:T(8,128)(2,1)} %value_ref.3) | copy-start | bytes 3145732
  1.3 1.2 %copy-start.2 = (bf16[512,1024]{1,0:T(8,128)(2,1)S(1)}, bf16[512,1024]{1,0:T(8,128)(2,1)}, u32[]{:S(2)}) copy-start(bf16[512,1024]{1,0:T(8,128)(2,1)} %key_ref.7) | copy-start | bytes 3145732
  2.5 0.7 %copy-start.5 = (s32[512,8]{0,1:T(8,128)S(1)}, s32[512,8]{0,1:T(8,128)}, u32[]{:S(2)}) copy-start(s32[512,8]{0,1:T(8,128)} %param.10) | copy-start | bytes 49156
  3.2 0.7 %copy-start.6 = (s32[3]{0:T(128)S(1)}, s32[3]{0:T(128)}, u32[]{:S(2)}) copy-start(s32[3]{0:T(128)} %doc_ref.3) | copy-start | bytes 40
  3.9 0.7 %copy-start.7 = (f32[8]{0:T(128)S(1)}, f32[8]{0:T(128)}, u32[]{:S(2)}) copy-start(f32[8]{0:T(128)} %rate_ref.3) | copy-start | bytes 100
  4.6 4.5 %copy-start.1 = (bf16[512,1024]{1,0:T(8,128)(2,1)S(1)}, bf16[512,1024]{1,0:T(8,128)(2,1)}, u32[]{:S(2)}) copy-start(bf16[512,1024]{1,0:T(8,128)(2,1)} %value_ref.3) | copy-start | bytes 3145732
  4.6 4.5 %copy-start.3 = (bf16[512,1024]{1,0:T(8,128)(2,1)S(1)}, bf16[512,1024]{1,0:T(8,128)(2,1)}, u32[]{:S(2)}) copy-start(bf16[512,1024]{1,0:T(8,128)(2,1)} %key_ref.7) | copy-start | bytes 3145732
  4.6 4.5 %copy-start.4 = (bf16[256,1024]{1,0:T(8,128)(2,1)S(1)}, bf16[256,1024]{1,0:T(8,128)(2,1)}, u32[]{:S(2)}) copy-start(bf16[256,1024]{1,0:T(8,128)(2,1)} %query_ref.1) | copy-start | bytes 1572868
  6.5 6.8 %collective-permute-start = (f32[4,72,128]{2,1,0:T(8,128)S(1)}, f32[4,72,128]{2,1,0:T(8,128)S(1)}, u32[]{:S(2)}, u32[]{:S(2)}) collective-permute-start(f32[4,72,128]{2,1,0:T(8,128)S(1)} %get-tuple-element.31), channel_id=1, source_target_pairs={{0,4},{4,8},{8,12},{1,5},{5,9},{9,13},{2,6},{6,10},{10,14},{3,7},{... | collective-permute-start | bytes 442376 | tf_op jit(solution)/shard_map/ppermute | solution.py:403
  7.8 26.1 %copy-start.8 = (f32[8]{0:T(128)S(1)}, f32[8]{0:T(128)}, u32[]{:S(2)}) copy-start(f32[8]{0:T(128)} %ridge_ref.3) | copy-start | bytes 100
  7.8 10.9 %collective-permute-start.3 = (f32[4,128,128]{2,1,0:T(8,128)S(1)}, f32[4,128,128]{2,1,0:T(8,128)S(1)}, u32[]{:S(2)}, u32[]{:S(2)}) collective-permute-start(f32[4,128,128]{2,1,0:T(8,128)S(1)} %get-tuple-element.36), channel_id=1, source_target_pairs={{0,4},{4,8},{8,12},{1,5},{5,9},{9,13},{2,6},{6,10},{10,14},{3,7},{... | collective-permute-start | bytes 786440 | tf_op jit(solution)/shard_map/ppermute | solution.py:403
  13.4 7.7 %collective-permute-start.1 = (f32[4,72,128]{2,1,0:T(8,128)S(1)}, f32[4,72,128]{2,1,0:T(8,128)S(1)}, u32[]{:S(2)}, u32[]{:S(2)}) collective-permute-start(f32[4,72,128]{2,1,0:T(8,128)S(1)} %multiply_add_fusion.3), channel_id=1, source_target_pairs={{0,8},{4,12},{1,9},{5,13},{2,10},{6,14},{3,11},{7,15},{16,24},{20,... | collective-permute-start | bytes 442376 | tf_op jit(solution)/shard_map/ppermute | solution.py:411
  18.7 23.3 %collective-permute-start.4 = (f32[4,128,128]{2,1,0:T(8,128)S(1)}, f32[4,128,128]{2,1,0:T(8,128)S(1)}, u32[]{:S(2)}, u32[]{:S(2)}) collective-permute-start(f32[4,128,128]{2,1,0:T(8,128)S(1)} %multiply_add_fusion.1), channel_id=1, source_target_pairs={{0,8},{4,12},{1,9},{5,13},{2,10},{6,14},{3,11},{7,15},{16,24},{20,... | collective-permute-start | bytes 786440 | tf_op jit(solution)/shard_map/ppermute | solution.py:412
  21.2 16.7 %collective-permute-start.2 = (f32[4,72,128]{2,1,0:T(8,128)S(1)}, f32[4,72,128]{2,1,0:T(8,128)S(1)}, u32[]{:S(2)}, u32[]{:S(2)}) collective-permute-start(f32[4,72,128]{2,1,0:T(8,128)S(1)} %multiply_add_fusion.2.gram_ref), channel_id=1, source_target_pairs={{0,1},{1,0},{2,3},{3,2},{4,5},{5,4},{6,7},{7,6},{8,9},{9,8},{10,11... | collective-permute-start | bytes 442376 | tf_op jit(solution)/shard_map/ppermute | solution.py:419
  42.1 1.7 %collective-permute-start.5 = (f32[4,128,128]{2,1,0:T(8,128)S(1)}, f32[4,128,128]{2,1,0:T(8,128)S(1)}, u32[]{:S(2)}, u32[]{:S(2)}) collective-permute-start(f32[4,128,128]{2,1,0:T(8,128)S(1)} %multiply_add_fusion.memory_ref), channel_id=1, source_target_pairs={{0,1},{1,0},{2,3},{3,2},{4,5},{5,4},{6,7},{7,6},{8,9},{9,8},{10,11... | collective-permute-start | bytes 786440 | tf_op jit(solution)/shard_map/ppermute | solution.py:419

commit v2 on v1

--- a/solution.py
+++ b/solution.py
@@ -102,12 +102,20 @@
 
 
 def sums_kernel(
-    where_ref, doc_ref, rate_ref, key_ref, value_ref, bins_ref, gram_ref, memory_ref, weight_ref, decay_ref,
-    *, total, heads, width,
+    where_ref, doc_ref, rate_ref, key_hbm, value_hbm, bins_ref, gram_ref, memory_ref, *rest,
+    total, heads, width, cut,
 ):
-    shard = key_ref.shape[0]
+    weight_ref, decay_ref, both_ref, sems = rest[-4:]
+    shard = key_hbm.shape[0]
     first = where_ref[0] * shard
     core = where_ref[1]
+    copies = []
+    for i in range(heads):
+        cols = pl.ds(pl.multiple_of((core * heads + i) * width, width), width)
+        for part, source in enumerate((key_hbm, value_hbm)):
+            target = both_ref.at[part, i]
+            copies.append(pltpu.make_async_copy(source.at[:, cols], target, sems.at[i, part]))
+            copies[-1].start()
     scale = scale_column(rate_ref, total)
     cumulative = running_rows(bins_ref[...])
     last = cumulative[:, shard - 1 :]
@@ -120,14 +128,53 @@
     decay_ref[...] = jnp.broadcast_to(jnp.where(through, jnp.exp(scale * last), 0.0), decay_ref.shape)
     for i in range(heads):
         head = core * heads + i
-        cols = slice(i * width, (i + 1) * width)
-        key = key_ref[:, cols]
-        both = jnp.concatenate([key, value_ref[:, cols]], 1)
+        copies[2 * i].wait()
+        copies[2 * i + 1].wait()
+        key = both_ref[0, i]
+        both = jnp.concatenate([key, both_ref[1, i]], 1)
         sums = weighted_sums(key.T, weight_ref[pl.ds(head, 1), :], both)
-        packed, tail = pack_gram(sums[:, :width], decay_ref[pl.ds(head, 1), :])
-        gram_ref[i, : width // 2, :] = packed
-        gram_ref[i, width // 2 :, :] = tail
-        memory_ref[i] = sums[:, width:]
+        state = jnp.concatenate(pack_gram(sums[:, :width], decay_ref[pl.ds(head, 1), :]), 0)
+        if cut == 0:
+            gram_ref[i] = state
+            memory_ref[i] = sums[:, width:]
+        else:
+            gram_second, memory_second, gram_sent, memory_sent = rest[:4]
+            at = i % cut
+            (gram_ref if i < cut else gram_second)[at] = state
+            (memory_ref if i < cut else memory_second)[at] = sums[:, width:]
+
+            @pl.when((where_ref[0] == 1) == (i >= cut))
+            def _(at=at, state=state, sums=sums):
+                gram_sent[at] = state
+                memory_sent[at] = sums[:, width:]
+
+
+def between_kernel(
+    where_ref, first_ref, second_ref, near_ref, far_ref, gram_first, gram_second, gram_near,
+    ahead_ref, sent_ref, joined_ref, *, half,
+):
+    place = where_ref[0]
+    line = slice(half + 1, half + 2)
+    for i in range(first_ref.shape[0]):
+        near = near_ref[i]
+        ahead = first_ref[i] + gram_first[i, line, :] * near
+        joined = near + gram_near[i, line, :] * far_ref[i]
+        second = second_ref[i]
+        behind = second + gram_second[i, line, :] * joined
+        ahead_ref[i] = ahead
+        joined_ref[i] = joined
+        sent_ref[i] = jnp.where(place == 1, ahead, jnp.where(place == 2, behind, second))
+
+
+def gather_kernel(where_ref, near_ref, joined_ref, nearer_ref, farther_ref, gram_near, prior_ref, *, half):
+    place = where_ref[0]
+    cut = near_ref.shape[0]
+    line = slice(half + 1, half + 2)
+    for i in range(cut):
+        nearer = nearer_ref[i]
+        own = near_ref[i] + gram_near[i, line, :] * farther_ref[i]
+        prior_ref[i] = jnp.where(place == 2, nearer, own)
+        prior_ref[cut + i] = jnp.where(place == 2, joined_ref[i], nearer)
 
 
 def prepare_kernel(
@@ -202,27 +249,30 @@
     group = lax.rem(core + turn, cores)
     own = pl.ds(pl.multiple_of(core * rows, rows), rows)
     half = width // 2
-    per_step = range(query_t_ref.shape[0])
-    base = (group * steps + pl.program_id(0)) * query_t_ref.shape[0]
+    step = gram_ref.shape[0] // steps
+    skip = pl.program_id(0) * step
+    per_step = range(step)
+    base = group * gram_ref.shape[0] + skip
 
     def row_sum(x):
         return jnp.sum(x, axis=0, keepdims=True)
 
     def head_program(i):
-        cols = slice(i * width, (i + 1) * width)
-        ridge = ridge_ref[base + i]
-        carried = carried_ref[pl.ds(base + i, 1), :]
-        decay = mid_ref[i, half + 1 : half + 2, :]
-        packed = mid_ref[i, :half, :] + decay * gram_ref[i, :half, :]
-        diagonal = mid_ref[i, half : half + 1, :] + decay * gram_ref[i, half : half + 1, :]
+        head = base + i
+        cols = pl.ds(pl.multiple_of(head * width, width), width)
+        ridge = ridge_ref[head]
+        carried = carried_ref[pl.ds(head, 1), :]
+        decay = mid_ref[head, half + 1 : half + 2, :]
+        packed = mid_ref[head, :half, :] + decay * gram_ref[skip + i, :half, :]
+        diagonal = mid_ref[head, half : half + 1, :] + decay * gram_ref[skip + i, half : half + 1, :]
         high, low = split(unpack_gram(packed, diagonal))
         system = jnp.concatenate(
             [jnp.concatenate([high, low], 0), jnp.concatenate([high, jnp.zeros_like(low)], 0)], 1
         )
         key = key_ref[own, cols]
         keys = jnp.concatenate([key, key], 1)
-        key_pair = jnp.concatenate([key_t_ref[i], key_t_ref[i]], 1)
-        query_t = query_t_ref[i]
+        key_pair = jnp.concatenate([key_t_ref[head], key_t_ref[head]], 1)
+        query_t = query_t_ref[head]
         direction = query_t.astype(f32)
         residual = direction
         energy = row_sum(direction * direction)
@@ -238,13 +288,13 @@
                 product = dot_nn(system, pair)
             yield
             if iteration > 0:
-                weighted = plain * gate_ref[i]
+                weighted = plain * gate_ref[head]
                 if not last:
                     weighted_pair = jnp.concatenate(split(weighted), 0)
             earlier = carried * (product[:width] + product[width:]) + ridge * direction
             yield
             if iteration == 0:
-                applied = earlier + within_ref[i]
+                applied = earlier + within_ref[head]
             elif not last:
                 within = dot_nn(key_pair, weighted_pair)
                 yield
@@ -264,14 +314,14 @@
             yield
         plain = dot_nn(keys, jnp.concatenate(split(result), 0))
         high, low = split(carried * result)
-        solution_ref[i] = jnp.concatenate([high.T, low.T], 1)
+        solution_ref[skip + i] = jnp.concatenate([high.T, low.T], 1)
         yield
-        weighted_pair = jnp.concatenate(split(plain * gate_ref[i]), 0)
+        weighted_pair = jnp.concatenate(split(plain * gate_ref[head]), 0)
         yield
-        value_t = value_t_ref[i]
+        value_t = value_t_ref[head]
         chunk = dot_nn(jnp.concatenate([value_t, value_t], 1), weighted_pair)
         yield
-        chunk_ref[i] = chunk.T
+        chunk_ref[skip + i] = chunk.T
 
     programs = [head_program(i) for i in per_step]
     running = []
@@ -283,12 +333,14 @@
                 running.remove(program)
 
 
-def read_kernel(where_ref, solution_ref, chunk_ref, mid_ref, mid_memory_ref, memory_ref, *rest, width):
+def read_kernel(where_ref, solution_ref, chunk_ref, mid_ref, mid_memory_ref, memory_ref, *rest, cores, turn, width):
     out_ref = rest[-1]
     half = width // 2
-    for i in range(solution_ref.shape[0]):
-        decay = mid_ref[i, 1:2, :]
-        memory = mid_memory_ref[i] + decay * memory_ref[i]
+    heads = solution_ref.shape[0]
+    base = lax.rem(where_ref[1] + turn, cores) * heads
+    for i in range(heads):
+        decay = mid_ref[base + i, half + 1 : half + 2, :]
+        memory = mid_memory_ref[base + i] + decay * memory_ref[i]
         high, low = split(memory)
         pair = jnp.concatenate(
             [jnp.concatenate([high, high], 0), jnp.concatenate([low, jnp.zeros_like(low)], 0)], 1
@@ -312,6 +364,11 @@
     bins = gate_bins.T
     smem = pl.BlockSpec(memory_space=pltpu.SMEM)
     any_space = pl.BlockSpec(memory_space=pl.ANY)
+    hbm = pl.BlockSpec(memory_space=pltpu.HBM)
+    vmem = pl.BlockSpec(memory_space=pltpu.VMEM)
+
+    def pinned(x):
+        return pltpu.with_memory_space_constraint(x, pltpu.HBM)
 
     def full(*shape):
         return pl.BlockSpec(shape, lambda i, where_ref: (0,) * len(shape))
@@ -333,20 +390,25 @@
             **options,
         )
 
-    group = pl.BlockSpec((shard, heads * width), lambda i, where_ref: (0, where_ref[1]))
-    gram_sum, memory_sum = call(
-        functools.partial(sums_kernel, total=total, heads=heads, width=width),
+    cut = heads // 2 if seq == 4 and heads % 2 == 0 else 0
+    part = cut or heads
+    gram_shape = jax.ShapeDtypeStruct((part, half + PAD, width), f32)
+    memory_shape = jax.ShapeDtypeStruct((part, width, width), f32)
+    sums = call(
+        functools.partial(sums_kernel, total=total, heads=heads, width=width, cut=cut),
         1,
-        [smem, smem, group, group, full(head_count, shard)],
-        [full(heads, half + PAD, width), full(heads, width, width)],
+        [smem, smem, hbm, hbm, full(head_count, shard)],
+        [vmem] * (6 if cut else 2),
+        [gram_shape, memory_shape] * (3 if cut else 1),
         [
-            jax.ShapeDtypeStruct((heads, half + PAD, width), f32),
-            jax.ShapeDtypeStruct((heads, width, width), f32),
+            pltpu.VMEM((head_count, shard), f32),
+            pltpu.VMEM((head_count, width), f32),
+            pltpu.VMEM((2, heads, shard, width), bf16),
+            pltpu.SemaphoreType.DMA((heads, 2)),
         ],
-        [pltpu.VMEM((head_count, shard), f32), pltpu.VMEM((head_count, width), f32)],
         "shard_sums",
         1 << 30,
-    )(where, doc_lengths, decay_rates, key_vectors, value_vectors, bins)
+    )(where, pinned(doc_lengths), pinned(decay_rates), pinned(key_vectors), pinned(value_vectors), pinned(bins))
 
     step = min(PER_STEP, heads)
 
@@ -393,27 +455,74 @@
         4 << 30,
     )(where, doc_lengths, decay_rates, queries, key_vectors, value_vectors, bins)
 
-    own_decay = gram_sum[:, half + 1 : half + 2, :]
-    body = (jnp.arange(half + PAD) < half + 1)[None, :, None]
-    gram_prior = memory_prior = None
-    covered = 0
-    while covered < seq - 1:
-        if covered == 0:
-            hop = functools.partial(lax.ppermute, axis_name="seq", perm=[(i, i + 1) for i in range(seq - 1)])
-            gram_prior, memory_prior = hop(gram_sum), hop(memory_sum)
-            covered = 1
-        else:
+    def hop(x, pairs):
+        return lax.ppermute(x, "seq", pairs)
+
+    def after(x, *others):
+        return lax.optimization_barrier((x, others))[0]
+
+    if cut:
+        gram_first, memory_first, gram_second, memory_second, gram_sent, memory_sent = sums
+        chain, jump, leap = [(0, 1), (1, 2), (2, 3)], [(0, 2)], [(1, 3)]
+
+        def between(first, second, near, far):
+            return call(
+                functools.partial(between_kernel, half=half),
+                1,
+                [vmem] * 7,
+                [vmem] * 3,
+                [jax.ShapeDtypeStruct(first.shape, f32)] * 3,
+                [],
+                "between",
+                1 << 20,
+            )(where, first, second, near, far, gram_first, gram_second, gram_near)
+
+        def gathered(near, joined, nearer, farther):
+            return call(
+                functools.partial(gather_kernel, half=half),
+                1,
+                [vmem] * 5,
+                vmem,
+                jax.ShapeDtypeStruct((heads, *near.shape[1:]), f32),
+                [],
+                "gather",
+                1 << 20,
+            )(where, near, joined, nearer, farther, gram_near)
+
+        gram_near, gram_far = hop(gram_sent, chain), hop(gram_second, jump)
+        memory_near, memory_far = hop(memory_sent, chain), hop(memory_second, jump)
+        gram_ahead, gram_sent, gram_joined = between(gram_first, gram_second, gram_near, gram_far)
+        gram_nearer, gram_farther = hop(gram_sent, chain), hop(gram_ahead, leap)
+        gram_prior = gathered(gram_near, gram_joined, gram_nearer, gram_farther)
+        memory_ahead, memory_sent, memory_joined = between(memory_first, memory_second, memory_near, memory_far)
+        memory_sent, memory_ahead = after((memory_sent, memory_ahead), gram_nearer, gram_farther)
+        memory_nearer, memory_farther = hop(memory_sent, chain), hop(memory_ahead, leap)
+
+        def memory_at(*ready):
+            nearer, farther = after((memory_nearer, memory_farther), *ready)
+            return gathered(memory_near, memory_joined, nearer, farther)
+
+    else:
+        gram_sum, memory_sum = sums
+        own_decay = gram_sum[:, half + 1 : half + 2, :]
+        body = (jnp.arange(half + PAD) < half + 1)[None, :, None]
+        gram_prior, memory_prior = jnp.zeros_like(gram_sum), jnp.zeros_like(memory_sum)
+        covered = 0
+        while covered < seq - 1:
             shift = covered + 1
-            hop = functools.partial(
-                lax.ppermute, axis_name="seq", perm=[(i, i + shift) for i in range(seq - shift)]
-            )
-            prior_decay = gram_prior[:, half + 1 : half + 2, :]
-            gram_in = hop(jnp.where(body, gram_sum, 0.0) + own_decay * gram_prior)
-            memory_in = hop(memory_sum + own_decay * memory_prior)
-            gram_prior = jnp.where(body, gram_prior, 0.0) + prior_decay * gram_in
+            pairs = [(i, i + shift) for i in range(seq - shift)]
+            if covered == 0:
+                gram_prior, memory_prior = hop(gram_sum, pairs), hop(memory_sum, pairs)
+            else:
+                prior_decay = gram_prior[:, half + 1 : half + 2, :]
+                gram_in = hop(jnp.where(body, gram_sum, 0.0) + own_decay * gram_prior, pairs)
+                memory_in = hop(memory_sum + own_decay * memory_prior, pairs)
+                gram_prior = jnp.where(body, gram_prior, 0.0) + prior_decay * gram_in
+                memory_prior = memory_prior + prior_decay * memory_in
             covered = covered + shift
-            if covered < seq - 1:
-                memory_prior = memory_prior + prior_decay * memory_in
+
+        def memory_at(*ready):
+            return after(memory_prior, *ready)
 
     def swap(x):
         return lax.ppermute(x, "sub", [(i, (i + 1) % cores) for i in range(cores)])
@@ -421,35 +530,12 @@
     steps = heads // step
     solved = []
     for turn in range(cores):
-
-        def group_index(i, where_ref, turn=turn):
-            return lax.rem(where_ref[1] + turn, cores) * steps + i
-
-        def block(*shape):
-            return pl.BlockSpec(
-                (step, *shape), lambda i, where_ref: (group_index(i, where_ref),) + (0,) * len(shape)
-            )
-
-        def local_block(*shape):
-            return pl.BlockSpec((step, *shape), lambda i, where_ref: (i,) + (0,) * len(shape))
-
         solved.append(
             call(
                 functools.partial(solve_kernel, cores=cores, turn=turn, width=width),
                 steps,
-                [
-                    smem,
-                    pl.BlockSpec((shard, step * width), lambda i, where_ref: (0, group_index(i, where_ref))),
-                    block(rows, rows),
-                    block(width, rows),
-                    block(width, rows),
-                    block(width, rows),
-                    block(width, rows),
-                    block(half + PAD, width),
-                    full(head_count, rows),
-                    local_block(half + PAD, width),
-                ],
-                [local_block(rows, 2 * width), local_block(rows, width)],
+                [smem] + [vmem] * 9,
+                [vmem] * 2,
                 [
                     jax.ShapeDtypeStruct((heads, rows, 2 * width), bf16),
                     jax.ShapeDtypeStruct((heads, rows, width), f32),
@@ -463,28 +549,10 @@
             )
         )
 
-    if covered > 1:
-        solved, memory_in = lax.optimization_barrier((solved, memory_in))
-        memory_prior = memory_prior + prior_decay * memory_in
+    memory_prior = memory_at(*solved)
     output = None
     for turn in range(cores):
-
-        def group_all(*shape, turn=turn):
-            return pl.BlockSpec(
-                (heads, *shape),
-                lambda i, where_ref: (lax.rem(where_ref[1] + turn, cores),) + (0,) * len(shape),
-            )
-
-        in_specs = [
-            full(heads, rows, 2 * width),
-            full(heads, rows, width),
-            pl.BlockSpec(
-                (heads, PAD, width),
-                lambda i, where_ref, turn=turn: (lax.rem(where_ref[1] + turn, cores), half // PAD, 0),
-            ),
-            group_all(width, width),
-            full(heads, width, width),
-        ]
+        in_specs = [vmem] * 5
         operands = [where, *solved[turn], mid_gram, mid_memory, memory_prior if turn == 0 else swap(memory_prior)]
         aliases = {}
         if output is not None:
@@ -492,7 +560,7 @@
             in_specs.append(any_space)
             operands.append(output)
         output = call(
-            functools.partial(read_kernel, width=width),
+            functools.partial(read_kernel, cores=cores, turn=turn, width=width),
             1,
             in_specs,
             pl.BlockSpec(

time: 45.7 us -> 45 us (0.985)
  the two profiles are of different devices: /device:TPU:31 before, /device:TPU:0 now
where the time goes in v2:
time: 45 us; the launch traced here: 44.6 us
  Pallas kernels  22.1 us (49%)
  starting transfers between devices  22.1 us (49%)
    ppermute x8, starting transfers between devices, hop(): return lax.ppermute(x, 'seq', pairs)  21.8 us
    pallas_call x2, Pallas kernels, per_device(): call(functools.partial(solve_kernel, cores=cores, turn=turn, width=width)...  8.21 us
    pallas_call x1, Pallas kernels, per_device(): call(functools.partial(sums_kernel, total=total, heads=heads, width=width...  4.26 us
    pallas_call x1, Pallas kernels, per_device(): call(functools.partial(prepare_kernel, total=total, width=width), head_co...  4.15 us
    pallas_call x2, Pallas kernels, per_device(): call(functools.partial(read_kernel, cores=cores, turn=turn, width=width),...  3.13 us
    pallas_call x2, Pallas kernels, between(): call(functools.partial(between_kernel, half=half), 1, [vmem] * 7, [vmem]...  1.16 us
    pallas_call x2, Pallas kernels, gathered(): call(functools.partial(gather_kernel, half=half), 1, [vmem] * 5, vmem, ja...  1.14 us
  transfers between devices with their start and end apart: 10, of which 0 were waited for; matrix products, arithmetic and copies ran while one was open for 0% of the time, Pallas kernels for 34%

profile of v2, /device:TPU:0, one launch (start us, length us, event | category | flops | bytes accessed | tf_op | source)
XLA Modules:
  0.0 44.6 jit_solution(11868821354206576146)
XLA Ops:
  0.0 0.1 pad_add_fusion.where_ref
  0.1 0.0 copy-start.4
  0.1 0.0 copy-start.5
  0.1 4.3 %shard_sums.1 = (f32[2,72,128]{2,1,0:T(8,128)S(1)}, f32[2,128,128]{2,1,0:T(8,128)S(1)}, f32[2,72,128]{2,1,0:T(8,128)S(1)}, f32[2,128,128]{2,1,0:T(8,128)S(1)}, f...) custom-call(s32[2]{0:T(128)S(1)} %pad_add_fusion.where_ref, s32[3]{0:T(128)} %doc_ref.3, f32[8]{0:T(128)} %rate_ref.3, ...), custom_call_target="tpu_custom_call" | custom-call | flops 1073741824 | bytes 4194304 | tf_op jit(solution)/shard_map/shard_sums/pallas_call | solution.py:397
  4.4 5.0 %collective-permute-start = (f32[2,72,128]{2,1,0:T(8,128)S(1)}, f32[2,72,128]{2,1,0:T(8,128)S(1)}, u32[]{:S(2)}, u32[]{:S(2)}) collective-permute-start(f32[2,72,128]{2,1,0:T(8,128)S(1)} %get-tuple-element.40), channel_id=1, source_target_pairs={{0,4},{4,8},{8,12},{1,5},{5,9},{9,13},{2,6},{6,10},{10,14},{3,7},{... | collective-permute-start | bytes 221192 | tf_op jit(solution)/shard_map/ppermute | solution.py:459
  9.3 4.5 %collective-permute-start.1 = (f32[2,72,128]{2,1,0:T(8,128)S(1)}, f32[2,72,128]{2,1,0:T(8,128)S(1)}, u32[]{:S(2)}, u32[]{:S(2)}) collective-permute-start(f32[2,72,128]{2,1,0:T(8,128)S(1)} %get-tuple-element.42.second_ref.gram_second), channel_id=1, source_target_pairs={{0,8},{1,9},{2,10},{3,11},{16,24},{17,25},{18,26},{19,27}} | collective-permute-start | bytes 221192 | tf_op jit(solution)/shard_map/ppermute | solution.py:459
  13.9 1.3 %collective-permute-start.5 = (f32[2,128,128]{2,1,0:T(8,128)S(1)}, f32[2,128,128]{2,1,0:T(8,128)S(1)}, u32[]{:S(2)}, u32[]{:S(2)}) collective-permute-start(f32[2,128,128]{2,1,0:T(8,128)S(1)} %get-tuple-element.49), channel_id=1, source_target_pairs={{0,4},{4,8},{8,12},{1,5},{5,9},{9,13},{2,6},{6,10},{10,14},{3,7},{... | collective-permute-start | bytes 393224 | tf_op jit(solution)/shard_map/ppermute | solution.py:459
  15.2 1.9 %collective-permute-start.6 = (f32[2,128,128]{2,1,0:T(8,128)S(1)}, f32[2,128,128]{2,1,0:T(8,128)S(1)}, u32[]{:S(2)}, u32[]{:S(2)}) collective-permute-start(f32[2,128,128]{2,1,0:T(8,128)S(1)} %get-tuple-element.51.second_ref), channel_id=1, source_target_pairs={{0,8},{1,9},{2,10},{3,11},{16,24},{17,25},{18,26},{19,27}} | collective-permute-start | bytes 393224 | tf_op jit(solution)/shard_map/ppermute | solution.py:459
  17.1 0.0 collective-permute-done.near_ref.gram_near
  17.1 0.0 collective-permute-done.1.far_ref
  17.1 0.6 %between.2 = (f32[2,72,128]{2,1,0:T(8,128)S(1)}, f32[2,72,128]{2,1,0:T(8,128)S(1)}, f32[2,72,128]{2,1,0:T(8,128)S(1)}) custom-call(s32[2]{0:T(128)S(1)} %pad_add_fusion.where_ref, f32[2,72,128]{2,1,0:T(8,128)S(1)} %get-tuple-element.41.first_ref.gram_first, f32[2,72,128]{2,1,0:T(8,128)S(1)} %get-tuple-element.42.second_ref.gram_second, ...), custom_call_target="tpu_custom_call" | custom-call | flops 1048576 | bytes 4194304 | tf_op jit(solution)/shard_map/between/pallas_call | solution.py:469
  17.7 1.3 %collective-permute-start.2 = (f32[2,72,128]{2,1,0:T(8,128)S(1)}, f32[2,72,128]{2,1,0:T(8,128)S(1)}, u32[]{:S(2)}, u32[]{:S(2)}) collective-permute-start(f32[2,72,128]{2,1,0:T(8,128)S(1)} %get-tuple-element.44), channel_id=1, source_target_pairs={{0,4},{4,8},{8,12},{1,5},{5,9},{9,13},{2,6},{6,10},{10,14},{3,7},{... | collective-permute-start | bytes 221192 | tf_op jit(solution)/shard_map/ppermute | solution.py:459
  19.0 0.0 copy-start.6
  19.0 0.7 %collective-permute-start.3 = (f32[2,72,128]{2,1,0:T(8,128)S(1)}, f32[2,72,128]{2,1,0:T(8,128)S(1)}, u32[]{:S(2)}, u32[]{:S(2)}) collective-permute-start(f32[2,72,128]{2,1,0:T(8,128)S(1)} %get-tuple-element.45), channel_id=1, source_target_pairs={{4,12},{5,13},{6,14},{7,15},{20,28},{21,29},{22,30},{23,31}} | collective-permute-start | bytes 221192 | tf_op jit(solution)/shard_map/ppermute | solution.py:459
  19.7 4.1 %prepare.1 = (f32[8,256,256]{2,1,0:T(8,128)S(1)}, bf16[8,128,256]{2,1,0:T(8,128)(2,1)S(1)}, bf16[8,128,256]{2,1,0:T(8,128)(2,1)S(1)}, bf16[8,128,256]{2,1,0:T(8,...) custom-call(s32[2]{0:T(128)S(1)} %pad_add_fusion.where_ref, ...), custom_call_target="tpu_custom_call" | custom-call | flops 4294967296 | bytes 4194304 | tf_op jit(solution)/shard_map/prepare/pallas_call | solution.py:424
  23.9 0.0 collective-permute-done.5.near_ref
  23.9 0.0 collective-permute-done.6.far_ref
  23.9 0.6 %between.3 = (f32[2,128,128]{2,1,0:T(8,128)S(1)}, f32[2,128,128]{2,1,0:T(8,128)S(1)}, f32[2,128,128]{2,1,0:T(8,128)S(1)}) custom-call(s32[2]{0:T(128)S(1)} %pad_add_fusion.where_ref, f32[2,128,128]{2,1,0:T(8,128)S(1)} %get-tuple-element.50.first_ref, f32[2,128,128]{2,1,0:T(8,128)S(1)} %get-tuple-element.51.second_ref, ...), custom_call_target="tpu_custom_call" | custom-call | flops 1048576 | bytes 4194304 | tf_op jit(solution)/shard_map/between/pallas_call | solution.py:469
  24.5 0.0 collective-permute-done.3.farther_ref
  24.5 0.6 %gather.2.gram_ref = f32[4,72,128]{2,1,0:T(8,128)S(1)} custom-call(s32[2]{0:T(128)S(1)} %pad_add_fusion.where_ref, f32[2,72,128]{2,1,0:T(8,128)S(1)} %collective-permute-done.near_ref.gram_near, f32[2,72,128]{2,1,0:T(8,128)S(1)} %get-tuple-element.43.joined_ref, f32[2,72,128]{2,1,0:T(8,128)S(1)} %collective-permute-done.2.nearer_ref, ...), custom_call_target="tpu_custom_call" | custom-call | flops 1048576 | bytes 4194304 | tf_op jit(solution)/shard_map/gather/pallas_call | solution.py:481
  25.1 0.1 collective-permute-start.4
  25.2 6.5 %collective-permute-start.7 = (f32[2,128,128]{2,1,0:T(8,128)S(1)}, f32[2,128,128]{2,1,0:T(8,128)S(1)}, u32[]{:S(2)}, u32[]{:S(2)}) collective-permute-start(f32[2,128,128]{2,1,0:T(8,128)S(1)} %get-tuple-element.55), channel_id=1, source_target_pairs={{0,4},{4,8},{8,12},{1,5},{5,9},{9,13},{2,6},{6,10},{10,14},{3,7},{... | collective-permute-start | bytes 393224 | tf_op jit(solution)/shard_map/ppermute | solution.py:459
  31.7 0.7 %collective-permute-start.8 = (f32[2,128,128]{2,1,0:T(8,128)S(1)}, f32[2,128,128]{2,1,0:T(8,128)S(1)}, u32[]{:S(2)}, u32[]{:S(2)}) collective-permute-start(f32[2,128,128]{2,1,0:T(8,128)S(1)} %get-tuple-element.56), channel_id=1, source_target_pairs={{4,12},{5,13},{6,14},{7,15},{20,28},{21,29},{22,30},{23,31}} | collective-permute-start | bytes 393224 | tf_op jit(solution)/shard_map/ppermute | solution.py:459
  32.3 4.1 %solve_0.1 = (bf16[4,256,256]{2,1,0:T(8,128)(2,1)S(1)}, f32[4,256,128]{2,1,0:T(8,128)S(1)}) custom-call(s32[2]{0:T(128)S(1)} %pad_add_fusion.where_ref, f32[8]{0:T(128)S(1)} %copy-done.6, bf16[512,1024]{1,0:T(8,128)(2,1)S(1)} %copy-done.1, f32[8,256,256]{2,1,0:T(8,128)S(1)} %get-tuple-element.33.gate_ref, ...), custom_call_target="tpu_custom_call" | custom-call | flops 2147483648 | bytes 4194304 | tf_op jit(solution)/shard_map/solve_0/pallas_call | solution.py:534
  36.5 0.0 collective-permute-done.4.gram_ref
  36.5 4.1 %solve_1.1 = (bf16[4,256,256]{2,1,0:T(8,128)(2,1)S(1)}, f32[4,256,128]{2,1,0:T(8,128)S(1)}) custom-call(s32[2]{0:T(128)S(1)} %pad_add_fusion.where_ref, f32[8]{0:T(128)S(1)} %copy-done.6, bf16[512,1024]{1,0:T(8,128)(2,1)S(1)} %copy-done.1, f32[8,256,256]{2,1,0:T(8,128)S(1)} %get-tuple-element.33.gate_ref, ...), custom_call_target="tpu_custom_call" | custom-call | flops 2147483648 | bytes 4194304 | tf_op jit(solution)/shard_map/solve_1/pallas_call | solution.py:534
  40.6 0.0 collective-permute-done.7.nearer_ref
  40.6 0.0 collective-permute-done.8.farther_ref
  40.6 0.6 %gather.3.memory_ref = f32[4,128,128]{2,1,0:T(8,128)S(1)} custom-call(s32[2]{0:T(128)S(1)} %pad_add_fusion.where_ref, f32[2,128,128]{2,1,0:T(8,128)S(1)} %collective-permute-done.5.near_ref, f32[2,128,128]{2,1,0:T(8,128)S(1)} %get-tuple-element.52.joined_ref, f32[2,128,128]{2,1,0:T(8,128)S(1)} %collective-permute-done.7.nearer_ref, ...), custom_call_target="tpu_custom_call" | custom-call | flops 1048576 | bytes 4194304 | tf_op jit(solution)/shard_map/gather/pallas_call | solution.py:481
  41.2 0.3 collective-permute-start.9
  41.5 1.6 %read_0.1.rest_0_ = bf16[256,1024]{1,0:T(8,128)(2,1)} custom-call(s32[2]{0:T(128)S(1)} %pad_add_fusion.where_ref, bf16[4,256,256]{2,1,0:T(8,128)(2,1)S(1)} %get-tuple-element.57.solution_ref, f32[4,256,128]{2,1,0:T(8,128)S(1)} %get-tuple-element.58.chunk_ref, f32[8,72,128]{2,1,0:T(8,128)S(1)} %get-tuple-element.38.mid_ref, ...), custom_call_target="tpu_custom_call" | custom-call | flops 268435456 | bytes 4194304 | tf_op jit(solution)/shard_map/read_0/pallas_call | solution.py:562
  43.0 1.6 %read_1.1 = bf16[256,1024]{1,0:T(8,128)(2,1)} custom-call(s32[2]{0:T(128)S(1)} %pad_add_fusion.where_ref, bf16[4,256,256]{2,1,0:T(8,128)(2,1)S(1)} %get-tuple-element.46.solution_ref, f32[4,256,128]{2,1,0:T(8,128)S(1)} %get-tuple-element.47.chunk_ref, f32[8,72,128]{2,1,0:T(8,128)S(1)} %get-tuple-element.38.mid_ref, ...), custom_call_target="tpu_custom_call", output_to_operand_aliasing={{}: (6, {})} | custom-call | flops 268435456 | bytes 4194304 | tf_op jit(solution)/shard_map/read_1/pallas_call | solution.py:562
  (13 shorter events, 0.0 us)
Async XLA Ops:
  0.1 19.6 %copy-start = (bf16[512,1024]{1,0:T(8,128)(2,1)S(1)}, bf16[512,1024]{1,0:T(8,128)(2,1)}, u32[]{:S(2)}) copy-start(bf16[512,1024]{1,0:T(8,128)(2,1)} %value_hbm.1) | copy-start | bytes 3145732
  0.1 19.6 %copy-start.1 = (bf16[512,1024]{1,0:T(8,128)(2,1)S(1)}, bf16[512,1024]{1,0:T(8,128)(2,1)}, u32[]{:S(2)}) copy-start(bf16[512,1024]{1,0:T(8,128)(2,1)} %key_ref.5) | copy-start | bytes 3145732
  0.1 19.6 %copy-start.2 = (bf16[256,1024]{1,0:T(8,128)(2,1)S(1)}, bf16[256,1024]{1,0:T(8,128)(2,1)}, u32[]{:S(2)}) copy-start(bf16[256,1024]{1,0:T(8,128)(2,1)} %query_ref.1) | copy-start | bytes 1572868
  0.1 19.6 %copy-start.3 = (s32[512,8]{0,1:T(8,128)S(1)}, s32[512,8]{0,1:T(8,128)}, u32[]{:S(2)}) copy-start(s32[512,8]{0,1:T(8,128)} %param.10) | copy-start | bytes 49156
  0.1 19.6 %copy-start.4 = (s32[3]{0:T(128)S(1)}, s32[3]{0:T(128)}, u32[]{:S(2)}) copy-start(s32[3]{0:T(128)} %doc_ref.3) | copy-start | bytes 40
  0.1 19.6 %copy-start.5 = (f32[8]{0:T(128)S(1)}, f32[8]{0:T(128)}, u32[]{:S(2)}) copy-start(f32[8]{0:T(128)} %rate_ref.3) | copy-start | bytes 100
  4.4 12.7 %collective-permute-start = (f32[2,72,128]{2,1,0:T(8,128)S(1)}, f32[2,72,128]{2,1,0:T(8,128)S(1)}, u32[]{:S(2)}, u32[]{:S(2)}) collective-permute-start(f32[2,72,128]{2,1,0:T(8,128)S(1)} %get-tuple-element.40), channel_id=1, source_target_pairs={{0,4},{4,8},{8,12},{1,5},{5,9},{9,13},{2,6},{6,10},{10,14},{3,7},{... | collective-permute-start | bytes 221192 | tf_op jit(solution)/shard_map/ppermute | solution.py:459
  9.3 7.8 %collective-permute-start.1 = (f32[2,72,128]{2,1,0:T(8,128)S(1)}, f32[2,72,128]{2,1,0:T(8,128)S(1)}, u32[]{:S(2)}, u32[]{:S(2)}) collective-permute-start(f32[2,72,128]{2,1,0:T(8,128)S(1)} %get-tuple-element.42.second_ref.gram_second), channel_id=1, source_target_pairs={{0,8},{1,9},{2,10},{3,11},{16,24},{17,25},{18,26},{19,27}} | collective-permute-start | bytes 221192 | tf_op jit(solution)/shard_map/ppermute | solution.py:459
  13.9 10.0 %collective-permute-start.5 = (f32[2,128,128]{2,1,0:T(8,128)S(1)}, f32[2,128,128]{2,1,0:T(8,128)S(1)}, u32[]{:S(2)}, u32[]{:S(2)}) collective-permute-start(f32[2,128,128]{2,1,0:T(8,128)S(1)} %get-tuple-element.49), channel_id=1, source_target_pairs={{0,4},{4,8},{8,12},{1,5},{5,9},{9,13},{2,6},{6,10},{10,14},{3,7},{... | collective-permute-start | bytes 393224 | tf_op jit(solution)/shard_map/ppermute | solution.py:459
  15.2 8.7 %collective-permute-start.6 = (f32[2,128,128]{2,1,0:T(8,128)S(1)}, f32[2,128,128]{2,1,0:T(8,128)S(1)}, u32[]{:S(2)}, u32[]{:S(2)}) collective-permute-start(f32[2,128,128]{2,1,0:T(8,128)S(1)} %get-tuple-element.51.second_ref), channel_id=1, source_target_pairs={{0,8},{1,9},{2,10},{3,11},{16,24},{17,25},{18,26},{19,27}} | collective-permute-start | bytes 393224 | tf_op jit(solution)/shard_map/ppermute | solution.py:459
  17.7 6.8 %collective-permute-start.2 = (f32[2,72,128]{2,1,0:T(8,128)S(1)}, f32[2,72,128]{2,1,0:T(8,128)S(1)}, u32[]{:S(2)}, u32[]{:S(2)}) collective-permute-start(f32[2,72,128]{2,1,0:T(8,128)S(1)} %get-tuple-element.44), channel_id=1, source_target_pairs={{0,4},{4,8},{8,12},{1,5},{5,9},{9,13},{2,6},{6,10},{10,14},{3,7},{... | collective-permute-start | bytes 221192 | tf_op jit(solution)/shard_map/ppermute | solution.py:459
  19.0 13.3 %copy-start.6 = (f32[8]{0:T(128)S(1)}, f32[8]{0:T(128)}, u32[]{:S(2)}) copy-start(f32[8]{0:T(128)} %ridge_ref.3) | copy-start | bytes 100
  19.0 5.5 %collective-permute-start.3 = (f32[2,72,128]{2,1,0:T(8,128)S(1)}, f32[2,72,128]{2,1,0:T(8,128)S(1)}, u32[]{:S(2)}, u32[]{:S(2)}) collective-permute-start(f32[2,72,128]{2,1,0:T(8,128)S(1)} %get-tuple-element.45), channel_id=1, source_target_pairs={{4,12},{5,13},{6,14},{7,15},{20,28},{21,29},{22,30},{23,31}} | collective-permute-start | bytes 221192 | tf_op jit(solution)/shard_map/ppermute | solution.py:459
  25.1 11.4 %collective-permute-start.4 = (f32[4,72,128]{2,1,0:T(8,128)S(1)}, f32[4,72,128]{2,1,0:T(8,128)S(1)}, u32[]{:S(2)}, u32[]{:S(2)}) collective-permute-start(f32[4,72,128]{2,1,0:T(8,128)S(1)} %gather.2.gram_ref), channel_id=1, source_target_pairs={{0,1},{1,0},{2,3},{3,2},{4,5},{5,4},{6,7},{7,6},{8,9},{9,8},{10,11... | collective-permute-start | bytes 442376 | tf_op jit(solution)/shard_map/ppermute | solution.py:528
  25.2 15.4 %collective-permute-start.7 = (f32[2,128,128]{2,1,0:T(8,128)S(1)}, f32[2,128,128]{2,1,0:T(8,128)S(1)}, u32[]{:S(2)}, u32[]{:S(2)}) collective-permute-start(f32[2,128,128]{2,1,0:T(8,128)S(1)} %get-tuple-element.55), channel_id=1, source_target_pairs={{0,4},{4,8},{8,12},{1,5},{5,9},{9,13},{2,6},{6,10},{10,14},{3,7},{... | collective-permute-start | bytes 393224 | tf_op jit(solution)/shard_map/ppermute | solution.py:459
  31.7 8.9 %collective-permute-start.8 = (f32[2,128,128]{2,1,0:T(8,128)S(1)}, f32[2,128,128]{2,1,0:T(8,128)S(1)}, u32[]{:S(2)}, u32[]{:S(2)}) collective-permute-start(f32[2,128,128]{2,1,0:T(8,128)S(1)} %get-tuple-element.56), channel_id=1, source_target_pairs={{4,12},{5,13},{6,14},{7,15},{20,28},{21,29},{22,30},{23,31}} | collective-permute-start | bytes 393224 | tf_op jit(solution)/shard_map/ppermute | solution.py:459
  41.2 1.9 %collective-permute-start.9 = (f32[4,128,128]{2,1,0:T(8,128)S(1)}, f32[4,128,128]{2,1,0:T(8,128)S(1)}, u32[]{:S(2)}, u32[]{:S(2)}) collective-permute-start(f32[4,128,128]{2,1,0:T(8,128)S(1)} %gather.3.memory_ref), channel_id=1, source_target_pairs={{0,1},{1,0},{2,3},{3,2},{4,5},{5,4},{6,7},{7,6},{8,9},{9,8},{10,11... | collective-permute-start | bytes 786440 | tf_op jit(solution)/shard_map/ppermute | solution.py:528

commit v3 on v2

--- a/solution.py
+++ b/solution.py
@@ -102,10 +102,9 @@
 
 
 def sums_kernel(
-    where_ref, doc_ref, rate_ref, key_hbm, value_hbm, bins_ref, gram_ref, memory_ref, *rest,
-    total, heads, width, cut,
+    where_ref, doc_ref, rate_ref, key_hbm, value_hbm, bins_ref, gram_ref, memory_ref,
+    weight_ref, decay_ref, both_ref, sems, *, total, heads, width,
 ):
-    weight_ref, decay_ref, both_ref, sems = rest[-4:]
     shard = key_hbm.shape[0]
     first = where_ref[0] * shard
     core = where_ref[1]
@@ -134,47 +133,41 @@
         both = jnp.concatenate([key, both_ref[1, i]], 1)
         sums = weighted_sums(key.T, weight_ref[pl.ds(head, 1), :], both)
         state = jnp.concatenate(pack_gram(sums[:, :width], decay_ref[pl.ds(head, 1), :]), 0)
-        if cut == 0:
-            gram_ref[i] = state
-            memory_ref[i] = sums[:, width:]
-        else:
-            gram_second, memory_second, gram_sent, memory_sent = rest[:4]
-            at = i % cut
-            (gram_ref if i < cut else gram_second)[at] = state
-            (memory_ref if i < cut else memory_second)[at] = sums[:, width:]
-
-            @pl.when((where_ref[0] == 1) == (i >= cut))
-            def _(at=at, state=state, sums=sums):
-                gram_sent[at] = state
-                memory_sent[at] = sums[:, width:]
-
-
-def between_kernel(
-    where_ref, first_ref, second_ref, near_ref, far_ref, gram_first, gram_second, gram_near,
-    ahead_ref, sent_ref, joined_ref, *, half,
-):
-    place = where_ref[0]
-    line = slice(half + 1, half + 2)
-    for i in range(first_ref.shape[0]):
-        near = near_ref[i]
-        ahead = first_ref[i] + gram_first[i, line, :] * near
-        joined = near + gram_near[i, line, :] * far_ref[i]
-        second = second_ref[i]
-        behind = second + gram_second[i, line, :] * joined
-        ahead_ref[i] = ahead
-        joined_ref[i] = joined
-        sent_ref[i] = jnp.where(place == 1, ahead, jnp.where(place == 2, behind, second))
-
-
-def gather_kernel(where_ref, near_ref, joined_ref, nearer_ref, farther_ref, gram_near, prior_ref, *, half):
-    place = where_ref[0]
-    cut = near_ref.shape[0]
-    line = slice(half + 1, half + 2)
-    for i in range(cut):
-        nearer = nearer_ref[i]
-        own = near_ref[i] + gram_near[i, line, :] * farther_ref[i]
-        prior_ref[i] = jnp.where(place == 2, nearer, own)
-        prior_ref[cut + i] = jnp.where(place == 2, joined_ref[i], nearer)
+        gram_ref[i] = state
+        memory_ref[i] = sums[:, width:]
+
+
+def decay_line(gram_ref, i, half):
+    return gram_ref[i, half + 1 : half + 2, :]
+
+
+def include_kernel(where_ref, own_ref, before_ref, own_gram, before_gram, out_ref, *, half, fresh):
+    received = (where_ref[0] & 1) == 1
+    for i in range(own_ref.shape[0]):
+        decay = decay_line(own_gram, i, half)
+        state = own_ref[i] + decay * before_ref[i]
+        if own_ref.shape[1] != own_ref.shape[2]:
+            over = decay_line(before_gram, i, half)
+            over = jnp.where(received, over, 1.0) if fresh else over
+            state = jnp.where(iota(state.shape, 0) > half, decay * over, state)
+        out_ref[i] = state
+
+
+def extend_kernel(where_ref, before_ref, before_gram, *rest, half, bit, fresh):
+    out_ref = rest[-1]
+    first_received = (where_ref[0] & 1) == 1
+    received = ((where_ref[0] >> bit) & 1) == 1
+    for i in range(before_ref.shape[0]):
+        arrived = rest[0][i]
+        for other in rest[1:-1]:
+            arrived = arrived + other[i]
+        over = decay_line(before_gram, i, half)
+        over = jnp.where(first_received, over, 1.0) if fresh else over
+        state = before_ref[i] + over * arrived
+        if before_ref.shape[1] != before_ref.shape[2]:
+            passed = jnp.where(received, over * arrived[half + 1 : half + 2], over)
+            state = jnp.where(iota(state.shape, 0) > half, passed, state)
+        out_ref[i] = state
 
 
 def prepare_kernel(
@@ -390,16 +383,15 @@
             **options,
         )
 
-    cut = heads // 2 if seq == 4 and heads % 2 == 0 else 0
-    part = cut or heads
-    gram_shape = jax.ShapeDtypeStruct((part, half + PAD, width), f32)
-    memory_shape = jax.ShapeDtypeStruct((part, width, width), f32)
-    sums = call(
-        functools.partial(sums_kernel, total=total, heads=heads, width=width, cut=cut),
+    gram_sum, memory_sum = call(
+        functools.partial(sums_kernel, total=total, heads=heads, width=width),
         1,
         [smem, smem, hbm, hbm, full(head_count, shard)],
-        [vmem] * (6 if cut else 2),
-        [gram_shape, memory_shape] * (3 if cut else 1),
+        [vmem] * 2,
+        [
+            jax.ShapeDtypeStruct((heads, half + PAD, width), f32),
+            jax.ShapeDtypeStruct((heads, width, width), f32),
+        ],
         [
             pltpu.VMEM((head_count, shard), f32),
             pltpu.VMEM((head_count, width), f32),
@@ -455,74 +447,59 @@
         4 << 30,
     )(where, doc_lengths, decay_rates, queries, key_vectors, value_vectors, bins)
 
-    def hop(x, pairs):
-        return lax.ppermute(x, "seq", pairs)
-
     def after(x, *others):
         return lax.optimization_barrier((x, others))[0]
 
-    if cut:
-        gram_first, memory_first, gram_second, memory_second, gram_sent, memory_sent = sums
-        chain, jump, leap = [(0, 1), (1, 2), (2, 3)], [(0, 2)], [(1, 3)]
-
-        def between(first, second, near, far):
-            return call(
-                functools.partial(between_kernel, half=half),
-                1,
-                [vmem] * 7,
-                [vmem] * 3,
-                [jax.ShapeDtypeStruct(first.shape, f32)] * 3,
-                [],
-                "between",
-                1 << 20,
-            )(where, first, second, near, far, gram_first, gram_second, gram_near)
-
-        def gathered(near, joined, nearer, farther):
-            return call(
-                functools.partial(gather_kernel, half=half),
-                1,
-                [vmem] * 5,
-                vmem,
-                jax.ShapeDtypeStruct((heads, *near.shape[1:]), f32),
-                [],
-                "gather",
-                1 << 20,
-            )(where, near, joined, nearer, farther, gram_near)
-
-        gram_near, gram_far = hop(gram_sent, chain), hop(gram_second, jump)
-        memory_near, memory_far = hop(memory_sent, chain), hop(memory_second, jump)
-        gram_ahead, gram_sent, gram_joined = between(gram_first, gram_second, gram_near, gram_far)
-        gram_nearer, gram_farther = hop(gram_sent, chain), hop(gram_ahead, leap)
-        gram_prior = gathered(gram_near, gram_joined, gram_nearer, gram_farther)
-        memory_ahead, memory_sent, memory_joined = between(memory_first, memory_second, memory_near, memory_far)
-        memory_sent, memory_ahead = after((memory_sent, memory_ahead), gram_nearer, gram_farther)
-        memory_nearer, memory_farther = hop(memory_sent, chain), hop(memory_ahead, leap)
-
-        def memory_at(*ready):
-            nearer, farther = after((memory_nearer, memory_farther), *ready)
-            return gathered(memory_near, memory_joined, nearer, farther)
-
-    else:
-        gram_sum, memory_sum = sums
-        own_decay = gram_sum[:, half + 1 : half + 2, :]
-        body = (jnp.arange(half + PAD) < half + 1)[None, :, None]
-        gram_prior, memory_prior = jnp.zeros_like(gram_sum), jnp.zeros_like(memory_sum)
-        covered = 0
-        while covered < seq - 1:
-            shift = covered + 1
-            pairs = [(i, i + shift) for i in range(seq - shift)]
-            if covered == 0:
-                gram_prior, memory_prior = hop(gram_sum, pairs), hop(memory_sum, pairs)
-            else:
-                prior_decay = gram_prior[:, half + 1 : half + 2, :]
-                gram_in = hop(jnp.where(body, gram_sum, 0.0) + own_decay * gram_prior, pairs)
-                memory_in = hop(memory_sum + own_decay * memory_prior, pairs)
-                gram_prior = jnp.where(body, gram_prior, 0.0) + prior_decay * gram_in
-                memory_prior = memory_prior + prior_decay * memory_in
-            covered = covered + shift
-
-        def memory_at(*ready):
-            return after(memory_prior, *ready)
+    def hops(x, size):
+        got = []
+        for offset in range(size):
+            pairs = [
+                (left + size - 1, left + size + offset)
+                for left in range(0, seq, 2 * size)
+                if left + size + offset < seq
+            ]
+            if pairs:
+                got.append(lax.ppermute(x, "seq", pairs))
+        return got
+
+    def small(kernel, name, operands):
+        return call(
+            kernel,
+            1,
+            [vmem] * len(operands),
+            vmem,
+            jax.ShapeDtypeStruct(operands[0].shape, f32),
+            [],
+            name,
+            1 << 20,
+        )(where, *operands)
+
+    def include(own, before, before_gram, fresh):
+        kernel = functools.partial(include_kernel, half=half, fresh=fresh)
+        return small(kernel, "include", [own, before, gram_sum, before_gram])
+
+    def extend(before, before_gram, got, bit, fresh):
+        kernel = functools.partial(extend_kernel, half=half, bit=bit, fresh=fresh)
+        return small(kernel, "extend", [before, before_gram, *got])
+
+    (gram_prior,), (memory_prior,) = hops(gram_sum, 1), hops(memory_sum, 1)
+    size, bit = 2, 1
+    pending = None
+    while size < seq:
+        fresh = bit == 1
+        if pending is not None:
+            memory_prior = extend(*pending)
+        gram_got = hops(include(gram_sum, gram_prior, gram_prior, fresh), size)
+        memory_got = hops(include(memory_sum, memory_prior, gram_prior, fresh), size)
+        pending = (memory_prior, gram_prior, memory_got, bit, fresh)
+        gram_prior = extend(gram_prior, gram_prior, gram_got, bit, fresh)
+        size, bit = 2 * size, bit + 1
+
+    def memory_at(*ready):
+        if pending is None:
+            return memory_prior
+        before, before_gram, got, *rest = pending
+        return extend(before, before_gram, after(got, *ready), *rest)
 
     def swap(x):
         return lax.ppermute(x, "sub", [(i, (i + 1) % cores) for i in range(cores)])

time: 45 us -> 40.1 us (0.89)
  the two profiles are of different devices: /device:TPU:0 before, /device:TPU:15 now
where the time goes in v3:
time: 40.1 us; the launch traced here: 39.8 us
  Pallas kernels  22.2 us (55%)
  starting transfers between devices  13.2 us (33%)
  waiting for transfers between devices  4.05 us (10%)
    ppermute x6, starting transfers between devices, hops(): got.append(lax.ppermute(x, 'seq', pairs))  10.1 us
    pallas_call x2, Pallas kernels, per_device(): call(functools.partial(solve_kernel, cores=cores, turn=turn, width=width)...  8.42 us
    pallas_call x1, Pallas kernels, per_device(): call(functools.partial(sums_kernel, total=total, heads=heads, width=width...  4.23 us
    pallas_call x1, Pallas kernels, per_device(): call(functools.partial(prepare_kernel, total=total, width=width), head_co...  4.15 us
    ppermute x6, waiting for transfers between devices, hops(): got.append(lax.ppermute(x, 'seq', pairs))  4.04 us
    pallas_call x2, Pallas kernels, per_device(): call(functools.partial(read_kernel, cores=cores, turn=turn, width=width),...  3.13 us
    ppermute x2, starting transfers between devices, swap(): return lax.ppermute(x, 'sub', [(i, (i + 1) % cores) for i in range(cores)])  3.11 us
    pallas_call x4, Pallas kernels, small(): call(kernel, 1, [vmem] * len(operands), vmem, jax.ShapeDtypeStruct(operan...  2.28 us
  transfers between devices with their start and end apart: 8, of which 1 were waited for; matrix products, arithmetic and copies ran while one was open for 0% of the time, Pallas kernels for 40%

profile of v3, /device:TPU:15, one launch (start us, length us, event | category | flops | bytes accessed | tf_op | source)
XLA Modules:
  0.0 39.8 jit_solution(16831585913687405254)
XLA Ops:
  0.0 0.1 pad_add_fusion.where_ref
  0.1 0.0 copy-start.4
  0.1 0.0 copy-start.5
  0.1 4.2 %shard_sums.1 = (f32[4,72,128]{2,1,0:T(8,128)S(1)}, f32[4,128,128]{2,1,0:T(8,128)S(1)}) custom-call(s32[2]{0:T(128)S(1)} %pad_add_fusion.where_ref, s32[3]{0:T(128)} %doc_ref.3, f32[8]{0:T(128)} %rate_ref.3, bf16[512,1024]{1,0:T(8,128)(2,1)} %key_ref.5, bf16[512,1024]{1,0:T(8,128)(2,1)} %value_hbm.1, s32[8,512]{1,0:T(8,128)} %bitcast.3), custom_call_target="tpu_custom_call" | custom-call | flops 1073741824 | bytes 4194304 | tf_op jit(solution)/shard_map/shard_sums/pallas_call | solution.py:386
  4.3 1.3 %collective-permute-start = (f32[4,72,128]{2,1,0:T(8,128)S(1)}, f32[4,72,128]{2,1,0:T(8,128)S(1)}, u32[]{:S(2)}, u32[]{:S(2)}) collective-permute-start(f32[4,72,128]{2,1,0:T(8,128)S(1)} %get-tuple-element.28.own_ref.own_gram), channel_id=1, source_target_pairs={{0,4},{8,12},{1,5},{9,13},{2,6},{10,14},{3,7},{11,15},{16,20},{24,... | collective-permute-start | bytes 442376 | tf_op jit(solution)/shard_map/ppermute | solution.py:462
  5.6 1.3 %collective-permute-start.4 = (f32[4,128,128]{2,1,0:T(8,128)S(1)}, f32[4,128,128]{2,1,0:T(8,128)S(1)}, u32[]{:S(2)}, u32[]{:S(2)}) collective-permute-start(f32[4,128,128]{2,1,0:T(8,128)S(1)} %get-tuple-element.32.own_ref), channel_id=1, source_target_pairs={{0,4},{8,12},{1,5},{9,13},{2,6},{10,14},{3,7},{11,15},{16,20},{24,... | collective-permute-start | bytes 786440 | tf_op jit(solution)/shard_map/ppermute | solution.py:462
  6.9 4.0 %collective-permute-done.before_ref.before_gram = f32[4,72,128]{2,1,0:T(8,128)S(1)} collective-permute-done((f32[4,72,128]{2,1,0:T(8,128)S(1)}, f32[4,72,128]{2,1,0:T(8,128)S(1)}, u32[]{:S(2)}, u32[]{:S(2)}) %collective-permute-start) | collective-permute-done | bytes 147488 | tf_op jit(solution)/shard_map/ppermute | solution.py:462
  11.0 0.6 %include.2 = f32[4,72,128]{2,1,0:T(8,128)S(1)} custom-call(s32[2]{0:T(128)S(1)} %pad_add_fusion.where_ref, f32[4,72,128]{2,1,0:T(8,128)S(1)} %get-tuple-element.28.own_ref.own_gram, f32[4,72,128]{2,1,0:T(8,128)S(1)} %collective-permute-done.before_ref.before_gram, f32[4,72,128]{2,1,0:T(8,128)S(1)} %get-tuple-element.28.own_ref.own_gram, ...), custom_call_target="tpu_custom_call" | custom-call | flops 1048576 | bytes 4194304 | tf_op jit(solution)/shard_map/include/pallas_call | solution.py:466
  11.5 0.0 copy-start.6
  11.6 2.3 %collective-permute-start.1 = (f32[4,72,128]{2,1,0:T(8,128)S(1)}, f32[4,72,128]{2,1,0:T(8,128)S(1)}, u32[]{:S(2)}, u32[]{:S(2)}) collective-permute-start(f32[4,72,128]{2,1,0:T(8,128)S(1)} %include.2), channel_id=1, source_target_pairs={{4,8},{5,9},{6,10},{7,11},{20,24},{21,25},{22,26},{23,27}} | collective-permute-start | bytes 442376 | tf_op jit(solution)/shard_map/ppermute | solution.py:462
  13.9 2.6 %collective-permute-start.2 = (f32[4,72,128]{2,1,0:T(8,128)S(1)}, f32[4,72,128]{2,1,0:T(8,128)S(1)}, u32[]{:S(2)}, u32[]{:S(2)}) collective-permute-start(f32[4,72,128]{2,1,0:T(8,128)S(1)} %include.2), channel_id=1, source_target_pairs={{4,12},{5,13},{6,14},{7,15},{20,28},{21,29},{22,30},{23,31}} | collective-permute-start | bytes 442376 | tf_op jit(solution)/shard_map/ppermute | solution.py:462
  16.5 0.0 copy-done
  16.5 0.0 copy-done.1
  16.5 4.1 %prepare.1 = (f32[8,256,256]{2,1,0:T(8,128)S(1)}, bf16[8,128,256]{2,1,0:T(8,128)(2,1)S(1)}, bf16[8,128,256]{2,1,0:T(8,128)(2,1)S(1)}, bf16[8,128,256]{2,1,0:T(8,...) custom-call(s32[2]{0:T(128)S(1)} %pad_add_fusion.where_ref, ...), custom_call_target="tpu_custom_call" | custom-call | flops 4294967296 | bytes 4194304 | tf_op jit(solution)/shard_map/prepare/pallas_call | solution.py:416
  20.7 0.0 collective-permute-done.4.before_ref
  20.7 0.6 %include.3 = f32[4,128,128]{2,1,0:T(8,128)S(1)} custom-call(s32[2]{0:T(128)S(1)} %pad_add_fusion.where_ref, f32[4,128,128]{2,1,0:T(8,128)S(1)} %get-tuple-element.32.own_ref, f32[4,128,128]{2,1,0:T(8,128)S(1)} %collective-permute-done.4.before_ref, f32[4,72,128]{2,1,0:T(8,128)S(1)} %get-tuple-element.28.own_ref.own_gram, ...), custom_call_target="tpu_custom_call" | custom-call | flops 1048576 | bytes 4194304 | tf_op jit(solution)/shard_map/include/pallas_call | solution.py:466
  21.3 1.3 %collective-permute-start.5 = (f32[4,128,128]{2,1,0:T(8,128)S(1)}, f32[4,128,128]{2,1,0:T(8,128)S(1)}, u32[]{:S(2)}, u32[]{:S(2)}) collective-permute-start(f32[4,128,128]{2,1,0:T(8,128)S(1)} %include.3), channel_id=1, source_target_pairs={{4,8},{5,9},{6,10},{7,11},{20,24},{21,25},{22,26},{23,27}} | collective-permute-start | bytes 786440 | tf_op jit(solution)/shard_map/ppermute | solution.py:462
  22.6 1.3 %collective-permute-start.6 = (f32[4,128,128]{2,1,0:T(8,128)S(1)}, f32[4,128,128]{2,1,0:T(8,128)S(1)}, u32[]{:S(2)}, u32[]{:S(2)}) collective-permute-start(f32[4,128,128]{2,1,0:T(8,128)S(1)} %include.3), channel_id=1, source_target_pairs={{4,12},{5,13},{6,14},{7,15},{20,28},{21,29},{22,30},{23,31}} | collective-permute-start | bytes 786440 | tf_op jit(solution)/shard_map/ppermute | solution.py:462
  23.9 0.0 collective-permute-done.1.rest_0_
  23.9 0.0 collective-permute-done.2.rest_1_
  23.9 0.6 %extend.2.gram_ref = f32[4,72,128]{2,1,0:T(8,128)S(1)} custom-call(s32[2]{0:T(128)S(1)} %pad_add_fusion.where_ref, f32[4,72,128]{2,1,0:T(8,128)S(1)} %collective-permute-done.before_ref.before_gram, f32[4,72,128]{2,1,0:T(8,128)S(1)} %collective-permute-done.before_ref.before_gram, f32[4,72,128]{2,1,0:T(8,128)S(1)} %collective-permute-done.1.rest_0_, ...), custom_call_target="tpu_custom_call" | custom-call | flops 1048576 | bytes 4194304 | tf_op jit(solution)/shard_map/extend/pallas_call | solution.py:466
  24.5 3.0 %collective-permute-start.3 = (f32[4,72,128]{2,1,0:T(8,128)S(1)}, f32[4,72,128]{2,1,0:T(8,128)S(1)}, u32[]{:S(2)}, u32[]{:S(2)}) collective-permute-start(f32[4,72,128]{2,1,0:T(8,128)S(1)} %extend.2.gram_ref), channel_id=1, source_target_pairs={{0,1},{1,0},{2,3},{3,2},{4,5},{5,4},{6,7},{7,6},{8,9},{9,8},{10,11... | collective-permute-start | bytes 442376 | tf_op jit(solution)/shard_map/ppermute | solution.py:505
  27.5 4.2 %solve_0.1 = (bf16[4,256,256]{2,1,0:T(8,128)(2,1)S(1)}, f32[4,256,128]{2,1,0:T(8,128)S(1)}) custom-call(s32[2]{0:T(128)S(1)} %pad_add_fusion.where_ref, f32[8]{0:T(128)S(1)} %copy-done.6, bf16[512,1024]{1,0:T(8,128)(2,1)S(1)} %copy-done.1, f32[8,256,256]{2,1,0:T(8,128)S(1)} %get-tuple-element.21.gate_ref, ...), custom_call_target="tpu_custom_call" | custom-call | flops 2147483648 | bytes 4194304 | tf_op jit(solution)/shard_map/solve_0/pallas_call | solution.py:511
  31.7 0.0 collective-permute-done.3.gram_ref
  31.7 4.2 %solve_1.1 = (bf16[4,256,256]{2,1,0:T(8,128)(2,1)S(1)}, f32[4,256,128]{2,1,0:T(8,128)S(1)}) custom-call(s32[2]{0:T(128)S(1)} %pad_add_fusion.where_ref, f32[8]{0:T(128)S(1)} %copy-done.6, bf16[512,1024]{1,0:T(8,128)(2,1)S(1)} %copy-done.1, f32[8,256,256]{2,1,0:T(8,128)S(1)} %get-tuple-element.21.gate_ref, ...), custom_call_target="tpu_custom_call" | custom-call | flops 2147483648 | bytes 4194304 | tf_op jit(solution)/shard_map/solve_1/pallas_call | solution.py:511
  35.9 0.0 collective-permute-done.5.rest_0_
  36.0 0.0 collective-permute-done.6.rest_1_
  36.0 0.6 %extend.3.memory_ref = f32[4,128,128]{2,1,0:T(8,128)S(1)} custom-call(s32[2]{0:T(128)S(1)} %pad_add_fusion.where_ref, f32[4,128,128]{2,1,0:T(8,128)S(1)} %collective-permute-done.4.before_ref, f32[4,72,128]{2,1,0:T(8,128)S(1)} %collective-permute-done.before_ref.before_gram, f32[4,128,128]{2,1,0:T(8,128)S(1)} %collective-permute-done.5.rest_0_, ...), custom_call_target="tpu_custom_call" | custom-call | flops 1048576 | bytes 4194304 | tf_op jit(solution)/shard_map/extend/pallas_call | solution.py:466
  36.6 0.1 collective-permute-start.7
  36.6 1.6 %read_0.1.rest_0_ = bf16[256,1024]{1,0:T(8,128)(2,1)} custom-call(s32[2]{0:T(128)S(1)} %pad_add_fusion.where_ref, bf16[4,256,256]{2,1,0:T(8,128)(2,1)S(1)} %get-tuple-element.33.solution_ref, f32[4,256,128]{2,1,0:T(8,128)S(1)} %get-tuple-element.34.chunk_ref, f32[8,72,128]{2,1,0:T(8,128)S(1)} %get-tuple-element.26.mid_ref, ...), custom_call_target="tpu_custom_call" | custom-call | flops 268435456 | bytes 4194304 | tf_op jit(solution)/shard_map/read_0/pallas_call | solution.py:539
  38.2 0.0 collective-permute-done.7.memory_ref
  38.2 1.6 %read_1.1 = bf16[256,1024]{1,0:T(8,128)(2,1)} custom-call(s32[2]{0:T(128)S(1)} %pad_add_fusion.where_ref, bf16[4,256,256]{2,1,0:T(8,128)(2,1)S(1)} %get-tuple-element.29.solution_ref, f32[4,256,128]{2,1,0:T(8,128)S(1)} %get-tuple-element.30.chunk_ref, f32[8,72,128]{2,1,0:T(8,128)S(1)} %get-tuple-element.26.mid_ref, ...), custom_call_target="tpu_custom_call", output_to_operand_aliasing={{}: (6, {})} | custom-call | flops 268435456 | bytes 4194304 | tf_op jit(solution)/shard_map/read_1/pallas_call | solution.py:539
  (9 shorter events, 0.0 us)
Async XLA Ops:
  0.1 16.4 %copy-start = (bf16[512,1024]{1,0:T(8,128)(2,1)S(1)}, bf16[512,1024]{1,0:T(8,128)(2,1)}, u32[]{:S(2)}) copy-start(bf16[512,1024]{1,0:T(8,128)(2,1)} %value_hbm.1) | copy-start | bytes 3145732
  0.1 16.4 %copy-start.1 = (bf16[512,1024]{1,0:T(8,128)(2,1)S(1)}, bf16[512,1024]{1,0:T(8,128)(2,1)}, u32[]{:S(2)}) copy-start(bf16[512,1024]{1,0:T(8,128)(2,1)} %key_ref.5) | copy-start | bytes 3145732
  0.1 16.4 %copy-start.2 = (bf16[256,1024]{1,0:T(8,128)(2,1)S(1)}, bf16[256,1024]{1,0:T(8,128)(2,1)}, u32[]{:S(2)}) copy-start(bf16[256,1024]{1,0:T(8,128)(2,1)} %query_ref.1) | copy-start | bytes 1572868
  0.1 16.4 %copy-start.3 = (s32[512,8]{0,1:T(8,128)S(1)}, s32[512,8]{0,1:T(8,128)}, u32[]{:S(2)}) copy-start(s32[512,8]{0,1:T(8,128)} %param.10) | copy-start | bytes 49156
  0.1 16.4 %copy-start.4 = (s32[3]{0:T(128)S(1)}, s32[3]{0:T(128)}, u32[]{:S(2)}) copy-start(s32[3]{0:T(128)} %doc_ref.3) | copy-start | bytes 40
  0.1 16.4 %copy-start.5 = (f32[8]{0:T(128)S(1)}, f32[8]{0:T(128)}, u32[]{:S(2)}) copy-start(f32[8]{0:T(128)} %rate_ref.3) | copy-start | bytes 100
  4.3 6.6 %collective-permute-start = (f32[4,72,128]{2,1,0:T(8,128)S(1)}, f32[4,72,128]{2,1,0:T(8,128)S(1)}, u32[]{:S(2)}, u32[]{:S(2)}) collective-permute-start(f32[4,72,128]{2,1,0:T(8,128)S(1)} %get-tuple-element.28.own_ref.own_gram), channel_id=1, source_target_pairs={{0,4},{8,12},{1,5},{9,13},{2,6},{10,14},{3,7},{11,15},{16,20},{24,... | collective-permute-start | bytes 442376 | tf_op jit(solution)/shard_map/ppermute | solution.py:462
  5.6 15.0 %collective-permute-start.4 = (f32[4,128,128]{2,1,0:T(8,128)S(1)}, f32[4,128,128]{2,1,0:T(8,128)S(1)}, u32[]{:S(2)}, u32[]{:S(2)}) collective-permute-start(f32[4,128,128]{2,1,0:T(8,128)S(1)} %get-tuple-element.32.own_ref), channel_id=1, source_target_pairs={{0,4},{8,12},{1,5},{9,13},{2,6},{10,14},{3,7},{11,15},{16,20},{24,... | collective-permute-start | bytes 786440 | tf_op jit(solution)/shard_map/ppermute | solution.py:462
  11.5 16.0 %copy-start.6 = (f32[8]{0:T(128)S(1)}, f32[8]{0:T(128)}, u32[]{:S(2)}) copy-start(f32[8]{0:T(128)} %ridge_ref.3) | copy-start | bytes 100
  11.6 12.3 %collective-permute-start.1 = (f32[4,72,128]{2,1,0:T(8,128)S(1)}, f32[4,72,128]{2,1,0:T(8,128)S(1)}, u32[]{:S(2)}, u32[]{:S(2)}) collective-permute-start(f32[4,72,128]{2,1,0:T(8,128)S(1)} %include.2), channel_id=1, source_target_pairs={{4,8},{5,9},{6,10},{7,11},{20,24},{21,25},{22,26},{23,27}} | collective-permute-start | bytes 442376 | tf_op jit(solution)/shard_map/ppermute | solution.py:462
  13.9 10.0 %collective-permute-start.2 = (f32[4,72,128]{2,1,0:T(8,128)S(1)}, f32[4,72,128]{2,1,0:T(8,128)S(1)}, u32[]{:S(2)}, u32[]{:S(2)}) collective-permute-start(f32[4,72,128]{2,1,0:T(8,128)S(1)} %include.2), channel_id=1, source_target_pairs={{4,12},{5,13},{6,14},{7,15},{20,28},{21,29},{22,30},{23,31}} | collective-permute-start | bytes 442376 | tf_op jit(solution)/shard_map/ppermute | solution.py:462
  21.3 14.7 %collective-permute-start.5 = (f32[4,128,128]{2,1,0:T(8,128)S(1)}, f32[4,128,128]{2,1,0:T(8,128)S(1)}, u32[]{:S(2)}, u32[]{:S(2)}) collective-permute-start(f32[4,128,128]{2,1,0:T(8,128)S(1)} %include.3), channel_id=1, source_target_pairs={{4,8},{5,9},{6,10},{7,11},{20,24},{21,25},{22,26},{23,27}} | collective-permute-start | bytes 786440 | tf_op jit(solution)/shard_map/ppermute | solution.py:462
  22.6 13.4 %collective-permute-start.6 = (f32[4,128,128]{2,1,0:T(8,128)S(1)}, f32[4,128,128]{2,1,0:T(8,128)S(1)}, u32[]{:S(2)}, u32[]{:S(2)}) collective-permute-start(f32[4,128,128]{2,1,0:T(8,128)S(1)} %include.3), channel_id=1, source_target_pairs={{4,12},{5,13},{6,14},{7,15},{20,28},{21,29},{22,30},{23,31}} | collective-permute-start | bytes 786440 | tf_op jit(solution)/shard_map/ppermute | solution.py:462
  24.5 7.2 %collective-permute-start.3 = (f32[4,72,128]{2,1,0:T(8,128)S(1)}, f32[4,72,128]{2,1,0:T(8,128)S(1)}, u32[]{:S(2)}, u32[]{:S(2)}) collective-permute-start(f32[4,72,128]{2,1,0:T(8,128)S(1)} %extend.2.gram_ref), channel_id=1, source_target_pairs={{0,1},{1,0},{2,3},{3,2},{4,5},{5,4},{6,7},{7,6},{8,9},{9,8},{10,11... | collective-permute-start | bytes 442376 | tf_op jit(solution)/shard_map/ppermute | solution.py:505
  36.6 1.7 %collective-permute-start.7 = (f32[4,128,128]{2,1,0:T(8,128)S(1)}, f32[4,128,128]{2,1,0:T(8,128)S(1)}, u32[]{:S(2)}, u32[]{:S(2)}) collective-permute-start(f32[4,128,128]{2,1,0:T(8,128)S(1)} %extend.3.memory_ref), channel_id=1, source_target_pairs={{0,1},{1,0},{2,3},{3,2},{4,5},{5,4},{6,7},{7,6},{8,9},{9,8},{10,11... | collective-permute-start | bytes 786440 | tf_op jit(solution)/shard_map/ppermute | solution.py:505

commit v4 on v3

--- a/solution.py
+++ b/solution.py
@@ -13,6 +13,7 @@
 bf16 = jnp.bfloat16
 PAD = 8
 PER_STEP = 4
+BLOCK = 4
 VMEM = 24 << 20
 
 
@@ -78,15 +79,14 @@
     return product[:width] + product[width:]
 
 
-def pack_gram(gram, decay):
+def pack_gram(gram):
     width = gram.shape[0]
     half = width // 2
     turned = pltpu.roll(gram[half:], half, 1)
     row, col = iota((half, width), 0), iota((half, width), 1)
     packed = jnp.where((col < half) & (row > col), turned, gram[:half])
     diagonal = jnp.sum(jnp.where(row == col, turned, 0.0), axis=0, keepdims=True)
-    tail = jnp.where(iota((PAD, width), 0) == 0, diagonal, decay)
-    return packed, tail
+    return packed, diagonal
 
 
 def unpack_gram(packed, diagonal):
@@ -106,6 +106,7 @@
     weight_ref, decay_ref, both_ref, sems, *, total, heads, width,
 ):
     shard = key_hbm.shape[0]
+    half = width // 2
     first = where_ref[0] * shard
     core = where_ref[1]
     copies = []
@@ -132,42 +133,76 @@
         key = both_ref[0, i]
         both = jnp.concatenate([key, both_ref[1, i]], 1)
         sums = weighted_sums(key.T, weight_ref[pl.ds(head, 1), :], both)
-        state = jnp.concatenate(pack_gram(sums[:, :width], decay_ref[pl.ds(head, 1), :]), 0)
-        gram_ref[i] = state
+        packed, diagonal = pack_gram(sums[:, :width])
+        gram_ref[i * half : (i + 1) * half, :] = packed
+        gram_ref[heads * half + i : heads * half + i + 1, :] = diagonal
+        tail = heads * half + heads + i
+        gram_ref[tail : tail + 1, :] = decay_ref[pl.ds(head, 1), :]
         memory_ref[i] = sums[:, width:]
 
 
-def decay_line(gram_ref, i, half):
-    return gram_ref[i, half + 1 : half + 2, :]
-
-
-def include_kernel(where_ref, own_ref, before_ref, own_gram, before_gram, out_ref, *, half, fresh):
-    received = (where_ref[0] & 1) == 1
-    for i in range(own_ref.shape[0]):
-        decay = decay_line(own_gram, i, half)
-        state = own_ref[i] + decay * before_ref[i]
-        if own_ref.shape[1] != own_ref.shape[2]:
-            over = decay_line(before_gram, i, half)
-            over = jnp.where(received, over, 1.0) if fresh else over
-            state = jnp.where(iota(state.shape, 0) > half, decay * over, state)
-        out_ref[i] = state
-
-
-def extend_kernel(where_ref, before_ref, before_gram, *rest, half, bit, fresh):
+def decay_line(gram_ref, i, heads):
+    row = gram_ref.shape[0] - tail_rows(heads) + heads + i
+    return gram_ref[row : row + 1, :]
+
+
+def tail_rows(heads):
+    return -(-2 * heads // 8) * 8
+
+
+def gram_rows(i, heads, half):
+    return (slice(i * half, (i + 1) * half), slice(heads * half + i, heads * half + i + 1))
+
+
+def direct_kernel(where_ref, *rest, heads, half, block):
+    got, out_ref = rest[:-1], rest[-1]
+    out_ref[...] = jnp.zeros_like(out_ref)
+    arrived = lax.rem(where_ref[0], block)
+    for i in range(heads):
+        decays = [decay_line(ref, i, heads) for ref in got]
+        for rows in gram_rows(i, heads, half):
+            state = got[-1][rows, :]
+            for ref, decay in zip(got[-2::-1], decays[-2::-1]):
+                state = ref[rows, :] + decay * state
+            out_ref[rows, :] = state
+        over = jnp.ones_like(decays[0])
+        for place, decay in enumerate(decays):
+            over = jnp.where(arrived > place, over * decay, over)
+        line = heads * half + heads + i
+        out_ref[line : line + 1, :] = over
+
+
+def include_kernel(where_ref, own_ref, before_ref, own_gram, *rest, heads, half):
     out_ref = rest[-1]
-    first_received = (where_ref[0] & 1) == 1
+    memory = len(own_ref.shape) == 3
+    for i in range(heads):
+        decay = decay_line(own_gram, i, heads)
+        if memory:
+            out_ref[i] = own_ref[i] + decay * before_ref[i]
+            continue
+        for rows in gram_rows(i, heads, half):
+            out_ref[rows, :] = own_ref[rows, :] + decay * before_ref[rows, :]
+        line = heads * half + heads + i
+        out_ref[line : line + 1, :] = decay * decay_line(before_ref, i, heads)
+
+
+def extend_kernel(where_ref, before_ref, before_gram, *rest, heads, half, bit, fresh):
+    out_ref, got = rest[-1], rest[:-1]
+    memory = len(before_ref.shape) == 3
     received = ((where_ref[0] >> bit) & 1) == 1
-    for i in range(before_ref.shape[0]):
-        arrived = rest[0][i]
-        for other in rest[1:-1]:
-            arrived = arrived + other[i]
-        over = decay_line(before_gram, i, half)
-        over = jnp.where(first_received, over, 1.0) if fresh else over
-        state = before_ref[i] + over * arrived
-        if before_ref.shape[1] != before_ref.shape[2]:
-            passed = jnp.where(received, over * arrived[half + 1 : half + 2], over)
-            state = jnp.where(iota(state.shape, 0) > half, passed, state)
-        out_ref[i] = state
+    for i in range(heads):
+        over = decay_line(before_gram, i, heads)
+        if fresh:
+            over = jnp.where((where_ref[0] & 1) == 1, over, 1.0)
+        if memory:
+            out_ref[i] = before_ref[i] + over * functools.reduce(jnp.add, [ref[i] for ref in got])
+            continue
+        for rows in gram_rows(i, heads, half):
+            arrived = functools.reduce(jnp.add, [ref[rows, :] for ref in got])
+            out_ref[rows, :] = before_ref[rows, :] + over * arrived
+        passed = functools.reduce(jnp.add, [decay_line(ref, i, heads) for ref in got])
+        line = heads * half + heads + i
+        out_ref[line : line + 1, :] = jnp.where(received, over * passed, over)
 
 
 def prepare_kernel(
@@ -214,9 +249,11 @@
         key_t = key_ref[:, cols].T
         both = jnp.concatenate([key_ref[:, cols], value_ref[:, cols]], 1)
         sums = weighted_sums(key_t, mid_ref[pl.ds(head, 1), :], both)
-        packed, tail = pack_gram(sums[:, :width], decay_ref[pl.ds(head, 1), :])
+        packed, diagonal = pack_gram(sums[:, :width])
         mid_gram_ref[i, : width // 2, :] = packed
-        mid_gram_ref[i, width // 2 :, :] = tail
+        mid_gram_ref[i, width // 2 :, :] = jnp.where(
+            iota((PAD, width), 0) == 0, diagonal, decay_ref[pl.ds(head, 1), :]
+        )
         mid_memory_ref[i] = sums[:, width:]
         key_own = key_ref[own, cols]
         own_t = key_own.T
@@ -238,14 +275,11 @@
 ):
     rows = query_t_ref.shape[2]
     core = where_ref[1]
-    steps = pl.num_programs(0)
+    heads = solution_ref.shape[0]
     group = lax.rem(core + turn, cores)
     own = pl.ds(pl.multiple_of(core * rows, rows), rows)
     half = width // 2
-    step = gram_ref.shape[0] // steps
-    skip = pl.program_id(0) * step
-    per_step = range(step)
-    base = group * gram_ref.shape[0] + skip
+    base = group * heads
 
     def row_sum(x):
         return jnp.sum(x, axis=0, keepdims=True)
@@ -256,8 +290,9 @@
         ridge = ridge_ref[head]
         carried = carried_ref[pl.ds(head, 1), :]
         decay = mid_ref[head, half + 1 : half + 2, :]
-        packed = mid_ref[head, :half, :] + decay * gram_ref[skip + i, :half, :]
-        diagonal = mid_ref[head, half : half + 1, :] + decay * gram_ref[skip + i, half : half + 1, :]
+        body, line = gram_rows(i, heads, half)
+        packed = mid_ref[head, :half, :] + decay * gram_ref[body, :]
+        diagonal = mid_ref[head, half : half + 1, :] + decay * gram_ref[line, :]
         high, low = split(unpack_gram(packed, diagonal))
         system = jnp.concatenate(
             [jnp.concatenate([high, low], 0), jnp.concatenate([high, jnp.zeros_like(low)], 0)], 1
@@ -307,16 +342,16 @@
             yield
         plain = dot_nn(keys, jnp.concatenate(split(result), 0))
         high, low = split(carried * result)
-        solution_ref[skip + i] = jnp.concatenate([high.T, low.T], 1)
+        solution_ref[i] = jnp.concatenate([high.T, low.T], 1)
         yield
         weighted_pair = jnp.concatenate(split(plain * gate_ref[head]), 0)
         yield
         value_t = value_t_ref[head]
         chunk = dot_nn(jnp.concatenate([value_t, value_t], 1), weighted_pair)
         yield
-        chunk_ref[skip + i] = chunk.T
-
-    programs = [head_program(i) for i in per_step]
+        chunk_ref[i] = chunk.T
+
+    programs = [head_program(i) for i in range(heads)]
     running = []
     while programs or running:
         if programs:
@@ -389,7 +424,7 @@
         [smem, smem, hbm, hbm, full(head_count, shard)],
         [vmem] * 2,
         [
-            jax.ShapeDtypeStruct((heads, half + PAD, width), f32),
+            jax.ShapeDtypeStruct((heads * half + tail_rows(heads), width), f32),
             jax.ShapeDtypeStruct((heads, width, width), f32),
         ],
         [
@@ -462,9 +497,9 @@
                 got.append(lax.ppermute(x, "seq", pairs))
         return got
 
-    def small(kernel, name, operands):
+    def small(kernel, name, operands, **options):
         return call(
-            kernel,
+            functools.partial(kernel, heads=heads, half=half, **options),
             1,
             [vmem] * len(operands),
             vmem,
@@ -474,43 +509,52 @@
             1 << 20,
         )(where, *operands)
 
-    def include(own, before, before_gram, fresh):
-        kernel = functools.partial(include_kernel, half=half, fresh=fresh)
-        return small(kernel, "include", [own, before, gram_sum, before_gram])
-
-    def extend(before, before_gram, got, bit, fresh):
-        kernel = functools.partial(extend_kernel, half=half, bit=bit, fresh=fresh)
-        return small(kernel, "extend", [before, before_gram, *got])
-
-    (gram_prior,), (memory_prior,) = hops(gram_sum, 1), hops(memory_sum, 1)
+    block = min(BLOCK, seq)
+    gram_near = [
+        lax.ppermute(gram_sum, "seq", [(i, i + ahead) for i in range(seq - ahead) if i % block + ahead < block])
+        for ahead in range(1, block)
+    ]
+    nearest = gram_near[0]
+    (memory_prior,) = hops(memory_sum, 1)
     size, bit = 2, 1
-    pending = None
+    pending = gram_prior = None
     while size < seq:
-        fresh = bit == 1
         if pending is not None:
-            memory_prior = extend(*pending)
-        gram_got = hops(include(gram_sum, gram_prior, gram_prior, fresh), size)
-        memory_got = hops(include(memory_sum, memory_prior, gram_prior, fresh), size)
-        pending = (memory_prior, gram_prior, memory_got, bit, fresh)
-        gram_prior = extend(gram_prior, gram_prior, gram_got, bit, fresh)
+            memory_prior = small(extend_kernel, "extend", pending[0], **pending[1])
+        if size >= block:
+            if gram_prior is None:
+                gram_prior = small(direct_kernel, "direct", gram_near, block=block)
+            gram_got = hops(small(include_kernel, "include", [gram_sum, gram_prior, gram_sum]), size)
+            before_gram = gram_prior
+            gram_prior = small(
+                extend_kernel, "extend", [gram_prior, gram_prior, *gram_got], bit=bit, fresh=False
+            )
+        else:
+            before_gram = nearest
+        included = small(include_kernel, "include", [memory_sum, memory_prior, gram_sum])
+        memory_got = hops(included, size)
+        if gram_prior is None:
+            gram_near = after(gram_near, included)
+        pending = [memory_prior, before_gram, *memory_got], {"bit": bit, "fresh": size < block}
         size, bit = 2 * size, bit + 1
+    if gram_prior is None:
+        gram_prior = small(direct_kernel, "direct", gram_near, block=block)
 
     def memory_at(*ready):
         if pending is None:
             return memory_prior
-        before, before_gram, got, *rest = pending
-        return extend(before, before_gram, after(got, *ready), *rest)
+        (before, before_gram, *got), options = pending
+        return small(extend_kernel, "extend", [before, before_gram, *after(got, *ready)], **options)
 
     def swap(x):
         return lax.ppermute(x, "sub", [(i, (i + 1) % cores) for i in range(cores)])
 
-    steps = heads // step
     solved = []
     for turn in range(cores):
         solved.append(
             call(
                 functools.partial(solve_kernel, cores=cores, turn=turn, width=width),
-                steps,
+                1,
                 [smem] + [vmem] * 9,
                 [vmem] * 2,
                 [

time: 40.1 us -> 42.7 us (1.065)
  the two profiles are of different devices: /device:TPU:15 before, /device:TPU:31 now
where the time goes in v4:
time: 42.7 us; the launch traced here: 41.9 us
  Pallas kernels  21.6 us (51%)
  starting transfers between devices  10.7 us (25%)
  waiting for transfers between devices  9.29 us (22%)
    ppermute x3, waiting for transfers between devices, hops(): got.append(lax.ppermute(x, 'seq', pairs))  9.28 us
    pallas_call x2, Pallas kernels, per_device(): call(functools.partial(solve_kernel, cores=cores, turn=turn, width=width)...  8.46 us
    pallas_call x1, Pallas kernels, per_device(): call(functools.partial(prepare_kernel, total=total, width=width), head_co...  4.15 us
    pallas_call x1, Pallas kernels, per_device(): call(functools.partial(sums_kernel, total=total, heads=heads, width=width...  4.13 us
    ppermute x3, starting transfers between devices, per_device(): lax.ppermute(gram_sum, 'seq', [(i, i + ahead) for i in range(seq - ahead)...  3.88 us
    ppermute x2, starting transfers between devices, swap(): return lax.ppermute(x, 'sub', [(i, (i + 1) % cores) for i in range(cores)])  3.55 us
    ppermute x3, starting transfers between devices, hops(): got.append(lax.ppermute(x, 'seq', pairs))  3.26 us
    pallas_call x2, Pallas kernels, per_device(): call(functools.partial(read_kernel, cores=cores, turn=turn, width=width),...  3.14 us
  transfers between devices with their start and end apart: 8, of which 2 were waited for; matrix products, arithmetic and copies ran while one was open for 0% of the time, Pallas kernels for 37%

profile of v4, /device:TPU:31, one launch (start us, length us, event | category | flops | bytes accessed | tf_op | source)
XLA Modules:
  0.0 41.9 jit_solution(9045806600394167655)
XLA Ops:
  0.0 0.0 copy-start.1
  0.0 0.0 copy-start
  0.0 0.1 pad_add_fusion.where_ref
  0.1 4.1 %shard_sums.1 = (f32[264,128]{1,0:T(8,128)S(1)}, f32[4,128,128]{2,1,0:T(8,128)S(1)}) custom-call(s32[2]{0:T(128)S(1)} %pad_add_fusion.where_ref, s32[3]{0:T(128)} %doc_ref.3, f32[8]{0:T(128)} %rate_ref.3, bf16[512,1024]{1,0:T(8,128)(2,1)} %key_ref.5, bf16[512,1024]{1,0:T(8,128)(2,1)} %value_hbm.1, s32[8,512]{1,0:T(8,128)} %bitcast.3), custom_call_target="tpu_custom_call" | custom-call | flops 1073741824 | bytes 4194304 | tf_op jit(solution)/shard_map/shard_sums/pallas_call | solution.py:421
  4.3 1.3 %collective-permute-start = (f32[264,128]{1,0:T(8,128)S(1)}, f32[264,128]{1,0:T(8,128)S(1)}, u32[]{:S(2)}, u32[]{:S(2)}) collective-permute-start(f32[264,128]{1,0:T(8,128)S(1)} %get-tuple-element.31.own_gram), channel_id=1, source_target_pairs={{0,4},{4,8},{8,12},{1,5},{5,9},{9,13},{2,6},{6,10},{10,14},{3,7},{... | collective-permute-start | bytes 405512 | tf_op jit(solution)/shard_map/ppermute | solution.py:514
  5.6 1.3 %collective-permute-start.1 = (f32[264,128]{1,0:T(8,128)S(1)}, f32[264,128]{1,0:T(8,128)S(1)}, u32[]{:S(2)}, u32[]{:S(2)}) collective-permute-start(f32[264,128]{1,0:T(8,128)S(1)} %get-tuple-element.31.own_gram), channel_id=1, source_target_pairs={{0,8},{4,12},{1,9},{5,13},{2,10},{6,14},{3,11},{7,15},{16,24},{20,... | collective-permute-start | bytes 405512 | tf_op jit(solution)/shard_map/ppermute | solution.py:514
  6.9 1.3 %collective-permute-start.2 = (f32[264,128]{1,0:T(8,128)S(1)}, f32[264,128]{1,0:T(8,128)S(1)}, u32[]{:S(2)}, u32[]{:S(2)}) collective-permute-start(f32[264,128]{1,0:T(8,128)S(1)} %get-tuple-element.31.own_gram), channel_id=1, source_target_pairs={{0,12},{1,13},{2,14},{3,15},{16,28},{17,29},{18,30},{19,31}} | collective-permute-start | bytes 405512 | tf_op jit(solution)/shard_map/ppermute | solution.py:514
  8.2 0.0 copy-start.6
  8.2 1.3 %collective-permute-start.3 = (f32[4,128,128]{2,1,0:T(8,128)S(1)}, f32[4,128,128]{2,1,0:T(8,128)S(1)}, u32[]{:S(2)}, u32[]{:S(2)}) collective-permute-start(f32[4,128,128]{2,1,0:T(8,128)S(1)} %get-tuple-element.32.own_ref), channel_id=1, source_target_pairs={{0,4},{8,12},{1,5},{9,13},{2,6},{10,14},{3,7},{11,15},{16,20},{24,... | collective-permute-start | bytes 786440 | tf_op jit(solution)/shard_map/ppermute | solution.py:497
  9.5 0.0 copy-done.3
  9.5 0.0 copy-done.4
  9.5 0.0 copy-done.5
  9.5 4.1 %prepare.1 = (f32[8,256,256]{2,1,0:T(8,128)S(1)}, bf16[8,128,256]{2,1,0:T(8,128)(2,1)S(1)}, bf16[8,128,256]{2,1,0:T(8,128)(2,1)S(1)}, bf16[8,128,256]{2,1,0:T(8,...) custom-call(s32[2]{0:T(128)S(1)} %pad_add_fusion.where_ref, ...), custom_call_target="tpu_custom_call" | custom-call | flops 4294967296 | bytes 4194304 | tf_op jit(solution)/shard_map/prepare/pallas_call | solution.py:451
  13.7 8.6 %collective-permute-done.3.before_ref = f32[4,128,128]{2,1,0:T(8,128)S(1)} collective-permute-done((f32[4,128,128]{2,1,0:T(8,128)S(1)}, f32[4,128,128]{2,1,0:T(8,128)S(1)}, u32[]{:S(2)}, u32[]{:S(2)}) %collective-permute-start.3) | collective-permute-done | bytes 262176 | tf_op jit(solution)/shard_map/ppermute | solution.py:497
  22.3 0.6 %include.1 = f32[4,128,128]{2,1,0:T(8,128)S(1)} custom-call(s32[2]{0:T(128)S(1)} %pad_add_fusion.where_ref, f32[4,128,128]{2,1,0:T(8,128)S(1)} %get-tuple-element.32.own_ref, f32[4,128,128]{2,1,0:T(8,128)S(1)} %collective-permute-done.3.before_ref, f32[264,128]{1,0:T(8,128)S(1)} %get-tuple-element.31.own_gram), custom_call_target="tpu_custom_call" | custom-call | flops 1048576 | bytes 4194304 | tf_op jit(solution)/shard_map/include/pallas_call | solution.py:501
  22.9 0.7 %collective-permute-start.5 = (f32[4,128,128]{2,1,0:T(8,128)S(1)}, f32[4,128,128]{2,1,0:T(8,128)S(1)}, u32[]{:S(2)}, u32[]{:S(2)}) collective-permute-start(f32[4,128,128]{2,1,0:T(8,128)S(1)} %include.1), channel_id=1, source_target_pairs={{4,8},{5,9},{6,10},{7,11},{20,24},{21,25},{22,26},{23,27}} | collective-permute-start | bytes 786440 | tf_op jit(solution)/shard_map/ppermute | solution.py:497
  23.6 1.3 %collective-permute-start.6 = (f32[4,128,128]{2,1,0:T(8,128)S(1)}, f32[4,128,128]{2,1,0:T(8,128)S(1)}, u32[]{:S(2)}, u32[]{:S(2)}) collective-permute-start(f32[4,128,128]{2,1,0:T(8,128)S(1)} %include.1), channel_id=1, source_target_pairs={{4,12},{5,13},{6,14},{7,15},{20,28},{21,29},{22,30},{23,31}} | collective-permute-start | bytes 786440 | tf_op jit(solution)/shard_map/ppermute | solution.py:497
  24.9 0.0 collective-permute-done.rest_0_.before_gram
  24.9 0.0 collective-permute-done.1.rest_1_
  24.9 0.0 collective-permute-done.2.rest_2_
  24.9 0.6 %direct.1.gram_ref = f32[264,128]{1,0:T(8,128)S(1)} custom-call(s32[2]{0:T(128)S(1)} %pad_add_fusion.where_ref, f32[264,128]{1,0:T(8,128)S(1)} %collective-permute-done.rest_0_.before_gram, f32[264,128]{1,0:T(8,128)S(1)} %collective-permute-done.1.rest_1_, f32[264,128]{1,0:T(8,128)S(1)} %collective-permute-done.2.rest_2_), custom_call_target="tpu_custom_call" | custom-call | flops 1048576 | bytes 4194304 | tf_op jit(solution)/shard_map/direct/pallas_call | solution.py:501
  25.5 1.3 %collective-permute-start.4 = (f32[264,128]{1,0:T(8,128)S(1)}, f32[264,128]{1,0:T(8,128)S(1)}, u32[]{:S(2)}, u32[]{:S(2)}) collective-permute-start(f32[264,128]{1,0:T(8,128)S(1)} %direct.1.gram_ref), channel_id=1, source_target_pairs={{0,1},{1,0},{2,3},{3,2},{4,5},{5,4},{6,7},{7,6},{8,9},{9,8},{10,11... | collective-permute-start | bytes 405512 | tf_op jit(solution)/shard_map/ppermute | solution.py:550
  26.8 4.2 %solve_0.1 = (bf16[4,256,256]{2,1,0:T(8,128)(2,1)S(1)}, f32[4,256,128]{2,1,0:T(8,128)S(1)}) custom-call(s32[2]{0:T(128)S(1)} %pad_add_fusion.where_ref, f32[8]{0:T(128)S(1)} %copy-done.6, bf16[512,1024]{1,0:T(8,128)(2,1)S(1)} %copy-done.1, f32[8,256,256]{2,1,0:T(8,128)S(1)} %get-tuple-element.24.gate_ref, ...), custom_call_target="tpu_custom_call" | custom-call | flops 2147483648 | bytes 4194304 | tf_op jit(solution)/shard_map/solve_0/pallas_call | solution.py:555
  31.1 0.0 collective-permute-done.4.gram_ref
  31.1 4.2 %solve_1.1 = (bf16[4,256,256]{2,1,0:T(8,128)(2,1)S(1)}, f32[4,256,128]{2,1,0:T(8,128)S(1)}) custom-call(s32[2]{0:T(128)S(1)} %pad_add_fusion.where_ref, f32[8]{0:T(128)S(1)} %copy-done.6, bf16[512,1024]{1,0:T(8,128)(2,1)S(1)} %copy-done.1, f32[8,256,256]{2,1,0:T(8,128)S(1)} %get-tuple-element.24.gate_ref, ...), custom_call_target="tpu_custom_call" | custom-call | flops 2147483648 | bytes 4194304 | tf_op jit(solution)/shard_map/solve_1/pallas_call | solution.py:555
  35.3 0.0 collective-permute-done.5.rest_0_
  35.3 0.6 %collective-permute-done.6.rest_1_ = f32[4,128,128]{2,1,0:T(8,128)S(1)} collective-permute-done((f32[4,128,128]{2,1,0:T(8,128)S(1)}, f32[4,128,128]{2,1,0:T(8,128)S(1)}, u32[]{:S(2)}, u32[]{:S(2)}) %collective-permute-start.6) | collective-permute-done | bytes 262176 | tf_op jit(solution)/shard_map/ppermute | solution.py:497
  35.9 0.6 %extend.1.memory_ref = f32[4,128,128]{2,1,0:T(8,128)S(1)} custom-call(s32[2]{0:T(128)S(1)} %pad_add_fusion.where_ref, f32[4,128,128]{2,1,0:T(8,128)S(1)} %collective-permute-done.3.before_ref, f32[264,128]{1,0:T(8,128)S(1)} %collective-permute-done.rest_0_.before_gram, f32[4,128,128]{2,1,0:T(8,128)S(1)} %collective-permute-done.5.rest_0_, ...), custom_call_target="tpu_custom_call" | custom-call | flops 1048576 | bytes 4194304 | tf_op jit(solution)/shard_map/extend/pallas_call | solution.py:501
  36.5 2.2 %collective-permute-start.7 = (f32[4,128,128]{2,1,0:T(8,128)S(1)}, f32[4,128,128]{2,1,0:T(8,128)S(1)}, u32[]{:S(2)}, u32[]{:S(2)}) collective-permute-start(f32[4,128,128]{2,1,0:T(8,128)S(1)} %extend.1.memory_ref), channel_id=1, source_target_pairs={{0,1},{1,0},{2,3},{3,2},{4,5},{5,4},{6,7},{7,6},{8,9},{9,8},{10,11... | collective-permute-start | bytes 786440 | tf_op jit(solution)/shard_map/ppermute | solution.py:550
  38.8 1.6 %read_0.1.rest_0_ = bf16[256,1024]{1,0:T(8,128)(2,1)} custom-call(s32[2]{0:T(128)S(1)} %pad_add_fusion.where_ref, bf16[4,256,256]{2,1,0:T(8,128)(2,1)S(1)} %get-tuple-element.39.solution_ref, f32[4,256,128]{2,1,0:T(8,128)S(1)} %get-tuple-element.40.chunk_ref, f32[8,72,128]{2,1,0:T(8,128)S(1)} %get-tuple-element.29.mid_ref, ...), custom_call_target="tpu_custom_call" | custom-call | flops 268435456 | bytes 4194304 | tf_op jit(solution)/shard_map/read_0/pallas_call | solution.py:583
  40.4 0.0 collective-permute-done.7.memory_ref
  40.4 1.6 %read_1.1 = bf16[256,1024]{1,0:T(8,128)(2,1)} custom-call(s32[2]{0:T(128)S(1)} %pad_add_fusion.where_ref, bf16[4,256,256]{2,1,0:T(8,128)(2,1)S(1)} %get-tuple-element.36.solution_ref, f32[4,256,128]{2,1,0:T(8,128)S(1)} %get-tuple-element.37.chunk_ref, f32[8,72,128]{2,1,0:T(8,128)S(1)} %get-tuple-element.29.mid_ref, ...), custom_call_target="tpu_custom_call", output_to_operand_aliasing={{}: (6, {})} | custom-call | flops 268435456 | bytes 4194304 | tf_op jit(solution)/shard_map/read_1/pallas_call | solution.py:583
  (8 shorter events, 0.0 us)
Async XLA Ops:
  0.0 9.5 %copy-start.3 = (s32[512,8]{0,1:T(8,128)S(1)}, s32[512,8]{0,1:T(8,128)}, u32[]{:S(2)}) copy-start(s32[512,8]{0,1:T(8,128)} %param.10) | copy-start | bytes 49156
  0.0 9.5 %copy-start.4 = (s32[3]{0:T(128)S(1)}, s32[3]{0:T(128)}, u32[]{:S(2)}) copy-start(s32[3]{0:T(128)} %doc_ref.3) | copy-start | bytes 40
  0.0 9.5 %copy-start.5 = (f32[8]{0:T(128)S(1)}, f32[8]{0:T(128)}, u32[]{:S(2)}) copy-start(f32[8]{0:T(128)} %rate_ref.3) | copy-start | bytes 100
  0.0 9.5 %copy-start.1 = (bf16[512,1024]{1,0:T(8,128)(2,1)S(1)}, bf16[512,1024]{1,0:T(8,128)(2,1)}, u32[]{:S(2)}) copy-start(bf16[512,1024]{1,0:T(8,128)(2,1)} %key_ref.5) | copy-start | bytes 3145732
  0.0 9.5 %copy-start = (bf16[512,1024]{1,0:T(8,128)(2,1)S(1)}, bf16[512,1024]{1,0:T(8,128)(2,1)}, u32[]{:S(2)}) copy-start(bf16[512,1024]{1,0:T(8,128)(2,1)} %value_hbm.1) | copy-start | bytes 3145732
  0.0 9.5 %copy-start.2 = (bf16[256,1024]{1,0:T(8,128)(2,1)S(1)}, bf16[256,1024]{1,0:T(8,128)(2,1)}, u32[]{:S(2)}) copy-start(bf16[256,1024]{1,0:T(8,128)(2,1)} %query_ref.1) | copy-start | bytes 1572868
  4.3 20.6 %collective-permute-start = (f32[264,128]{1,0:T(8,128)S(1)}, f32[264,128]{1,0:T(8,128)S(1)}, u32[]{:S(2)}, u32[]{:S(2)}) collective-permute-start(f32[264,128]{1,0:T(8,128)S(1)} %get-tuple-element.31.own_gram), channel_id=1, source_target_pairs={{0,4},{4,8},{8,12},{1,5},{5,9},{9,13},{2,6},{6,10},{10,14},{3,7},{... | collective-permute-start | bytes 405512 | tf_op jit(solution)/shard_map/ppermute | solution.py:514
  5.6 19.3 %collective-permute-start.1 = (f32[264,128]{1,0:T(8,128)S(1)}, f32[264,128]{1,0:T(8,128)S(1)}, u32[]{:S(2)}, u32[]{:S(2)}) collective-permute-start(f32[264,128]{1,0:T(8,128)S(1)} %get-tuple-element.31.own_gram), channel_id=1, source_target_pairs={{0,8},{4,12},{1,9},{5,13},{2,10},{6,14},{3,11},{7,15},{16,24},{20,... | collective-permute-start | bytes 405512 | tf_op jit(solution)/shard_map/ppermute | solution.py:514
  6.9 18.1 %collective-permute-start.2 = (f32[264,128]{1,0:T(8,128)S(1)}, f32[264,128]{1,0:T(8,128)S(1)}, u32[]{:S(2)}, u32[]{:S(2)}) collective-permute-start(f32[264,128]{1,0:T(8,128)S(1)} %get-tuple-element.31.own_gram), channel_id=1, source_target_pairs={{0,12},{1,13},{2,14},{3,15},{16,28},{17,29},{18,30},{19,31}} | collective-permute-start | bytes 405512 | tf_op jit(solution)/shard_map/ppermute | solution.py:514
  8.2 18.6 %copy-start.6 = (f32[8]{0:T(128)S(1)}, f32[8]{0:T(128)}, u32[]{:S(2)}) copy-start(f32[8]{0:T(128)} %ridge_ref.3) | copy-start | bytes 100
  8.2 14.2 %collective-permute-start.3 = (f32[4,128,128]{2,1,0:T(8,128)S(1)}, f32[4,128,128]{2,1,0:T(8,128)S(1)}, u32[]{:S(2)}, u32[]{:S(2)}) collective-permute-start(f32[4,128,128]{2,1,0:T(8,128)S(1)} %get-tuple-element.32.own_ref), channel_id=1, source_target_pairs={{0,4},{8,12},{1,5},{9,13},{2,6},{10,14},{3,7},{11,15},{16,20},{24,... | collective-permute-start | bytes 786440 | tf_op jit(solution)/shard_map/ppermute | solution.py:497
  22.9 12.4 %collective-permute-start.5 = (f32[4,128,128]{2,1,0:T(8,128)S(1)}, f32[4,128,128]{2,1,0:T(8,128)S(1)}, u32[]{:S(2)}, u32[]{:S(2)}) collective-permute-start(f32[4,128,128]{2,1,0:T(8,128)S(1)} %include.1), channel_id=1, source_target_pairs={{4,8},{5,9},{6,10},{7,11},{20,24},{21,25},{22,26},{23,27}} | collective-permute-start | bytes 786440 | tf_op jit(solution)/shard_map/ppermute | solution.py:497
  23.6 12.3 %collective-permute-start.6 = (f32[4,128,128]{2,1,0:T(8,128)S(1)}, f32[4,128,128]{2,1,0:T(8,128)S(1)}, u32[]{:S(2)}, u32[]{:S(2)}) collective-permute-start(f32[4,128,128]{2,1,0:T(8,128)S(1)} %include.1), channel_id=1, source_target_pairs={{4,12},{5,13},{6,14},{7,15},{20,28},{21,29},{22,30},{23,31}} | collective-permute-start | bytes 786440 | tf_op jit(solution)/shard_map/ppermute | solution.py:497
  25.5 5.5 %collective-permute-start.4 = (f32[264,128]{1,0:T(8,128)S(1)}, f32[264,128]{1,0:T(8,128)S(1)}, u32[]{:S(2)}, u32[]{:S(2)}) collective-permute-start(f32[264,128]{1,0:T(8,128)S(1)} %direct.1.gram_ref), channel_id=1, source_target_pairs={{0,1},{1,0},{2,3},{3,2},{4,5},{5,4},{6,7},{7,6},{8,9},{9,8},{10,11... | collective-permute-start | bytes 405512 | tf_op jit(solution)/shard_map/ppermute | solution.py:550
  36.5 3.8 %collective-permute-start.7 = (f32[4,128,128]{2,1,0:T(8,128)S(1)}, f32[4,128,128]{2,1,0:T(8,128)S(1)}, u32[]{:S(2)}, u32[]{:S(2)}) collective-permute-start(f32[4,128,128]{2,1,0:T(8,128)S(1)} %extend.1.memory_ref), channel_id=1, source_target_pairs={{0,1},{1,0},{2,3},{3,2},{4,5},{5,4},{6,7},{7,6},{8,9},{9,8},{10,11... | collective-permute-start | bytes 786440 | tf_op jit(solution)/shard_map/ppermute | solution.py:550

commit v5 on v3

--- a/solution.py
+++ b/solution.py
@@ -102,12 +102,14 @@
 
 
 def sums_kernel(
-    where_ref, doc_ref, rate_ref, key_hbm, value_hbm, bins_ref, gram_ref, memory_ref,
-    weight_ref, decay_ref, both_ref, sems, *, total, heads, width,
+    doc_ref, rate_ref, key_hbm, value_hbm, bins_hbm, gram_ref, memory_ref,
+    weight_ref, decay_ref, both_ref, bins_ref, sems, bins_sem, *, total, heads, width,
 ):
     shard = key_hbm.shape[0]
-    first = where_ref[0] * shard
-    core = where_ref[1]
+    first = lax.axis_index("seq") * shard
+    core = lax.axis_index("sub")
+    bins_copy = pltpu.make_async_copy(bins_hbm, bins_ref, bins_sem)
+    bins_copy.start()
     copies = []
     for i in range(heads):
         cols = pl.ds(pl.multiple_of((core * heads + i) * width, width), width)
@@ -116,6 +118,7 @@
             copies.append(pltpu.make_async_copy(source.at[:, cols], target, sems.at[i, part]))
             copies[-1].start()
     scale = scale_column(rate_ref, total)
+    bins_copy.wait()
     cumulative = running_rows(bins_ref[...])
     last = cumulative[:, shard - 1 :]
     position = first + iota((1, shard), 1)
@@ -141,8 +144,8 @@
     return gram_ref[i, half + 1 : half + 2, :]
 
 
-def include_kernel(where_ref, own_ref, before_ref, own_gram, before_gram, out_ref, *, half, fresh):
-    received = (where_ref[0] & 1) == 1
+def include_kernel(own_ref, before_ref, own_gram, before_gram, out_ref, *, half, fresh):
+    received = (lax.axis_index("seq") & 1) == 1
     for i in range(own_ref.shape[0]):
         decay = decay_line(own_gram, i, half)
         state = own_ref[i] + decay * before_ref[i]
@@ -153,10 +156,10 @@
         out_ref[i] = state
 
 
-def extend_kernel(where_ref, before_ref, before_gram, *rest, half, bit, fresh):
+def extend_kernel(before_ref, before_gram, *rest, half, bit, fresh):
     out_ref = rest[-1]
-    first_received = (where_ref[0] & 1) == 1
-    received = ((where_ref[0] >> bit) & 1) == 1
+    first_received = (lax.axis_index("seq") & 1) == 1
+    received = ((lax.axis_index("seq") >> bit) & 1) == 1
     for i in range(before_ref.shape[0]):
         arrived = rest[0][i]
         for other in rest[1:-1]:
@@ -171,13 +174,13 @@
 
 
 def prepare_kernel(
-    where_ref, doc_ref, rate_ref, query_ref, key_ref, value_ref, bins_ref,
+    doc_ref, rate_ref, query_ref, key_ref, value_ref, bins_ref,
     gate_ref, query_t_ref, key_t_ref, value_t_ref, within_ref, mid_gram_ref, mid_memory_ref, carried_ref,
     row_ref, column_ref, mid_ref, decay_ref, *, total, width,
 ):
     shard, rows = key_ref.shape[0], query_ref.shape[0]
-    first = where_ref[0] * shard
-    start = where_ref[1] * rows
+    first = lax.axis_index("seq") * shard
+    start = lax.axis_index("sub") * rows
     own = pl.ds(pl.multiple_of(start, rows), rows)
     before_doc = doc_of(doc_ref, first + start - 1)
     key_pos = first + start + iota((rows, 1), 0)
@@ -233,11 +236,11 @@
 
 
 def solve_kernel(
-    where_ref, ridge_ref, key_ref, gate_ref, query_t_ref, key_t_ref, value_t_ref, within_ref, mid_ref, carried_ref,
+    ridge_ref, key_ref, gate_ref, query_t_ref, key_t_ref, value_t_ref, within_ref, mid_ref, carried_ref,
     gram_ref, solution_ref, chunk_ref, *, cores, turn, width,
 ):
     rows = query_t_ref.shape[2]
-    core = where_ref[1]
+    core = lax.axis_index("sub")
     steps = pl.num_programs(0)
     group = lax.rem(core + turn, cores)
     own = pl.ds(pl.multiple_of(core * rows, rows), rows)
@@ -326,11 +329,11 @@
                 running.remove(program)
 
 
-def read_kernel(where_ref, solution_ref, chunk_ref, mid_ref, mid_memory_ref, memory_ref, *rest, cores, turn, width):
+def read_kernel(solution_ref, chunk_ref, mid_ref, mid_memory_ref, memory_ref, *rest, cores, turn, width):
     out_ref = rest[-1]
     half = width // 2
     heads = solution_ref.shape[0]
-    base = lax.rem(where_ref[1] + turn, cores) * heads
+    base = lax.rem(lax.axis_index("sub") + turn, cores) * heads
     for i in range(heads):
         decay = mid_ref[base + i, half + 1 : half + 2, :]
         memory = mid_memory_ref[base + i] + decay * memory_ref[i]
@@ -353,7 +356,6 @@
     cores = lax.axis_size("sub")
     heads = head_count // cores
     total = shard * seq
-    where = jnp.stack([lax.axis_index("seq"), lax.axis_index("sub")]).astype(jnp.int32)
     bins = gate_bins.T
     smem = pl.BlockSpec(memory_space=pltpu.SMEM)
     any_space = pl.BlockSpec(memory_space=pl.ANY)
@@ -364,18 +366,15 @@
         return pltpu.with_memory_space_constraint(x, pltpu.HBM)
 
     def full(*shape):
-        return pl.BlockSpec(shape, lambda i, where_ref: (0,) * len(shape))
+        return pl.BlockSpec(shape, lambda i: (0,) * len(shape))
 
     def call(kernel, grid, in_specs, out_specs, out_shape, scratch, name, cost, **options):
         return pl.pallas_call(
             kernel,
-            grid_spec=pltpu.PrefetchScalarGridSpec(
-                num_scalar_prefetch=1,
-                grid=(grid,),
-                in_specs=in_specs,
-                out_specs=out_specs,
-                scratch_shapes=scratch,
-            ),
+            grid=(grid,),
+            in_specs=in_specs,
+            out_specs=out_specs,
+            scratch_shapes=scratch,
             out_shape=out_shape,
             name=name,
             cost_estimate=pl.CostEstimate(flops=cost, bytes_accessed=4 << 20, transcendentals=0),
@@ -386,7 +385,7 @@
     gram_sum, memory_sum = call(
         functools.partial(sums_kernel, total=total, heads=heads, width=width),
         1,
-        [smem, smem, hbm, hbm, full(head_count, shard)],
+        [smem, smem, hbm, hbm, hbm],
         [vmem] * 2,
         [
             jax.ShapeDtypeStruct((heads, half + PAD, width), f32),
@@ -396,19 +395,21 @@
             pltpu.VMEM((head_count, shard), f32),
             pltpu.VMEM((head_count, width), f32),
             pltpu.VMEM((2, heads, shard, width), bf16),
+            pltpu.VMEM((head_count, shard), jnp.int32),
             pltpu.SemaphoreType.DMA((heads, 2)),
+            pltpu.SemaphoreType.DMA,
         ],
         "shard_sums",
         1 << 30,
-    )(where, pinned(doc_lengths), pinned(decay_rates), pinned(key_vectors), pinned(value_vectors), pinned(bins))
+    )(pinned(doc_lengths), pinned(decay_rates), pinned(key_vectors), pinned(value_vectors), pinned(bins))
 
     step = min(PER_STEP, heads)
 
     def head_block(*shape):
-        return pl.BlockSpec((step, *shape), lambda i, where_ref: (i,) + (0,) * len(shape))
+        return pl.BlockSpec((step, *shape), lambda i: (i,) + (0,) * len(shape))
 
     def step_block(count):
-        return pl.BlockSpec((count, step * width), lambda i, where_ref: (0, i))
+        return pl.BlockSpec((count, step * width), lambda i: (0, i))
 
     def per_head(*shape, dtype=f32):
         return jax.ShapeDtypeStruct((head_count, *shape), dtype)
@@ -445,7 +446,7 @@
         ],
         "prepare",
         4 << 30,
-    )(where, doc_lengths, decay_rates, queries, key_vectors, value_vectors, bins)
+    )(doc_lengths, decay_rates, queries, key_vectors, value_vectors, bins)
 
     def after(x, *others):
         return lax.optimization_barrier((x, others))[0]
@@ -472,7 +473,7 @@
             [],
             name,
             1 << 20,
-        )(where, *operands)
+        )(*operands)
 
     def include(own, before, before_gram, fresh):
         kernel = functools.partial(include_kernel, half=half, fresh=fresh)
@@ -483,6 +484,7 @@
         return small(kernel, "extend", [before, before_gram, *got])
 
     (gram_prior,), (memory_prior,) = hops(gram_sum, 1), hops(memory_sum, 1)
+    gram_prior = after(gram_prior, carried)
     size, bit = 2, 1
     pending = None
     while size < seq:
@@ -521,7 +523,7 @@
                 f"solve_{turn}",
                 2 << 30,
             )(
-                where, ridge_terms, key_vectors, gate, query_t, key_t, value_t, within, mid_gram, carried,
+                ridge_terms, key_vectors, gate, query_t, key_t, value_t, within, mid_gram, carried,
                 gram_prior if turn == 0 else swap(gram_prior),
             )
         )
@@ -530,7 +532,7 @@
     output = None
     for turn in range(cores):
         in_specs = [vmem] * 5
-        operands = [where, *solved[turn], mid_gram, mid_memory, memory_prior if turn == 0 else swap(memory_prior)]
+        operands = [*solved[turn], mid_gram, mid_memory, memory_prior if turn == 0 else swap(memory_prior)]
         aliases = {}
         if output is not None:
             aliases = {len(operands): 0}
@@ -541,7 +543,7 @@
             1,
             in_specs,
             pl.BlockSpec(
-                (rows, heads * width), lambda i, where_ref, turn=turn: (0, lax.rem(where_ref[1] + turn, cores))
+                (rows, heads * width), lambda i, turn=turn: (0, lax.rem(lax.axis_index("sub") + turn, cores))
             ),
             jax.ShapeDtypeStruct((rows, head_count * width), bf16),
             [],

time: 40.1 us -> 37.2 us (0.928)
  the two profiles are of different devices: /device:TPU:15 before, /device:TPU:31 now
where the time goes in v5:
time: 37.2 us; the launch traced here: 36.9 us
  Pallas kernels  16.7 us (45%)
  starting transfers between devices  11.7 us (31%)
  waiting for transfers between devices  8.3 us (22%)
    ppermute x6, waiting for transfers between devices, hops(): got.append(lax.ppermute(x, 'seq', pairs))  8.16 us
    pallas_call x2, Pallas kernels, per_device(): call(functools.partial(solve_kernel, cores=cores, turn=turn, width=width)...  7.07 us
    ppermute x6, starting transfers between devices, hops(): got.append(lax.ppermute(x, 'seq', pairs))  6.52 us
    ppermute x2, starting transfers between devices, swap(): return lax.ppermute(x, 'sub', [(i, (i + 1) % cores) for i in range(cores)])  5.14 us
    pallas_call x1, Pallas kernels, per_device(): call(functools.partial(sums_kernel, total=total, heads=heads, width=width...  3.86 us
    pallas_call x1, Pallas kernels, per_device(): call(functools.partial(prepare_kernel, total=total, width=width), head_co...  3.65 us
    pallas_call x2, Pallas kernels, per_device(): call(functools.partial(read_kernel, cores=cores, turn=turn, width=width),...  2.04 us
  transfers between devices with their start and end apart: 8, of which 5 were waited for; matrix products, arithmetic and copies ran while one was open for 0% of the time, Pallas kernels for 32%

profile of v5, /device:TPU:31, one launch (start us, length us, event | category | flops | bytes accessed | tf_op | source)
XLA Modules:
  0.0 36.9 jit_solution(8628789825767080298)
XLA Ops:
  0.0 0.0 copy-start.1
  0.0 0.0 copy-start
  0.0 0.0 copy-start.2
  0.0 3.9 %shard_sums.1 = (f32[4,72,128]{2,1,0:T(8,128)S(1)}, f32[4,128,128]{2,1,0:T(8,128)S(1)}) custom-call(s32[3]{0:T(128)} %doc_ref.3, f32[8]{0:T(128)} %rate_ref.3, bf16[512,1024]{1,0:T(8,128)(2,1)} %key_ref.5, bf16[512,1024]{1,0:T(8,128)(2,1)} %value_hbm.1, s32[8,512]{1,0:T(8,128)} %bitcast.1), custom_call_target="tpu_custom_call" | custom-call | flops 1073741824 | bytes 4194304 | tf_op jit(solution)/shard_map/shard_sums/pallas_call | solution.py:385
  3.9 1.3 %collective-permute-start = (f32[4,72,128]{2,1,0:T(8,128)S(1)}, f32[4,72,128]{2,1,0:T(8,128)S(1)}, u32[]{:S(2)}, u32[]{:S(2)}) collective-permute-start(f32[4,72,128]{2,1,0:T(8,128)S(1)} %get-tuple-element.29.own_ref.own_gram), channel_id=1, source_target_pairs={{0,4},{8,12},{1,5},{9,13},{2,6},{10,14},{3,7},{11,15},{16,20},{24,... | collective-permute-start | bytes 442376 | tf_op jit(solution)/shard_map/ppermute | solution.py:463
  5.2 1.3 %collective-permute-start.4 = (f32[4,128,128]{2,1,0:T(8,128)S(1)}, f32[4,128,128]{2,1,0:T(8,128)S(1)}, u32[]{:S(2)}, u32[]{:S(2)}) collective-permute-start(f32[4,128,128]{2,1,0:T(8,128)S(1)} %get-tuple-element.34.own_ref), channel_id=1, source_target_pairs={{0,4},{8,12},{1,5},{9,13},{2,6},{10,14},{3,7},{11,15},{16,20},{24,... | collective-permute-start | bytes 786440 | tf_op jit(solution)/shard_map/ppermute | solution.py:463
  6.5 0.0 copy-done.3
  6.5 0.0 copy-done.4
  6.5 0.0 copy-done.5
  6.5 0.0 copy-done.1
  6.5 0.0 copy-done
  6.6 0.0 copy-done.2
  6.6 3.7 %prepare.1 = (f32[8,256,256]{2,1,0:T(8,128)S(1)}, bf16[8,128,256]{2,1,0:T(8,128)(2,1)S(1)}, bf16[8,128,256]{2,1,0:T(8,128)(2,1)S(1)}, bf16[8,128,256]{2,1,0:T(8,...) custom-call(s32[3]{0:T(128)S(1)} %copy-done.4, ...), custom_call_target="tpu_custom_call" | custom-call | flops 4294967296 | bytes 4194304 | tf_op jit(solution)/shard_map/prepare/pallas_call | solution.py:417
  10.2 0.0 copy-start.6
  10.2 0.3 collective-permute-done.before_ref.before_gram
  10.6 0.7 %collective-permute-start.1 = (f32[4,72,128]{2,1,0:T(8,128)S(1)}, f32[4,72,128]{2,1,0:T(8,128)S(1)}, u32[]{:S(2)}, u32[]{:S(2)}) collective-permute-start(f32[4,72,128]{2,1,0:T(8,128)S(1)} %include.2), channel_id=1, source_target_pairs={{4,8},{5,9},{6,10},{7,11},{20,24},{21,25},{22,26},{23,27}} | collective-permute-start | bytes 442376 | tf_op jit(solution)/shard_map/ppermute | solution.py:463
  11.2 1.3 %collective-permute-start.2 = (f32[4,72,128]{2,1,0:T(8,128)S(1)}, f32[4,72,128]{2,1,0:T(8,128)S(1)}, u32[]{:S(2)}, u32[]{:S(2)}) collective-permute-start(f32[4,72,128]{2,1,0:T(8,128)S(1)} %include.2), channel_id=1, source_target_pairs={{4,12},{5,13},{6,14},{7,15},{20,28},{21,29},{22,30},{23,31}} | collective-permute-start | bytes 442376 | tf_op jit(solution)/shard_map/ppermute | solution.py:463
  12.5 3.6 %collective-permute-done.4.before_ref = f32[4,128,128]{2,1,0:T(8,128)S(1)} collective-permute-done((f32[4,128,128]{2,1,0:T(8,128)S(1)}, f32[4,128,128]{2,1,0:T(8,128)S(1)}, u32[]{:S(2)}, u32[]{:S(2)}) %collective-permute-start.4) | collective-permute-done | bytes 262176 | tf_op jit(solution)/shard_map/ppermute | solution.py:463
  16.2 0.7 %collective-permute-start.5 = (f32[4,128,128]{2,1,0:T(8,128)S(1)}, f32[4,128,128]{2,1,0:T(8,128)S(1)}, u32[]{:S(2)}, u32[]{:S(2)}) collective-permute-start(f32[4,128,128]{2,1,0:T(8,128)S(1)} %include.3), channel_id=1, source_target_pairs={{4,8},{5,9},{6,10},{7,11},{20,24},{21,25},{22,26},{23,27}} | collective-permute-start | bytes 786440 | tf_op jit(solution)/shard_map/ppermute | solution.py:463
  16.9 1.3 %collective-permute-start.6 = (f32[4,128,128]{2,1,0:T(8,128)S(1)}, f32[4,128,128]{2,1,0:T(8,128)S(1)}, u32[]{:S(2)}, u32[]{:S(2)}) collective-permute-start(f32[4,128,128]{2,1,0:T(8,128)S(1)} %include.3), channel_id=1, source_target_pairs={{4,12},{5,13},{6,14},{7,15},{20,28},{21,29},{22,30},{23,31}} | collective-permute-start | bytes 786440 | tf_op jit(solution)/shard_map/ppermute | solution.py:463
  18.2 0.0 collective-permute-done.1.rest_0_
  18.2 3.4 %collective-permute-done.2.rest_1_ = f32[4,72,128]{2,1,0:T(8,128)S(1)} collective-permute-done((f32[4,72,128]{2,1,0:T(8,128)S(1)}, f32[4,72,128]{2,1,0:T(8,128)S(1)}, u32[]{:S(2)}, u32[]{:S(2)}) %collective-permute-start.2) | collective-permute-done | bytes 147488 | tf_op jit(solution)/shard_map/ppermute | solution.py:463
  21.6 3.3 %collective-permute-start.3 = (f32[4,72,128]{2,1,0:T(8,128)S(1)}, f32[4,72,128]{2,1,0:T(8,128)S(1)}, u32[]{:S(2)}, u32[]{:S(2)}) collective-permute-start(f32[4,72,128]{2,1,0:T(8,128)S(1)} %extend.2.gram_ref), channel_id=1, source_target_pairs={{0,1},{1,0},{2,3},{3,2},{4,5},{5,4},{6,7},{7,6},{8,9},{9,8},{10,11... | collective-permute-start | bytes 442376 | tf_op jit(solution)/shard_map/ppermute | solution.py:507
  24.9 3.5 %solve_0.1 = (bf16[4,256,256]{2,1,0:T(8,128)(2,1)S(1)}, f32[4,256,128]{2,1,0:T(8,128)S(1)}) custom-call(f32[8]{0:T(128)S(1)} %copy-done.6, bf16[512,1024]{1,0:T(8,128)(2,1)S(1)} %copy-done.1, f32[8,256,256]{2,1,0:T(8,128)S(1)} %get-tuple-element.22.gate_ref, bf16[8,128,256]{2,1,0:T(8,128)(2,1)S(1)} %get-tuple-element.23.query_t_ref, ...), custom_call_target="tpu_custom_call" | custom-call | flops 2147483648 | bytes 4194304 | tf_op jit(solution)/shard_map/solve_0/pallas_call | solution.py:513
  28.5 0.0 collective-permute-done.3.gram_ref
  28.5 3.5 %solve_1.1 = (bf16[4,256,256]{2,1,0:T(8,128)(2,1)S(1)}, f32[4,256,128]{2,1,0:T(8,128)S(1)}) custom-call(f32[8]{0:T(128)S(1)} %copy-done.6, bf16[512,1024]{1,0:T(8,128)(2,1)S(1)} %copy-done.1, f32[8,256,256]{2,1,0:T(8,128)S(1)} %get-tuple-element.22.gate_ref, bf16[8,128,256]{2,1,0:T(8,128)(2,1)S(1)} %get-tuple-element.23.query_t_ref, ...), custom_call_target="tpu_custom_call" | custom-call | flops 2147483648 | bytes 4194304 | tf_op jit(solution)/shard_map/solve_1/pallas_call | solution.py:513
  32.0 0.0 collective-permute-done.5.rest_0_
  32.0 0.8 %collective-permute-done.6.rest_1_ = f32[4,128,128]{2,1,0:T(8,128)S(1)} collective-permute-done((f32[4,128,128]{2,1,0:T(8,128)S(1)}, f32[4,128,128]{2,1,0:T(8,128)S(1)}, u32[]{:S(2)}, u32[]{:S(2)}) %collective-permute-start.6) | collective-permute-done | bytes 262176 | tf_op jit(solution)/shard_map/ppermute | solution.py:463
  32.9 1.9 %collective-permute-start.7 = (f32[4,128,128]{2,1,0:T(8,128)S(1)}, f32[4,128,128]{2,1,0:T(8,128)S(1)}, u32[]{:S(2)}, u32[]{:S(2)}) collective-permute-start(f32[4,128,128]{2,1,0:T(8,128)S(1)} %extend.3.memory_ref), channel_id=1, source_target_pairs={{0,1},{1,0},{2,3},{3,2},{4,5},{5,4},{6,7},{7,6},{8,9},{9,8},{10,11... | collective-permute-start | bytes 786440 | tf_op jit(solution)/shard_map/ppermute | solution.py:507
  34.8 1.0 %read_0.1.rest_0_ = bf16[256,1024]{1,0:T(8,128)(2,1)} custom-call(bf16[4,256,256]{2,1,0:T(8,128)(2,1)S(1)} %get-tuple-element.35.solution_ref, f32[4,256,128]{2,1,0:T(8,128)S(1)} %get-tuple-element.36.chunk_ref, f32[8,72,128]{2,1,0:T(8,128)S(1)} %get-tuple-element.27.mid_ref, f32[8,128,128]{2,1,0:T(8,128)S(1)} %get-tuple-element.33.mid_memory_ref, ...), custom_call_target="tpu_custom_call" | custom-call | flops 268435456 | bytes 4194304 | tf_op jit(solution)/shard_map/read_0/pallas_call | solution.py:541
  35.8 0.1 collective-permute-done.7.memory_ref
  35.9 1.0 %read_1.1 = bf16[256,1024]{1,0:T(8,128)(2,1)} custom-call(bf16[4,256,256]{2,1,0:T(8,128)(2,1)S(1)} %get-tuple-element.31.solution_ref, f32[4,256,128]{2,1,0:T(8,128)S(1)} %get-tuple-element.32.chunk_ref, f32[8,72,128]{2,1,0:T(8,128)S(1)} %get-tuple-element.27.mid_ref, ...), custom_call_target="tpu_custom_call", output_to_operand_aliasing={{}: (5, {})} | custom-call | flops 268435456 | bytes 4194304 | tf_op jit(solution)/shard_map/read_1/pallas_call | solution.py:541
  (8 shorter events, 0.1 us)
Async XLA Ops:
  0.0 6.5 %copy-start.3 = (s32[512,8]{0,1:T(8,128)S(1)}, s32[512,8]{0,1:T(8,128)}, u32[]{:S(2)}) copy-start(s32[512,8]{0,1:T(8,128)} %param.10) | copy-start | bytes 49156
  0.0 6.5 %copy-start.4 = (s32[3]{0:T(128)S(1)}, s32[3]{0:T(128)}, u32[]{:S(2)}) copy-start(s32[3]{0:T(128)} %doc_ref.3) | copy-start | bytes 40
  0.0 6.5 %copy-start.5 = (f32[8]{0:T(128)S(1)}, f32[8]{0:T(128)}, u32[]{:S(2)}) copy-start(f32[8]{0:T(128)} %rate_ref.3) | copy-start | bytes 100
  0.0 6.5 %copy-start.1 = (bf16[512,1024]{1,0:T(8,128)(2,1)S(1)}, bf16[512,1024]{1,0:T(8,128)(2,1)}, u32[]{:S(2)}) copy-start(bf16[512,1024]{1,0:T(8,128)(2,1)} %key_ref.5) | copy-start | bytes 3145732
  0.0 6.5 %copy-start = (bf16[512,1024]{1,0:T(8,128)(2,1)S(1)}, bf16[512,1024]{1,0:T(8,128)(2,1)}, u32[]{:S(2)}) copy-start(bf16[512,1024]{1,0:T(8,128)(2,1)} %value_hbm.1) | copy-start | bytes 3145732
  0.0 6.5 %copy-start.2 = (bf16[256,1024]{1,0:T(8,128)(2,1)S(1)}, bf16[256,1024]{1,0:T(8,128)(2,1)}, u32[]{:S(2)}) copy-start(bf16[256,1024]{1,0:T(8,128)(2,1)} %query_ref.1) | copy-start | bytes 1572868
  3.9 6.6 %collective-permute-start = (f32[4,72,128]{2,1,0:T(8,128)S(1)}, f32[4,72,128]{2,1,0:T(8,128)S(1)}, u32[]{:S(2)}, u32[]{:S(2)}) collective-permute-start(f32[4,72,128]{2,1,0:T(8,128)S(1)} %get-tuple-element.29.own_ref.own_gram), channel_id=1, source_target_pairs={{0,4},{8,12},{1,5},{9,13},{2,6},{10,14},{3,7},{11,15},{16,20},{24,... | collective-permute-start | bytes 442376 | tf_op jit(solution)/shard_map/ppermute | solution.py:463
  5.2 10.9 %collective-permute-start.4 = (f32[4,128,128]{2,1,0:T(8,128)S(1)}, f32[4,128,128]{2,1,0:T(8,128)S(1)}, u32[]{:S(2)}, u32[]{:S(2)}) collective-permute-start(f32[4,128,128]{2,1,0:T(8,128)S(1)} %get-tuple-element.34.own_ref), channel_id=1, source_target_pairs={{0,4},{8,12},{1,5},{9,13},{2,6},{10,14},{3,7},{11,15},{16,20},{24,... | collective-permute-start | bytes 786440 | tf_op jit(solution)/shard_map/ppermute | solution.py:463
  10.2 14.7 %copy-start.6 = (f32[8]{0:T(128)S(1)}, f32[8]{0:T(128)}, u32[]{:S(2)}) copy-start(f32[8]{0:T(128)} %ridge_ref.3) | copy-start | bytes 100
  10.6 7.6 %collective-permute-start.1 = (f32[4,72,128]{2,1,0:T(8,128)S(1)}, f32[4,72,128]{2,1,0:T(8,128)S(1)}, u32[]{:S(2)}, u32[]{:S(2)}) collective-permute-start(f32[4,72,128]{2,1,0:T(8,128)S(1)} %include.2), channel_id=1, source_target_pairs={{4,8},{5,9},{6,10},{7,11},{20,24},{21,25},{22,26},{23,27}} | collective-permute-start | bytes 442376 | tf_op jit(solution)/shard_map/ppermute | solution.py:463
  11.2 10.4 %collective-permute-start.2 = (f32[4,72,128]{2,1,0:T(8,128)S(1)}, f32[4,72,128]{2,1,0:T(8,128)S(1)}, u32[]{:S(2)}, u32[]{:S(2)}) collective-permute-start(f32[4,72,128]{2,1,0:T(8,128)S(1)} %include.2), channel_id=1, source_target_pairs={{4,12},{5,13},{6,14},{7,15},{20,28},{21,29},{22,30},{23,31}} | collective-permute-start | bytes 442376 | tf_op jit(solution)/shard_map/ppermute | solution.py:463
  16.2 15.8 %collective-permute-start.5 = (f32[4,128,128]{2,1,0:T(8,128)S(1)}, f32[4,128,128]{2,1,0:T(8,128)S(1)}, u32[]{:S(2)}, u32[]{:S(2)}) collective-permute-start(f32[4,128,128]{2,1,0:T(8,128)S(1)} %include.3), channel_id=1, source_target_pairs={{4,8},{5,9},{6,10},{7,11},{20,24},{21,25},{22,26},{23,27}} | collective-permute-start | bytes 786440 | tf_op jit(solution)/shard_map/ppermute | solution.py:463
  16.9 16.0 %collective-permute-start.6 = (f32[4,128,128]{2,1,0:T(8,128)S(1)}, f32[4,128,128]{2,1,0:T(8,128)S(1)}, u32[]{:S(2)}, u32[]{:S(2)}) collective-permute-start(f32[4,128,128]{2,1,0:T(8,128)S(1)} %include.3), channel_id=1, source_target_pairs={{4,12},{5,13},{6,14},{7,15},{20,28},{21,29},{22,30},{23,31}} | collective-permute-start | bytes 786440 | tf_op jit(solution)/shard_map/ppermute | solution.py:463
  21.6 6.8 %collective-permute-start.3 = (f32[4,72,128]{2,1,0:T(8,128)S(1)}, f32[4,72,128]{2,1,0:T(8,128)S(1)}, u32[]{:S(2)}, u32[]{:S(2)}) collective-permute-start(f32[4,72,128]{2,1,0:T(8,128)S(1)} %extend.2.gram_ref), channel_id=1, source_target_pairs={{0,1},{1,0},{2,3},{3,2},{4,5},{5,4},{6,7},{7,6},{8,9},{9,8},{10,11... | collective-permute-start | bytes 442376 | tf_op jit(solution)/shard_map/ppermute | solution.py:507
  32.9 3.0 %collective-permute-start.7 = (f32[4,128,128]{2,1,0:T(8,128)S(1)}, f32[4,128,128]{2,1,0:T(8,128)S(1)}, u32[]{:S(2)}, u32[]{:S(2)}) collective-permute-start(f32[4,128,128]{2,1,0:T(8,128)S(1)} %extend.3.memory_ref), channel_id=1, source_target_pairs={{0,1},{1,0},{2,3},{3,2},{4,5},{5,4},{6,7},{7,6},{8,9},{9,8},{10,11... | collective-permute-start | bytes 786440 | tf_op jit(solution)/shard_map/ppermute | solution.py:507
